TPU v7x, 256 devices: a whole 4x4x8 slice. The times are simulated.
256 devices in a mesh: img: 64 (over z, x, core), ref: 4 (over y).
Axes of the slice: x: 4, y: 4, z: 8, core: 2. Of those that a mesh axis runs over, the one named last changes fastest.
Arguments:
- particles: bfloat16 [16384, 4096], P('img'), may hold values from -40 to 40
- projections: bfloat16 [512, 8, 4096], P(('img', 'ref')), may hold values from -6 to 6
- significance: int32 [64, 512], replicated, may hold values from 0 to 1, as said below
- insertion: int32 [512, 8, 2048], P(('img', 'ref')), may hold values from 0 to 4095
Outputs:
- volume: float32 [2, 1048576], P(None, ('img', 'ref'))
- log_evidence: float32 [16384], P('img')
Inputs may be any that keep to these rules, and one draw needn't show every extreme that they name: `significance`: runs are blocks o * 2 to o * 2 + 1, o counted over img and ref with img slowest. For each particle block and each run at most one block is significant; particle block q has one in run q * 4; in every draw some particle block has one in every run.
All inputs are finite; a program needn't handle non-finite values.
Results may differ from a plain program's by a relative error of at most 0.00064.
Values may be sent and summed in bfloat16 or wider, within the bound.
No kernel may reach another device: no remote copies, remote signals or barrier semaphores. Data moves between devices by JAX's collectives and lax.ppermute only.
A program may use at most 128 MiB of HBM per device.

v0:
```python
import math

import jax
import jax.numpy as jnp
import numpy as np
from jax import lax
from jax.experimental import pallas as pl
from jax.experimental.pallas import tpu as pltpu
from jax.sharding import PartitionSpec as P

SIDE = 64
PIX = 2048
FEATURES = 2 * PIX
VOX = 4096
Z, X, CORES, REFS = 8, 4, 2, 4
RUNS = Z * X
COLS = RUNS * 8
N = 256
SHIFTS = 5
ROWS = SHIFTS * N
NEGATIVE = -1e30
SCALE = 2.0 / math.sqrt(FEATURES)
HEADROOM = 2.5
EXTRA = 128


def shift_tables():
    p = np.arange(PIX)
    unit = np.float32(2.0 * math.pi / SIDE)
    ax = (unit * (p % SIDE - SIDE // 2).astype(np.float32)).astype(np.float64)
    ay = (unit * (p // SIDE).astype(np.float32)).astype(np.float64)
    rows = [np.cos(ax), np.sin(ax), np.cos(ay), np.sin(ay)]
    return np.stack(rows + rows).astype(np.float32)


VMEM = pl.BlockSpec(memory_space=pltpu.VMEM)
SMEM = pl.BlockSpec(memory_space=pltpu.SMEM)
LANES = 512
PTILE = 512


def in_vmem(value):
    return pltpu.with_memory_space_constraint(value, pltpu.VMEM)


def limit(mib):
    return pltpu.CompilerParams(vmem_limit_bytes=mib * 1024 * 1024)


def shift_kernel(table_ref, image_ref, out_re, out_im):
    for j in range(PIX // LANES):
        at = slice(j * LANES, (j + 1) * LANES)
        at_im = slice(PIX + j * LANES, PIX + (j + 1) * LANES)
        tables = [table_ref[k : k + 1, at] for k in range(4)]

        @pl.loop(0, N // 16)
        def _(i):
            rows = pl.ds(pl.multiple_of(i * 16, 16), 16)
            re_in, im_in = image_ref[rows, at], image_ref[rows, at_im]
            out_re[0, rows, at] = re_in
            out_im[0, rows, at] = im_in
            re, im = re_in.astype(jnp.float32), im_in.astype(jnp.float32)
            for k in range(2):
                c, s = tables[2 * k], tables[2 * k + 1]
                rc, rs, ic, is_ = re * c, re * s, im * c, im * s
                out_re[1 + 2 * k, rows, at] = (rc - is_).astype(jnp.bfloat16)
                out_im[1 + 2 * k, rows, at] = (rs + ic).astype(jnp.bfloat16)
                out_re[2 + 2 * k, rows, at] = (rc + is_).astype(jnp.bfloat16)
                out_im[2 + 2 * k, rows, at] = (ic - rs).astype(jnp.bfloat16)


def shifted_images(table, images):
    shape = pltpu.VMEM((SHIFTS, N, PIX), jnp.bfloat16)
    return pl.pallas_call(
        shift_kernel,
        in_specs=[VMEM, VMEM],
        out_specs=[VMEM, VMEM],
        out_shape=[shape, shape],
        compiler_params=limit(4),
        cost_estimate=pl.CostEstimate(
            flops=24 * N * PIX, bytes_accessed=12 * 1024 * 1024, transcendentals=0
        ),
        name="shift",
    )(in_vmem(table), in_vmem(images))


def run_entry(sig_ref, pos_ref, q, dz, dx):
    zz = lax.rem(pos_ref[0] + dz, Z)
    xx = lax.rem(pos_ref[1] + dx, X)
    at = (((zz * X + xx) * CORES + pos_ref[2]) * REFS + pos_ref[3]) * 2
    row = pos_ref[2] if q == 0 else 1 - pos_ref[2]
    return sig_ref[row, at], sig_ref[row, at + 1], zz


def score_kernel(sig_ref, pos_ref, *refs):
    by_z = refs[:Z]
    by_x = refs[Z : Z + X]
    sh = refs[Z + X : Z + X + 4]
    st_ref, stat_ref = refs[Z + X + 4 : Z + X + 6]
    sel, acc, mask = refs[Z + X + 6 :]
    stat_ref[...] = jnp.zeros_like(stat_ref)
    for q in range(2):
        for dz in range(Z):
            for dx in range(X):
                o = dz * X + dx
                first, second, zz = run_entry(sig_ref, pos_ref, q, dz, dx)
                sel[q, o, :, 0:PIX] = by_z[dz][dx, second]
                sel[q, o, :, PIX:] = by_x[dx][zz, second, :, 0:PIX]
                live = (first + second).astype(jnp.float32)
                mask[q, o * 8 : o * 8 + 8, :] = jnp.full((8, 128), live, jnp.float32)
    dims = (((1,), (1,)), ((), ()))
    for q in range(2):
        for half in range(2):
            part = lax.dot_general(
                sh[2 * q + half][...].reshape(ROWS, PIX),
                sel[q, :, :, half * PIX : (half + 1) * PIX].reshape(COLS, PIX),
                dims,
                preferred_element_type=jnp.float32,
            )
            if half == 0:
                acc[...] = part
            else:
                acc[...] += part
        live = mask[q, :, 0:1] > 0.5
        top = jnp.full((1, N), NEGATIVE, jnp.float32)
        for t in range(SHIFTS):
            s = acc[t * N : (t + 1) * N, :].T * SCALE
            s = jnp.where(live, s, NEGATIVE)
            st_ref[q, :, t * N : (t + 1) * N] = s
            top = jnp.maximum(top, jnp.max(s, axis=0, keepdims=True))
        total = jnp.zeros((1, N), jnp.float32)
        for t in range(SHIFTS):
            s = st_ref[q, :, t * N : (t + 1) * N]
            e = jnp.where(live, jnp.exp(s - top), 0.0)
            total = total + jnp.sum(e, axis=0, keepdims=True)
        stat_ref[q : q + 1, :] = top
        stat_ref[2 + q : 3 + q, :] = total
    largest = jnp.zeros((8, EXTRA), jnp.float32)
    for dx in range(X):
        for zz in range(Z):
            largest = jnp.maximum(largest, by_x[dx][zz, 0, :, PIX:].astype(jnp.float32))
    stat_ref[4:5, 0:EXTRA] = jnp.max(largest, axis=0, keepdims=True)


def score_all(sig, pos, by_z, by_x, shifted):
    return pl.pallas_call(
        score_kernel,
        in_specs=[SMEM, SMEM] + [VMEM] * (Z + X + 4),
        out_specs=[VMEM, VMEM],
        out_shape=[
            pltpu.VMEM((2, COLS, ROWS), jnp.float32),
            pltpu.VMEM((8, N), jnp.float32),
        ],
        scratch_shapes=[
            pltpu.VMEM((2, RUNS, 8, FEATURES), jnp.bfloat16),
            pltpu.VMEM((ROWS, COLS), jnp.float32),
            pltpu.VMEM((2, COLS, 128), jnp.float32),
        ],
        compiler_params=limit(24),
        cost_estimate=pl.CostEstimate(
            flops=4 * ROWS * COLS * FEATURES, bytes_accessed=28 * 1024 * 1024, transcendentals=2 * ROWS * COLS
        ),
        name="scores",
    )(sig, pos, *[in_vmem(v) for v in by_z], *[in_vmem(v) for v in by_x], *[in_vmem(v) for v in shifted])


def merge_kernel(stat_ref, other_ref, out_ref):
    out_ref[...] = jnp.zeros_like(out_ref)
    for q in range(2):
        a, b = stat_ref[q : q + 1, :], other_ref[1 - q : 2 - q, :]
        top = jnp.maximum(a, b)
        out_ref[q : q + 1, :] = top
        out_ref[2 + q : 3 + q, :] = stat_ref[2 + q : 3 + q, :] * jnp.exp(a - top) + other_ref[
            3 - q : 4 - q, :
        ] * jnp.exp(b - top)
    bound = jnp.max(jnp.maximum(stat_ref[4:5, :], other_ref[4:5, :]), axis=1, keepdims=True)
    out_ref[4:5, :] = jnp.broadcast_to(jnp.maximum(bound, 1e-30), (1, N))


def merge(stats, other):
    return pl.pallas_call(
        merge_kernel,
        in_specs=[VMEM, VMEM],
        out_specs=VMEM,
        out_shape=pltpu.VMEM((8, N), jnp.float32),
        compiler_params=limit(2),
        name="merge",
    )(in_vmem(stats), in_vmem(other))


def partial_kernel(z_first, first_call, sig_ref, pos_ref, *refs):
    if first_call:
        st_ref, *every, own_ref, mate_ref, out_ref, w_ref, ev_ref = refs
        for q in range(2):
            tops = [r[q : q + 1, :] for r in every]
            top = jnp.maximum(jnp.maximum(tops[0], tops[1]), jnp.maximum(tops[2], tops[3]))
            total = sum(r[2 + q : 3 + q, :] * jnp.exp(t - top) for r, t in zip(every, tops))
            evidence = top + jnp.log(total)
            if q == 0:
                ev_ref[...] = evidence

            @pl.loop(0, SHIFTS)
            def _(t):
                at = pl.ds(pl.multiple_of(t * N, N), N)
                w_ref[q, :, at] = jnp.exp(st_ref[q, :, at] - evidence).astype(jnp.bfloat16)

        bound_ref = every[0]
    else:
        w_ref, bound_ref, own_ref, mate_ref, out_ref = refs
    scale = HEADROOM / bound_ref[4:5, 0:1]
    entries = [
        [run_entry(sig_ref, pos_ref, q, dz, dx) for dz in range(Z) for dx in range(X)]
        for q in range(2)
    ]

    @pl.loop(0, PIX // PTILE)
    def _(i):
        at = pl.ds(pl.multiple_of(i * PTILE, PTILE), PTILE)
        for q, images in ((0, own_ref), (1, mate_ref)):
            value = (
                jnp.dot(
                    w_ref[q],
                    images[:, :, at].reshape(ROWS, PTILE),
                    preferred_element_type=jnp.float32,
                )
                * scale
            )
            for o in range(RUNS):
                _, second, zz = entries[q][o]
                base = (o if z_first else (o % X) * Z + zz) * 16
                rows = pl.ds(pl.multiple_of(base + second * 8, 8), 8)
                block = value[o * 8 : o * 8 + 8, :]
                if q == 0:
                    other = pl.ds(pl.multiple_of(base + (1 - second) * 8, 8), 8)
                    out_ref[rows, at] = block
                    out_ref[other, at] = jnp.zeros_like(block)
                else:
                    out_ref[rows, at] += block


def partial_sums(z_first, sig, pos, weights, own, mate):
    first_call = z_first
    out_shape = [pltpu.VMEM((2 * COLS, PIX), jnp.float32)]
    if first_call:
        out_shape.append(pltpu.VMEM((2, COLS, ROWS), jnp.bfloat16))
        out_shape.append(jax.ShapeDtypeStruct((1, N), jnp.float32))
    return pl.pallas_call(
        lambda *refs: partial_kernel(z_first, first_call, *refs),
        in_specs=[SMEM, SMEM] + [VMEM] * (len(weights) + 2),
        out_specs=[VMEM] * len(out_shape),
        out_shape=out_shape,
        compiler_params=limit(12),
        cost_estimate=pl.CostEstimate(
            flops=2 * ROWS * COLS * FEATURES, bytes_accessed=16 * 1024 * 1024, transcendentals=0
        ),
        name="partial_re" if first_call else "partial_im",
    )(sig, pos, *[in_vmem(v) for v in weights], in_vmem(own), in_vmem(mate))


HIGH, LOW = 32, 128
PART = 2048


def insert_kernel(bound_ref, w_ref, ins_ref, *refs):
    scale = bound_ref[4:5, 0:1] * (1.0 / HEADROOM)
    high_ids = lax.broadcasted_iota(jnp.int32, (HIGH, PART), 0)
    low_ids = lax.broadcasted_iota(jnp.int32, (LOW, PART), 0)

    def body(i, acc):
        row = pl.ds(i, 1)
        for j in range(PIX // PART):
            at = slice(j * PART, (j + 1) * PART)
            ids = ins_ref[row, at]
            high = lax.shift_right_logical(ids, 7)
            low = lax.bitwise_and(ids, LOW - 1)
            value = w_ref[row, at] * scale
            head = value.astype(jnp.bfloat16).astype(jnp.float32)
            tail = value - head
            here = high == high_ids
            rows = jnp.concatenate(
                [jnp.where(here, head, 0.0), jnp.where(here, tail, 0.0)], axis=0
            ).astype(jnp.bfloat16)
            table = jnp.where(low == low_ids, 1.0, 0.0).astype(jnp.bfloat16)
            acc = acc + lax.dot_general(
                rows, table, (((1,), (1,)), ((), ())), preferred_element_type=jnp.float32
            )
        return acc

    acc = lax.fori_loop(0, 16, body, jnp.zeros((2 * HIGH, LOW), jnp.float32), unroll=2)
    slab = acc[:HIGH] + acc[HIGH:]
    if len(refs) == 1:
        refs[0][...] = slab
    else:
        first_ref, out_ref = refs
        for h in range(HIGH):
            at = slice(h * LOW, (h + 1) * LOW)
            out_ref[0:1, at] = first_ref[h : h + 1, :]
            out_ref[1:2, at] = slab[h : h + 1, :]


def insert(bound, weighted, insertion, *first):
    shape = (2, VOX) if first else (HIGH, LOW)
    return pl.pallas_call(
        insert_kernel,
        in_specs=[VMEM] * (3 + len(first)),
        out_specs=VMEM,
        out_shape=jax.ShapeDtypeStruct(shape, jnp.float32),
        compiler_params=limit(8),
        cost_estimate=pl.CostEstimate(
            flops=4 * HIGH * LOW * 16 * PIX, bytes_accessed=512 * 1024, transcendentals=0
        ),
        name="insert_im" if first else "insert_re",
    )(bound, weighted.reshape(16, PIX), insertion, *first)


def img_index(z, x, c):
    return (z * X + x) * CORES + c


def pairs(dz, dx, dc=0):
    return [
        (img_index(z, x, c), img_index((z + dz) % Z, (x + dx) % X, (c + dc) % CORES))
        for z in range(Z)
        for x in range(X)
        for c in range(CORES)
    ]


Z_GROUPS = [[img_index(z, x, c) for z in range(Z)] for x in range(X) for c in range(CORES)]


def send(value, dz=0, dx=0, dc=0):
    return lax.ppermute(value, "img", pairs(dz, dx, dc))


def all_to_all_z(value):
    return lax.all_to_all(
        value, "img", split_axis=0, concat_axis=0, tiled=True, axis_index_groups=Z_GROUPS
    )


def gather_x_first(unit):
    row = jnp.stack([unit, send(unit, dx=-1), send(unit, dx=-2), send(unit, dx=1)])
    out = {0: row}
    ahead = behind = row
    for k in range(1, Z // 2 + 1):
        behind = send(behind, dz=1)
        out[Z - k] = behind
        if k < Z // 2:
            ahead = send(ahead, dz=-1)
            out[k] = ahead
    return [out[k] for k in range(Z)]


def gather_z_first(unit):
    copies = jnp.broadcast_to(unit[None], (Z,) + unit.shape)
    column = all_to_all_z(copies)
    return [column, send(column, dx=-1), send(column, dx=-2), send(column, dx=1)]


def wide(value):
    return value.astype(jnp.float32)


def narrow(value):
    return value.astype(jnp.float16)


def scatter_z_first(parts):
    half = Z // 2
    behind = narrow(parts[half])
    for k in range(half, 0, -1):
        if k < half:
            behind = narrow(parts[k] + wide(behind))
        behind = send(behind, dz=1)
    ahead = narrow(parts[half + 1])
    for k in range(half - 1, 0, -1):
        if k < half - 1:
            ahead = narrow(parts[Z - k] + wide(ahead))
        ahead = send(ahead, dz=-1)
    row = parts[0] + wide(behind) + wide(ahead)
    arrived = [send(narrow(row[k]), dx=k) for k in range(1, X)]
    return row[0] + wide(arrived[0]) + wide(arrived[1]) + wide(arrived[2])


def scatter_x_first(parts):
    arrived = [send(narrow(parts[k]), dx=k) for k in range(1, X)]
    column = parts[0] + wide(arrived[0]) + wide(arrived[1]) + wide(arrived[2])
    return jnp.sum(wide(all_to_all_z(narrow(column))), axis=0)


def exchange_refs(value):
    out = [value]
    for k in range(1, REFS):
        out.append(lax.ppermute(value, "ref", [(r, (r + k) % REFS) for r in range(REFS)]))
    return out


def one_device(particles, projections, significance, insertion):
    img = lax.axis_index("img")
    ref = lax.axis_index("ref")
    z, x, core = img >> 3, (img >> 1) & 3, img & 1
    pos = jnp.stack([z, x, core, ref]).astype(jnp.int32)
    sig = lax.dynamic_slice_in_dim(significance, img - core, 2, axis=0)
    table = jnp.asarray(shift_tables())

    mate = send(particles, dc=1)
    by_z = gather_x_first(projections[:, :, :PIX])
    largest = jnp.max(jnp.abs(particles))
    unit = jnp.concatenate(
        [projections[:, :, PIX:], jnp.broadcast_to(largest, (2, 8, EXTRA))], axis=2
    )
    unit, pos, sig = lax.optimization_barrier((unit, pos, sig))
    by_x = gather_z_first(unit)
    own_re, own_im = shifted_images(table, particles)
    mate_re, mate_im = shifted_images(table, mate)

    scores, stats = score_all(sig, pos, by_z, by_x, (own_re, own_im, mate_re, mate_im))
    merged = merge(stats, send(stats, dc=1))
    every = exchange_refs(merged)
    sums_re, weights, evidence = partial_sums(
        True, sig, pos, (scores, *every), own_re, mate_re
    )
    (sums_im,) = partial_sums(False, sig, pos, (weights, merged), own_im, mate_im)
    total_re = scatter_z_first(sums_re.reshape(Z, X, 2, 8, PIX))
    total_im = scatter_x_first(sums_im.reshape(X, Z, 2, 8, PIX))
    ids = insertion.reshape(16, PIX)
    volume_re = insert(merged, total_re, ids)
    volume = insert(merged, total_im, ids, volume_re)
    return volume, evidence.reshape(N)


def solution(mesh):
    in_specs = (P("img", None), P(("img", "ref"), None, None), P(), P(("img", "ref"), None, None))
    out_specs = (P(None, ("img", "ref")), P("img"))
    return jax.shard_map(
        one_device, mesh=mesh, in_specs=in_specs, out_specs=out_specs, check_vma=False
    )
```

profile of v0, /device:TPU:8, one launch (start us, length us, event | category | flops | bytes accessed | tf_op | source)
XLA Modules:
  0.0 151.1 jit_solution(4807761482542371680)
XLA Ops:
  0.8 2.6 %abs_reduce_fusion = bf16[]{:T(256)} fusion(bf16[256,4096]{1,0:T(8,128)(2,1)} %image_ref.1), kind=kLoop, calls=%fused_computation | loop fusion | flops 2097151 | bytes 2097154 | tf_op jit(solution)/shard_map/reduce_max | solution.py:409
  5.1 8.5 %all-to-all-start = ((bf16[8,2,8,2176]{3,2,1,0:T(8,128)(2,1)}), bf16[8,2,8,2176]{3,2,1,0:T(8,128)(2,1)S(1)}, u32[]{:S(2)}, u32[]{:S(2)}) async-start(bf16[8,2,8,2176]{3,2,1,0:T(8,128)(2,1)} %broadcast_in_dim.2), calls=%async_computation | async-start | bytes 1114112 | tf_op jit(solution)/shard_map/all_to_all | solution.py:337
  13.5 3.0 %collective-permute-start.1 = (bf16[2,8,2048]{2,1,0:T(8,128)(2,1)S(1)}, bf16[2,8,2048]{2,1,0:T(8,128)(2,1)S(1)}, u32[]{:S(2)}, u32[]{:S(2)}) collective-permute-start(bf16[2,8,2048]{2,1,0:T(8,128)(2,1)S(1)} %get-tuple-element.43), channel_id=1, source_target_pairs={{0,16},{4,20},{8,24},{12,28},{16,0},{20,4},{24,8},{28,12},{32,48},... | collective-permute-start | bytes 196616 | tf_op jit(solution)/shard_map/ppermute | solution.py:333
  26.6 8.7 %collective-permute-done.6.refs_7_ = bf16[4,2,8,2048]{3,2,1,0:T(8,128)(2,1)S(1)} collective-permute-done((bf16[4,2,8,2048]{3,2,1,0:T(8,128)(2,1)S(1)}, bf16[4,2,8,2048]{3,2,1,0:T(8,128)(2,1)S(1)}, u32[]{:S(2)}, u32[]{:S(2)}) %collective-permute-start.6) | collective-permute-done | bytes 262176 | tf_op jit(solution)/shard_map/ppermute | solution.py:333
  35.3 3.2 %collective-permute-start.4 = (bf16[4,2,8,2048]{3,2,1,0:T(8,128)(2,1)}, bf16[4,2,8,2048]{3,2,1,0:T(8,128)(2,1)}, u32[]{:S(2)}, u32[]{:S(2)}) collective-permute-start(bf16[4,2,8,2048]{3,2,1,0:T(8,128)(2,1)} %collective-permute-done.3.refs_1_), channel_id=1, source_target_pairs={{0,224},{4,228},{8,232},{12,236},{16,240},{20,244},{24,248},{28,25... | collective-permute-start | bytes 786440 | tf_op jit(solution)/shard_map/ppermute | solution.py:333
  40.0 2.7 %collective-permute-start.11 = (bf16[8,2,8,2176]{3,2,1,0:T(8,128)(2,1)S(1)}, bf16[8,2,8,2176]{3,2,1,0:T(8,128)(2,1)S(1)}, u32[]{:S(2)}, u32[]{:S(2)}) collective-permute-start(bf16[8,2,8,2176]{3,2,1,0:T(8,128)(2,1)S(1)} %all-to-all-done.refs_8_), channel_id=1, source_target_pairs={{0,16},{4,20},{8,24},{12,28},{16,0},{20,4},{24,8},{28,12},{32,48},... | collective-permute-start | bytes 1671176 | tf_op jit(solution)/shard_map/ppermute | solution.py:333
  44.1 2.7 %collective-permute-start.10 = (bf16[8,2,8,2176]{3,2,1,0:T(8,128)(2,1)S(1)}, bf16[8,2,8,2176]{3,2,1,0:T(8,128)(2,1)S(1)}, u32[]{:S(2)}, u32[]{:S(2)}) collective-permute-start(bf16[8,2,8,2176]{3,2,1,0:T(8,128)(2,1)S(1)} %all-to-all-done.refs_8_), channel_id=1, source_target_pairs={{0,24},{4,28},{8,0},{12,4},{16,8},{20,12},{24,16},{28,20},{32,56},... | collective-permute-start | bytes 1671176 | tf_op jit(solution)/shard_map/ppermute | solution.py:333
  46.9 7.8 %collective-permute-done.8.refs_5_ = bf16[4,2,8,2048]{3,2,1,0:T(8,128)(2,1)S(1)} collective-permute-done((bf16[4,2,8,2048]{3,2,1,0:T(8,128)(2,1)}, bf16[4,2,8,2048]{3,2,1,0:T(8,128)(2,1)S(1)}, u32[]{:S(2)}, u32[]{:S(2)}) %collective-permute-start.8) | collective-permute-done | bytes 262176 | tf_op jit(solution)/shard_map/ppermute | solution.py:333
  58.7 5.1 %shift.3 = (bf16[5,256,2048]{2,1,0:T(8,128)(2,1)S(1)}, bf16[5,256,2048]{2,1,0:T(8,128)(2,1)S(1)}) custom-call(f32[8,2048]{1,0:T(8,128)S(1)} %copy-done.5, bf16[256,4096]{1,0:T(8,128)(2,1)} %collective-permute-done.13.image_ref), custom_call_target="tpu_custom_call" | custom-call | flops 12582912 | bytes 12582912 | tf_op jit(solution)/shard_map/shift/pallas_call | solution.py:74
  65.9 8.1 %scores.1 = (f32[2,256,1280]{2,1,0:T(8,128)S(1)}, f32[8,256]{1,0:T(8,128)S(1)}) custom-call(s32[2,512]{1,0:T(2,128)S(1)} %constant_dynamic-slice_fusion.sig_ref.refs_0_, s32[4]{0:T(128)S(1)} %pad_add_fusion.pos_ref.refs_1_, bf16[4,2,8,2048]{3,2,1,0:T(8,128)(2,1)S(1)} %pad_maximum_fusion.refs_0_, bf16[4,2,8,2048]{3,2,1,0:T(8,128)(2,1)} %collective-permute-done.3.refs_1_, ...), custom_call_target="tpu_custom_call" | custom-call | flops 5368709120 | bytes 29360128 | tf_op jit(solution)/shard_map/scores/pallas_call | solution.py:146
  75.9 2.6 %collective-permute-start.16 = (f32[8,256]{1,0:T(8,128)S(1)}, f32[8,256]{1,0:T(8,128)S(1)}, u32[]{:S(2)}, u32[]{:S(2)}) collective-permute-start(f32[8,256]{1,0:T(8,128)S(1)} %merge.1.refs_3_.bound_ref), channel_id=1, source_target_pairs={{0,2},{1,3},{2,0},{3,1},{4,6},{5,7},{6,4},{7,5},{8,10},{9,11},{10,... | collective-permute-start | bytes 24584 | tf_op jit(solution)/shard_map/ppermute | solution.py:395
  84.6 5.7 %partial_re.1 = (f32[512,2048]{1,0:T(8,128)S(1)}, bf16[2,256,1280]{2,1,0:T(8,128)(2,1)S(1)}, f32[1,256]{1,0:T(1,128)}) custom-call(s32[2,512]{1,0:T(2,128)S(1)} %constant_dynamic-slice_fusion.sig_ref.refs_0_, s32[4]{0:T(128)S(1)} %pad_add_fusion.pos_ref.refs_1_, f32[2,256,1280]{2,1,0:T(8,128)S(1)} %get-tuple-element.22.refs_2_, ...), custom_call_target="tpu_custom_call" | custom-call | flops 2684354560 | bytes 16777216 | tf_op jit(solution)/shard_map/partial_re/pallas_call | solution.py:247
  90.3 4.7 %partial_im.1 = f32[512,2048]{1,0:T(8,128)S(1)} custom-call(s32[2,512]{1,0:T(2,128)S(1)} %constant_dynamic-slice_fusion.sig_ref.refs_0_, s32[4]{0:T(128)S(1)} %pad_add_fusion.pos_ref.refs_1_, bf16[2,256,1280]{2,1,0:T(8,128)(2,1)S(1)} %get-tuple-element.23.refs_2_, f32[8,256]{1,0:T(8,128)S(1)} %merge.1.refs_3_.bound_ref, ...), custom_call_target="tpu_custom_call" | custom-call | flops 2684354560 | bytes 16777216 | tf_op jit(solution)/shard_map/partial_im/pallas_call | solution.py:247
  103.1 3.2 %collective-permute-start.25 = (f16[4,2,8,2048]{3,2,1,0:T(8,128)(2,1)S(1)}, f16[4,2,8,2048]{3,2,1,0:T(8,128)(2,1)S(1)}, u32[]{:S(2)}, u32[]{:S(2)}) collective-permute-start(f16[4,2,8,2048]{3,2,1,0:T(8,128)(2,1)S(1)} %bitcast.55), channel_id=1, source_target_pairs={{0,224},{4,228},{8,232},{12,236},{16,240},{20,244},{24,248},{28,25... | collective-permute-start | bytes 786440 | tf_op jit(solution)/shard_map/ppermute | solution.py:333
  106.5 3.7 %collective-permute-done.25 = f16[4,2,8,2048]{3,2,1,0:T(8,128)(2,1)S(1)} collective-permute-done((f16[4,2,8,2048]{3,2,1,0:T(8,128)(2,1)S(1)}, f16[4,2,8,2048]{3,2,1,0:T(8,128)(2,1)S(1)}, u32[]{:S(2)}, u32[]{:S(2)}) %collective-permute-start.25) | collective-permute-done | bytes 262176 | tf_op jit(solution)/shard_map/ppermute | solution.py:333
  110.3 3.8 %collective-permute-start.26 = (f16[4,2,8,2048]{3,2,1,0:T(8,128)(2,1)S(1)}, f16[4,2,8,2048]{3,2,1,0:T(8,128)(2,1)S(1)}, u32[]{:S(2)}, u32[]{:S(2)}) collective-permute-start(f16[4,2,8,2048]{3,2,1,0:T(8,128)(2,1)S(1)} %add_convert_fusion.2), channel_id=1, source_target_pairs={{0,224},{4,228},{8,232},{12,236},{16,240},{20,244},{24,248},{28,25... | collective-permute-start | bytes 786440 | tf_op jit(solution)/shard_map/ppermute | solution.py:333
  114.2 3.8 %collective-permute-done.26 = f16[4,2,8,2048]{3,2,1,0:T(8,128)(2,1)S(1)} collective-permute-done((f16[4,2,8,2048]{3,2,1,0:T(8,128)(2,1)S(1)}, f16[4,2,8,2048]{3,2,1,0:T(8,128)(2,1)S(1)}, u32[]{:S(2)}, u32[]{:S(2)}) %collective-permute-start.26) | collective-permute-done | bytes 262176 | tf_op jit(solution)/shard_map/ppermute | solution.py:333
  118.2 3.8 %collective-permute-start.27 = (f16[4,2,8,2048]{3,2,1,0:T(8,128)(2,1)S(1)}, f16[4,2,8,2048]{3,2,1,0:T(8,128)(2,1)S(1)}, u32[]{:S(2)}, u32[]{:S(2)}) collective-permute-start(f16[4,2,8,2048]{3,2,1,0:T(8,128)(2,1)S(1)} %add_convert_fusion.1), channel_id=1, source_target_pairs={{0,224},{4,228},{8,232},{12,236},{16,240},{20,244},{24,248},{28,25... | collective-permute-start | bytes 786440 | tf_op jit(solution)/shard_map/ppermute | solution.py:333
  122.1 3.3 %collective-permute-done.18 = f16[8,2,8,2048]{3,2,1,0:T(8,128)(2,1)S(1)} collective-permute-done((f16[8,2,8,2048]{3,2,1,0:T(8,128)(2,1)S(1)}, f16[8,2,8,2048]{3,2,1,0:T(8,128)(2,1)S(1)}, u32[]{:S(2)}, u32[]{:S(2)}) %collective-permute-start.18) | collective-permute-done | bytes 524320 | tf_op jit(solution)/shard_map/ppermute | solution.py:333
  126.6 5.4 %all-to-all-start.1 = ((f16[8,2,8,2048]{3,2,1,0:T(8,128)(2,1)}), f16[8,2,8,2048]{3,2,1,0:T(8,128)(2,1)S(1)}, u32[]{:S(2)}, u32[]{:S(2)}) async-start(f16[8,2,8,2048]{3,2,1,0:T(8,128)(2,1)} %add_convert_fusion), calls=%async_computation.1 | async-start | bytes 1048576 | tf_op jit(solution)/shard_map/all_to_all | solution.py:337
  132.2 3.2 %collective-permute-start.30 = (f16[2,8,2048]{2,1,0:T(8,128)(2,1)S(1)}, f16[2,8,2048]{2,1,0:T(8,128)(2,1)S(1)}, u32[]{:S(2)}, u32[]{:S(2)}) collective-permute-start(f16[2,8,2048]{2,1,0:T(8,128)(2,1)S(1)} %get-tuple-element.40), channel_id=1, source_target_pairs={{0,24},{4,28},{8,0},{12,4},{16,8},{20,12},{24,16},{28,20},{32,56},... | collective-permute-start | bytes 196616 | tf_op jit(solution)/shard_map/ppermute | solution.py:333
  138.0 3.3 %collective-permute-done.29 = f16[2,8,2048]{2,1,0:T(8,128)(2,1)S(1)} collective-permute-done((f16[2,8,2048]{2,1,0:T(8,128)(2,1)S(1)}, f16[2,8,2048]{2,1,0:T(8,128)(2,1)S(1)}, u32[]{:S(2)}, u32[]{:S(2)}) %collective-permute-start.29) | collective-permute-done | bytes 65568 | tf_op jit(solution)/shard_map/ppermute | solution.py:333
  141.3 4.2 %insert_re.1.refs_0_ = f32[32,128]{1,0:T(8,128)S(1)} custom-call(f32[8,256]{1,0:T(8,128)S(1)} %merge.1.refs_3_.bound_ref, f32[16,2048]{1,0:T(8,128)S(1)} %fusion.3.w_ref, s32[16,2048]{1,0:T(8,128)S(1)} %bitcast.44), custom_call_target="tpu_custom_call" | custom-call | flops 536870912 | bytes 524288 | tf_op jit(solution)/shard_map/insert_re/pallas_call | solution.py:303
  146.3 4.9 %insert_im.1 = f32[2,4096]{1,0:T(2,128)} custom-call(f32[8,256]{1,0:T(8,128)S(1)} %merge.1.refs_3_.bound_ref, f32[16,2048]{1,0:T(8,128)S(1)} %bitcast.43, s32[16,2048]{1,0:T(8,128)S(1)} %bitcast.45, f32[32,128]{1,0:T(8,128)S(1)} %insert_re.1.refs_0_), custom_call_target="tpu_custom_call" | custom-call | flops 536870912 | bytes 524288 | tf_op jit(solution)/shard_map/insert_im/pallas_call | solution.py:303
  (90 shorter events, 42.1 us)
Async XLA Ops:
  0.7 54.1 %collective-permute-start.13 = (bf16[256,4096]{1,0:T(8,128)(2,1)}, bf16[256,4096]{1,0:T(8,128)(2,1)}, u32[]{:S(2)}, u32[]{:S(2)}) collective-permute-start(bf16[256,4096]{1,0:T(8,128)(2,1)} %image_ref.1), channel_id=1, source_target_pairs={{0,4},{4,0},{8,12},{12,8},{16,20},{20,16},{24,28},{28,24},{32,36},... | collective-permute-start | bytes 6291464 | tf_op jit(solution)/shard_map/ppermute | solution.py:333
  5.1 33.5 %all-to-all-start = ((bf16[8,2,8,2176]{3,2,1,0:T(8,128)(2,1)}), bf16[8,2,8,2176]{3,2,1,0:T(8,128)(2,1)S(1)}, u32[]{:S(2)}, u32[]{:S(2)}) async-start(bf16[8,2,8,2176]{3,2,1,0:T(8,128)(2,1)} %broadcast_in_dim.2), calls=%async_computation | async-start | bytes 1114112 | tf_op jit(solution)/shard_map/all_to_all | solution.py:337
  13.5 5.8 %collective-permute-start.1 = (bf16[2,8,2048]{2,1,0:T(8,128)(2,1)S(1)}, bf16[2,8,2048]{2,1,0:T(8,128)(2,1)S(1)}, u32[]{:S(2)}, u32[]{:S(2)}) collective-permute-start(bf16[2,8,2048]{2,1,0:T(8,128)(2,1)S(1)} %get-tuple-element.43), channel_id=1, source_target_pairs={{0,16},{4,20},{8,24},{12,28},{16,0},{20,4},{24,8},{28,12},{32,48},... | collective-permute-start | bytes 196616 | tf_op jit(solution)/shard_map/ppermute | solution.py:333
  23.2 12.1 %collective-permute-start.6 = (bf16[4,2,8,2048]{3,2,1,0:T(8,128)(2,1)S(1)}, bf16[4,2,8,2048]{3,2,1,0:T(8,128)(2,1)S(1)}, u32[]{:S(2)}, u32[]{:S(2)}) collective-permute-start(bf16[4,2,8,2048]{3,2,1,0:T(8,128)(2,1)S(1)} %pad_maximum_fusion.refs_0_), channel_id=1, source_target_pairs={{0,32},{4,36},{8,40},{12,44},{16,48},{20,52},{24,56},{28,60},{32,6... | collective-permute-start | bytes 786440 | tf_op jit(solution)/shard_map/ppermute | solution.py:333
  25.3 10.0 %collective-permute-start.3 = (bf16[4,2,8,2048]{3,2,1,0:T(8,128)(2,1)S(1)}, bf16[4,2,8,2048]{3,2,1,0:T(8,128)(2,1)}, u32[]{:S(2)}, u32[]{:S(2)}) collective-permute-start(bf16[4,2,8,2048]{3,2,1,0:T(8,128)(2,1)S(1)} %pad_maximum_fusion.refs_0_), channel_id=1, source_target_pairs={{0,224},{4,228},{8,232},{12,236},{16,240},{20,244},{24,248},{28,25... | collective-permute-start | bytes 786440 | tf_op jit(solution)/shard_map/ppermute | solution.py:333
  35.3 8.9 %collective-permute-start.7 = (bf16[4,2,8,2048]{3,2,1,0:T(8,128)(2,1)S(1)}, bf16[4,2,8,2048]{3,2,1,0:T(8,128)(2,1)}, u32[]{:S(2)}, u32[]{:S(2)}) collective-permute-start(bf16[4,2,8,2048]{3,2,1,0:T(8,128)(2,1)S(1)} %collective-permute-done.6.refs_7_), channel_id=1, source_target_pairs={{0,32},{4,36},{8,40},{12,44},{16,48},{20,52},{24,56},{28,60},{32,6... | collective-permute-start | bytes 786440 | tf_op jit(solution)/shard_map/ppermute | solution.py:333
  35.3 11.6 %collective-permute-start.4 = (bf16[4,2,8,2048]{3,2,1,0:T(8,128)(2,1)}, bf16[4,2,8,2048]{3,2,1,0:T(8,128)(2,1)}, u32[]{:S(2)}, u32[]{:S(2)}) collective-permute-start(bf16[4,2,8,2048]{3,2,1,0:T(8,128)(2,1)} %collective-permute-done.3.refs_1_), channel_id=1, source_target_pairs={{0,224},{4,228},{8,232},{12,236},{16,240},{20,244},{24,248},{28,25... | collective-permute-start | bytes 786440 | tf_op jit(solution)/shard_map/ppermute | solution.py:333
  38.5 25.3 %collective-permute-start.12 = (bf16[8,2,8,2176]{3,2,1,0:T(8,128)(2,1)S(1)}, bf16[8,2,8,2176]{3,2,1,0:T(8,128)(2,1)S(1)}, u32[]{:S(2)}, u32[]{:S(2)}) collective-permute-start(bf16[8,2,8,2176]{3,2,1,0:T(8,128)(2,1)S(1)} %all-to-all-done.refs_8_), channel_id=1, source_target_pairs={{0,8},{4,12},{8,16},{12,20},{16,24},{20,28},{24,0},{28,4},{32,40},... | collective-permute-start | bytes 1671176 | tf_op jit(solution)/shard_map/ppermute | solution.py:333
  40.0 25.9 %collective-permute-start.11 = (bf16[8,2,8,2176]{3,2,1,0:T(8,128)(2,1)S(1)}, bf16[8,2,8,2176]{3,2,1,0:T(8,128)(2,1)S(1)}, u32[]{:S(2)}, u32[]{:S(2)}) collective-permute-start(bf16[8,2,8,2176]{3,2,1,0:T(8,128)(2,1)S(1)} %all-to-all-done.refs_8_), channel_id=1, source_target_pairs={{0,16},{4,20},{8,24},{12,28},{16,0},{20,4},{24,8},{28,12},{32,48},... | collective-permute-start | bytes 1671176 | tf_op jit(solution)/shard_map/ppermute | solution.py:333
  44.1 21.8 %collective-permute-start.10 = (bf16[8,2,8,2176]{3,2,1,0:T(8,128)(2,1)S(1)}, bf16[8,2,8,2176]{3,2,1,0:T(8,128)(2,1)S(1)}, u32[]{:S(2)}, u32[]{:S(2)}) collective-permute-start(bf16[8,2,8,2176]{3,2,1,0:T(8,128)(2,1)S(1)} %all-to-all-done.refs_8_), channel_id=1, source_target_pairs={{0,24},{4,28},{8,0},{12,4},{16,8},{20,12},{24,16},{28,20},{32,56},... | collective-permute-start | bytes 1671176 | tf_op jit(solution)/shard_map/ppermute | solution.py:333
  46.9 7.8 %collective-permute-start.8 = (bf16[4,2,8,2048]{3,2,1,0:T(8,128)(2,1)}, bf16[4,2,8,2048]{3,2,1,0:T(8,128)(2,1)S(1)}, u32[]{:S(2)}, u32[]{:S(2)}) collective-permute-start(bf16[4,2,8,2048]{3,2,1,0:T(8,128)(2,1)} %collective-permute-done.7.refs_6_), channel_id=1, source_target_pairs={{0,32},{4,36},{8,40},{12,44},{16,48},{20,52},{24,56},{28,60},{32,6... | collective-permute-start | bytes 786440 | tf_op jit(solution)/shard_map/ppermute | solution.py:333
  54.7 9.1 %collective-permute-start.5 = (bf16[4,2,8,2048]{3,2,1,0:T(8,128)(2,1)}, bf16[4,2,8,2048]{3,2,1,0:T(8,128)(2,1)S(1)}, u32[]{:S(2)}, u32[]{:S(2)}) collective-permute-start(bf16[4,2,8,2048]{3,2,1,0:T(8,128)(2,1)} %collective-permute-done.4.refs_2_), channel_id=1, source_target_pairs={{0,224},{4,228},{8,232},{12,236},{16,240},{20,244},{24,248},{28,25... | collective-permute-start | bytes 786440 | tf_op jit(solution)/shard_map/ppermute | solution.py:333
  54.7 9.1 %collective-permute-start.9 = (bf16[4,2,8,2048]{3,2,1,0:T(8,128)(2,1)S(1)}, bf16[4,2,8,2048]{3,2,1,0:T(8,128)(2,1)S(1)}, u32[]{:S(2)}, u32[]{:S(2)}) collective-permute-start(bf16[4,2,8,2048]{3,2,1,0:T(8,128)(2,1)S(1)} %collective-permute-done.8.refs_5_), channel_id=1, source_target_pairs={{0,32},{4,36},{8,40},{12,44},{16,48},{20,52},{24,56},{28,60},{32,6... | collective-permute-start | bytes 786440 | tf_op jit(solution)/shard_map/ppermute | solution.py:333
  97.7 8.7 %collective-permute-start.21 = (f16[4,2,8,2048]{3,2,1,0:T(8,128)(2,1)S(1)}, f16[4,2,8,2048]{3,2,1,0:T(8,128)(2,1)S(1)}, u32[]{:S(2)}, u32[]{:S(2)}) collective-permute-start(f16[4,2,8,2048]{3,2,1,0:T(8,128)(2,1)S(1)} %bitcast.56), channel_id=1, source_target_pairs={{0,32},{4,36},{8,40},{12,44},{16,48},{20,52},{24,56},{28,60},{32,6... | collective-permute-start | bytes 786440 | tf_op jit(solution)/shard_map/ppermute | solution.py:333
  98.3 23.8 %collective-permute-start.20 = (f16[8,2,8,2048]{3,2,1,0:T(8,128)(2,1)S(1)}, f16[8,2,8,2048]{3,2,1,0:T(8,128)(2,1)S(1)}, u32[]{:S(2)}, u32[]{:S(2)}) collective-permute-start(f16[8,2,8,2048]{3,2,1,0:T(8,128)(2,1)S(1)} %bitcast.54), channel_id=1, source_target_pairs={{0,24},{4,28},{8,0},{12,4},{16,8},{20,12},{24,16},{28,20},{32,56},... | collective-permute-start | bytes 1572872 | tf_op jit(solution)/shard_map/ppermute | solution.py:333
  100.7 24.7 %collective-permute-start.18 = (f16[8,2,8,2048]{3,2,1,0:T(8,128)(2,1)S(1)}, f16[8,2,8,2048]{3,2,1,0:T(8,128)(2,1)S(1)}, u32[]{:S(2)}, u32[]{:S(2)}) collective-permute-start(f16[8,2,8,2048]{3,2,1,0:T(8,128)(2,1)S(1)} %bitcast.53), channel_id=1, source_target_pairs={{0,8},{4,12},{8,16},{12,20},{16,24},{20,28},{24,0},{28,4},{32,40},... | collective-permute-start | bytes 1572872 | tf_op jit(solution)/shard_map/ppermute | solution.py:333
  100.7 24.7 %collective-permute-start.19 = (f16[8,2,8,2048]{3,2,1,0:T(8,128)(2,1)S(1)}, f16[8,2,8,2048]{3,2,1,0:T(8,128)(2,1)S(1)}, u32[]{:S(2)}, u32[]{:S(2)}) collective-permute-start(f16[8,2,8,2048]{3,2,1,0:T(8,128)(2,1)S(1)} %bitcast.52), channel_id=1, source_target_pairs={{0,16},{4,20},{8,24},{12,28},{16,0},{20,4},{24,8},{28,12},{32,48},... | collective-permute-start | bytes 1572872 | tf_op jit(solution)/shard_map/ppermute | solution.py:333
  103.1 7.1 %collective-permute-start.25 = (f16[4,2,8,2048]{3,2,1,0:T(8,128)(2,1)S(1)}, f16[4,2,8,2048]{3,2,1,0:T(8,128)(2,1)S(1)}, u32[]{:S(2)}, u32[]{:S(2)}) collective-permute-start(f16[4,2,8,2048]{3,2,1,0:T(8,128)(2,1)S(1)} %bitcast.55), channel_id=1, source_target_pairs={{0,224},{4,228},{8,232},{12,236},{16,240},{20,244},{24,248},{28,25... | collective-permute-start | bytes 786440 | tf_op jit(solution)/shard_map/ppermute | solution.py:333
  106.4 7.7 %collective-permute-start.22 = (f16[4,2,8,2048]{3,2,1,0:T(8,128)(2,1)S(1)}, f16[4,2,8,2048]{3,2,1,0:T(8,128)(2,1)S(1)}, u32[]{:S(2)}, u32[]{:S(2)}) collective-permute-start(f16[4,2,8,2048]{3,2,1,0:T(8,128)(2,1)S(1)} %add_convert_fusion.5), channel_id=1, source_target_pairs={{0,32},{4,36},{8,40},{12,44},{16,48},{20,52},{24,56},{28,60},{32,6... | collective-permute-start | bytes 786440 | tf_op jit(solution)/shard_map/ppermute | solution.py:333
  110.3 7.8 %collective-permute-start.26 = (f16[4,2,8,2048]{3,2,1,0:T(8,128)(2,1)S(1)}, f16[4,2,8,2048]{3,2,1,0:T(8,128)(2,1)S(1)}, u32[]{:S(2)}, u32[]{:S(2)}) collective-permute-start(f16[4,2,8,2048]{3,2,1,0:T(8,128)(2,1)S(1)} %add_convert_fusion.2), channel_id=1, source_target_pairs={{0,224},{4,228},{8,232},{12,236},{16,240},{20,244},{24,248},{28,25... | collective-permute-start | bytes 786440 | tf_op jit(solution)/shard_map/ppermute | solution.py:333
  114.2 7.8 %collective-permute-start.23 = (f16[4,2,8,2048]{3,2,1,0:T(8,128)(2,1)S(1)}, f16[4,2,8,2048]{3,2,1,0:T(8,128)(2,1)S(1)}, u32[]{:S(2)}, u32[]{:S(2)}) collective-permute-start(f16[4,2,8,2048]{3,2,1,0:T(8,128)(2,1)S(1)} %add_convert_fusion.4), channel_id=1, source_target_pairs={{0,32},{4,36},{8,40},{12,44},{16,48},{20,52},{24,56},{28,60},{32,6... | collective-permute-start | bytes 786440 | tf_op jit(solution)/shard_map/ppermute | solution.py:333
  118.2 13.8 %collective-permute-start.27 = (f16[4,2,8,2048]{3,2,1,0:T(8,128)(2,1)S(1)}, f16[4,2,8,2048]{3,2,1,0:T(8,128)(2,1)S(1)}, u32[]{:S(2)}, u32[]{:S(2)}) collective-permute-start(f16[4,2,8,2048]{3,2,1,0:T(8,128)(2,1)S(1)} %add_convert_fusion.1), channel_id=1, source_target_pairs={{0,224},{4,228},{8,232},{12,236},{16,240},{20,244},{24,248},{28,25... | collective-permute-start | bytes 786440 | tf_op jit(solution)/shard_map/ppermute | solution.py:333
  122.0 9.9 %collective-permute-start.24 = (f16[4,2,8,2048]{3,2,1,0:T(8,128)(2,1)S(1)}, f16[4,2,8,2048]{3,2,1,0:T(8,128)(2,1)S(1)}, u32[]{:S(2)}, u32[]{:S(2)}) collective-permute-start(f16[4,2,8,2048]{3,2,1,0:T(8,128)(2,1)S(1)} %add_convert_fusion.3), channel_id=1, source_target_pairs={{0,32},{4,36},{8,40},{12,44},{16,48},{20,52},{24,56},{28,60},{32,6... | collective-permute-start | bytes 786440 | tf_op jit(solution)/shard_map/ppermute | solution.py:333
  126.6 19.6 %all-to-all-start.1 = ((f16[8,2,8,2048]{3,2,1,0:T(8,128)(2,1)}), f16[8,2,8,2048]{3,2,1,0:T(8,128)(2,1)S(1)}, u32[]{:S(2)}, u32[]{:S(2)}) async-start(f16[8,2,8,2048]{3,2,1,0:T(8,128)(2,1)} %add_convert_fusion), calls=%async_computation.1 | async-start | bytes 1048576 | tf_op jit(solution)/shard_map/all_to_all | solution.py:337
  (18 other events, 209.8 us)
where the time goes:
time: 153 us; the launch traced here: 151 us
  starting transfers between devices  59 us (39%)
  waiting for transfers between devices  44.8 us (29%)
  Pallas kernels  34.7 us (23%)
  local copies, waits for them, and re-layouts  6.41 us (4%)
  other arithmetic  5.19 us (3%)
    ppermute x28, waiting for transfers between devices, send(): return lax.ppermute(value, 'img', pairs(dz, dx, dc))  42.4 us
    ppermute x28, starting transfers between devices, send(): return lax.ppermute(value, 'img', pairs(dz, dx, dc))  40.2 us
    all_to_all x2, starting transfers between devices, all_to_all_z(): lax.all_to_all(value, 'img', split_axis=0, concat_axis=0, tiled=True, axi...  13.8 us
    pallas_call x2, Pallas kernels, partial_sums(): pl.pallas_call(lambda *refs: partial_kernel(z_first, first_call, *refs),...  10.4 us
    pallas_call x2, Pallas kernels, insert(): pl.pallas_call(insert_kernel, in_specs=[VMEM] * (3 + len(first)), out_spe...  9.11 us
    pallas_call x1, Pallas kernels, score_all(): pl.pallas_call(score_kernel, in_specs=[SMEM, SMEM] + [VMEM] * (Z + X + 4)...  8.13 us
    pallas_call x2, Pallas kernels, shifted_images(): pl.pallas_call(shift_kernel, in_specs=[VMEM, VMEM], out_specs=[VMEM, VMEM...  7.07 us
    ppermute x3, starting transfers between devices, exchange_refs(): lax.ppermute(value, 'ref', [(r, (r + k) % REFS) for r in range(REFS)])  4.94 us
  transfers between devices with their start and end apart: 33, of which 17 were waited for; matrix products, arithmetic and copies ran while one was open for 4% of the time, Pallas kernels for 7%

commit v1 on v0

--- a/solution.py
+++ b/solution.py
@@ -22,6 +22,9 @@
 SCALE = 2.0 / math.sqrt(FEATURES)
 HEADROOM = 2.5
 EXTRA = 128
+SPLIT = 2560
+REST = FEATURES - SPLIT
+BORDER = SPLIT - PIX
 
 
 def shift_tables():
@@ -45,6 +48,31 @@
 
 def limit(mib):
     return pltpu.CompilerParams(vmem_limit_bytes=mib * 1024 * 1024)
+
+
+def prepare_kernel(image_ref, proj_ref, out_ref):
+    top = jnp.zeros((16, FEATURES), jnp.bfloat16)
+    for i in range(N // 16):
+        top = jnp.maximum(top, jnp.abs(image_ref[i * 16 : i * 16 + 16, :]))
+    largest = jnp.max(top.astype(jnp.float32), axis=0, keepdims=True)
+    largest = jnp.max(largest, axis=1, keepdims=True)
+    spread = jnp.broadcast_to(largest, (8, EXTRA)).astype(jnp.bfloat16)
+    for b in range(2):
+        row = proj_ref[b, :, SPLIT:]
+        for k in range(Z):
+            out_ref[k, b, :, 0:REST] = row
+            out_ref[k, b, :, REST:] = spread
+
+
+def prepare(images, projections):
+    return pl.pallas_call(
+        prepare_kernel,
+        in_specs=[VMEM, VMEM],
+        out_specs=VMEM,
+        out_shape=jax.ShapeDtypeStruct((Z, 2, 8, REST + EXTRA), jnp.bfloat16),
+        compiler_params=limit(4),
+        name="prepare",
+    )(in_vmem(images), in_vmem(projections))
 
 
 def shift_kernel(table_ref, image_ref, out_re, out_im):
@@ -104,8 +132,8 @@
             for dx in range(X):
                 o = dz * X + dx
                 first, second, zz = run_entry(sig_ref, pos_ref, q, dz, dx)
-                sel[q, o, :, 0:PIX] = by_z[dz][dx, second]
-                sel[q, o, :, PIX:] = by_x[dx][zz, second, :, 0:PIX]
+                sel[q, o, :, 0:SPLIT] = by_z[dz][dx, second]
+                sel[q, o, :, SPLIT:] = by_x[dx][zz, second, :, 0:REST]
                 live = (first + second).astype(jnp.float32)
                 mask[q, o * 8 : o * 8 + 8, :] = jnp.full((8, 128), live, jnp.float32)
     dims = (((1,), (1,)), ((), ()))
@@ -138,7 +166,7 @@
     largest = jnp.zeros((8, EXTRA), jnp.float32)
     for dx in range(X):
         for zz in range(Z):
-            largest = jnp.maximum(largest, by_x[dx][zz, 0, :, PIX:].astype(jnp.float32))
+            largest = jnp.maximum(largest, by_x[dx][zz, 0, :, REST:].astype(jnp.float32))
     stat_ref[4:5, 0:EXTRA] = jnp.max(largest, axis=0, keepdims=True)
 
 
@@ -156,7 +184,7 @@
             pltpu.VMEM((ROWS, COLS), jnp.float32),
             pltpu.VMEM((2, COLS, 128), jnp.float32),
         ],
-        compiler_params=limit(24),
+        compiler_params=limit(8),
         cost_estimate=pl.CostEstimate(
             flops=4 * ROWS * COLS * FEATURES, bytes_accessed=28 * 1024 * 1024, transcendentals=2 * ROWS * COLS
         ),
@@ -188,9 +216,10 @@
     )(in_vmem(stats), in_vmem(other))
 
 
-def partial_kernel(z_first, first_call, sig_ref, pos_ref, *refs):
-    if first_call:
-        st_ref, *every, own_ref, mate_ref, out_ref, w_ref, ev_ref = refs
+def partial_kernel(z_first, sig_ref, pos_ref, *refs):
+    if z_first:
+        st_ref, *every = refs[:5]
+        images, (out_ref, w_ref, ev_ref) = refs[5:9], refs[9:]
         for q in range(2):
             tops = [r[q : q + 1, :] for r in every]
             top = jnp.maximum(jnp.maximum(tops[0], tops[1]), jnp.maximum(tops[2], tops[3]))
@@ -198,29 +227,29 @@
             evidence = top + jnp.log(total)
             if q == 0:
                 ev_ref[...] = evidence
-
-            @pl.loop(0, SHIFTS)
-            def _(t):
-                at = pl.ds(pl.multiple_of(t * N, N), N)
-                w_ref[q, :, at] = jnp.exp(st_ref[q, :, at] - evidence).astype(jnp.bfloat16)
-
+            for t in range(SHIFTS):
+                s = st_ref[q, :, t * N : (t + 1) * N]
+                w_ref[q, :, t * N : (t + 1) * N] = jnp.exp(s - evidence).astype(jnp.bfloat16)
         bound_ref = every[0]
+        tiles = ((0, 0, PIX // PTILE), (PIX, 1, BORDER // PTILE))
     else:
-        w_ref, bound_ref, own_ref, mate_ref, out_ref = refs
+        w_ref, bound_ref = refs[:2]
+        images, (out_ref,) = refs[2:6], refs[6:]
+        tiles = ((-BORDER, 1, PIX // PTILE),)
     scale = HEADROOM / bound_ref[4:5, 0:1]
     entries = [
         [run_entry(sig_ref, pos_ref, q, dz, dx) for dz in range(Z) for dx in range(X)]
         for q in range(2)
     ]
 
-    @pl.loop(0, PIX // PTILE)
-    def _(i):
-        at = pl.ds(pl.multiple_of(i * PTILE, PTILE), PTILE)
-        for q, images in ((0, own_ref), (1, mate_ref)):
+    def one_tile(offset, half, i):
+        at_in = pl.ds(pl.multiple_of(i * PTILE, PTILE), PTILE)
+        at = pl.ds(pl.multiple_of(offset + i * PTILE, PTILE), PTILE)
+        for q in range(2):
             value = (
                 jnp.dot(
                     w_ref[q],
-                    images[:, :, at].reshape(ROWS, PTILE),
+                    images[2 * q + half][:, :, at_in].reshape(ROWS, PTILE),
                     preferred_element_type=jnp.float32,
                 )
                 * scale
@@ -237,80 +266,91 @@
                 else:
                     out_ref[rows, at] += block
 
-
-def partial_sums(z_first, sig, pos, weights, own, mate):
-    first_call = z_first
-    out_shape = [pltpu.VMEM((2 * COLS, PIX), jnp.float32)]
-    if first_call:
+    for offset, half, count in tiles:
+        start = max(0, -offset) // PTILE
+        pl.loop(start, count)(lambda i, offset=offset, half=half: one_tile(offset, half, i))
+
+
+def partial_sums(z_first, sig, pos, weights, shifted):
+    out_shape = [pltpu.VMEM((2 * COLS, SPLIT if z_first else REST), jnp.float32)]
+    if z_first:
         out_shape.append(pltpu.VMEM((2, COLS, ROWS), jnp.bfloat16))
         out_shape.append(jax.ShapeDtypeStruct((1, N), jnp.float32))
     return pl.pallas_call(
-        lambda *refs: partial_kernel(z_first, first_call, *refs),
-        in_specs=[SMEM, SMEM] + [VMEM] * (len(weights) + 2),
+        lambda *refs: partial_kernel(z_first, *refs),
+        in_specs=[SMEM, SMEM] + [VMEM] * (len(weights) + 4),
         out_specs=[VMEM] * len(out_shape),
         out_shape=out_shape,
-        compiler_params=limit(12),
+        compiler_params=limit(4),
         cost_estimate=pl.CostEstimate(
             flops=2 * ROWS * COLS * FEATURES, bytes_accessed=16 * 1024 * 1024, transcendentals=0
         ),
-        name="partial_re" if first_call else "partial_im",
-    )(sig, pos, *[in_vmem(v) for v in weights], in_vmem(own), in_vmem(mate))
+        name="partial_first" if z_first else "partial_rest",
+    )(sig, pos, *[in_vmem(v) for v in weights], *[in_vmem(v) for v in shifted])
 
 
 HIGH, LOW = 32, 128
-PART = 2048
 
 
 def insert_kernel(bound_ref, w_ref, ins_ref, *refs):
     scale = bound_ref[4:5, 0:1] * (1.0 / HEADROOM)
-    high_ids = lax.broadcasted_iota(jnp.int32, (HIGH, PART), 0)
-    low_ids = lax.broadcasted_iota(jnp.int32, (LOW, PART), 0)
-
-    def body(i, acc):
+    rest = len(refs) == 3
+
+    def add(acc, i, at, at_ids, width):
         row = pl.ds(i, 1)
-        for j in range(PIX // PART):
-            at = slice(j * PART, (j + 1) * PART)
-            ids = ins_ref[row, at]
-            high = lax.shift_right_logical(ids, 7)
-            low = lax.bitwise_and(ids, LOW - 1)
-            value = w_ref[row, at] * scale
-            head = value.astype(jnp.bfloat16).astype(jnp.float32)
-            tail = value - head
-            here = high == high_ids
-            rows = jnp.concatenate(
-                [jnp.where(here, head, 0.0), jnp.where(here, tail, 0.0)], axis=0
-            ).astype(jnp.bfloat16)
-            table = jnp.where(low == low_ids, 1.0, 0.0).astype(jnp.bfloat16)
-            acc = acc + lax.dot_general(
-                rows, table, (((1,), (1,)), ((), ())), preferred_element_type=jnp.float32
-            )
-        return acc
-
-    acc = lax.fori_loop(0, 16, body, jnp.zeros((2 * HIGH, LOW), jnp.float32), unroll=2)
-    slab = acc[:HIGH] + acc[HIGH:]
-    if len(refs) == 1:
-        refs[0][...] = slab
-    else:
-        first_ref, out_ref = refs
+        ids = ins_ref[row, at_ids]
+        high = lax.shift_right_logical(ids, 7)
+        low = lax.bitwise_and(ids, LOW - 1)
+        value = w_ref[row, at] * scale
+        head = value.astype(jnp.bfloat16).astype(jnp.float32)
+        tail = value - head
+        here = high == lax.broadcasted_iota(jnp.int32, (HIGH, width), 0)
+        rows = jnp.concatenate(
+            [jnp.where(here, head, 0.0), jnp.where(here, tail, 0.0)], axis=0
+        ).astype(jnp.bfloat16)
+        there = low == lax.broadcasted_iota(jnp.int32, (LOW, width), 0)
+        table = jnp.where(there, 1.0, 0.0).astype(jnp.bfloat16)
+        return acc + lax.dot_general(
+            rows, table, (((1,), (1,)), ((), ())), preferred_element_type=jnp.float32
+        )
+
+    empty = jnp.zeros((2 * HIGH, LOW), jnp.float32)
+    if rest:
+        re_ref, im_ref, out_ref = refs
+        step = lambda i, acc: add(acc, i, slice(0, REST), slice(BORDER, PIX), REST)
+        acc = lax.fori_loop(0, 16, step, empty, unroll=2)
+        slab = im_ref[...] + acc[:HIGH] + acc[HIGH:]
         for h in range(HIGH):
             at = slice(h * LOW, (h + 1) * LOW)
-            out_ref[0:1, at] = first_ref[h : h + 1, :]
+            out_ref[0:1, at] = re_ref[h : h + 1, :]
             out_ref[1:2, at] = slab[h : h + 1, :]
-
-
-def insert(bound, weighted, insertion, *first):
-    shape = (2, VOX) if first else (HIGH, LOW)
+    else:
+        re_ref, im_ref = refs
+
+        def step(i, both):
+            re, im = both
+            re = add(re, i, slice(0, PIX), slice(0, PIX), PIX)
+            im = add(im, i, slice(PIX, SPLIT), slice(0, BORDER), BORDER)
+            return re, im
+
+        re, im = lax.fori_loop(0, 16, step, (empty, empty))
+        re_ref[...] = re[:HIGH] + re[HIGH:]
+        im_ref[...] = im[:HIGH] + im[HIGH:]
+
+
+def insert(bound, weighted, insertion, *slabs):
+    slab = jax.ShapeDtypeStruct((HIGH, LOW), jnp.float32)
     return pl.pallas_call(
         insert_kernel,
-        in_specs=[VMEM] * (3 + len(first)),
-        out_specs=VMEM,
-        out_shape=jax.ShapeDtypeStruct(shape, jnp.float32),
+        in_specs=[VMEM] * (3 + len(slabs)),
+        out_specs=VMEM if slabs else [VMEM, VMEM],
+        out_shape=jax.ShapeDtypeStruct((2, VOX), jnp.float32) if slabs else [slab, slab],
         compiler_params=limit(8),
         cost_estimate=pl.CostEstimate(
             flops=4 * HIGH * LOW * 16 * PIX, bytes_accessed=512 * 1024, transcendentals=0
         ),
-        name="insert_im" if first else "insert_re",
-    )(bound, weighted.reshape(16, PIX), insertion, *first)
+        name="insert_rest" if slabs else "insert_first",
+    )(bound, weighted.reshape(16, weighted.shape[-1]), insertion, *slabs)
 
 
 def img_index(z, x, c):
@@ -352,8 +392,7 @@
     return [out[k] for k in range(Z)]
 
 
-def gather_z_first(unit):
-    copies = jnp.broadcast_to(unit[None], (Z,) + unit.shape)
+def gather_z_first(copies):
     column = all_to_all_z(copies)
     return [column, send(column, dx=-1), send(column, dx=-2), send(column, dx=1)]
 
@@ -405,28 +444,24 @@
     table = jnp.asarray(shift_tables())
 
     mate = send(particles, dc=1)
-    by_z = gather_x_first(projections[:, :, :PIX])
-    largest = jnp.max(jnp.abs(particles))
-    unit = jnp.concatenate(
-        [projections[:, :, PIX:], jnp.broadcast_to(largest, (2, 8, EXTRA))], axis=2
-    )
-    unit, pos, sig = lax.optimization_barrier((unit, pos, sig))
-    by_x = gather_z_first(unit)
+    by_z = gather_x_first(projections[:, :, :SPLIT])
+    copies = prepare(particles, projections)
+    copies, pos, sig = lax.optimization_barrier((copies, pos, sig))
+    by_x = gather_z_first(copies)
     own_re, own_im = shifted_images(table, particles)
     mate_re, mate_im = shifted_images(table, mate)
 
-    scores, stats = score_all(sig, pos, by_z, by_x, (own_re, own_im, mate_re, mate_im))
+    shifted = (own_re, own_im, mate_re, mate_im)
+    scores, stats = score_all(sig, pos, by_z, by_x, shifted)
     merged = merge(stats, send(stats, dc=1))
     every = exchange_refs(merged)
-    sums_re, weights, evidence = partial_sums(
-        True, sig, pos, (scores, *every), own_re, mate_re
-    )
-    (sums_im,) = partial_sums(False, sig, pos, (weights, merged), own_im, mate_im)
-    total_re = scatter_z_first(sums_re.reshape(Z, X, 2, 8, PIX))
-    total_im = scatter_x_first(sums_im.reshape(X, Z, 2, 8, PIX))
+    sums, weights, evidence = partial_sums(True, sig, pos, (scores, *every), shifted)
+    (sums_rest,) = partial_sums(False, sig, pos, (weights, merged), shifted)
+    total = scatter_z_first(sums.reshape(Z, X, 2, 8, SPLIT))
+    total_rest = scatter_x_first(sums_rest.reshape(X, Z, 2, 8, REST))
     ids = insertion.reshape(16, PIX)
-    volume_re = insert(merged, total_re, ids)
-    volume = insert(merged, total_im, ids, volume_re)
+    slabs = insert(merged, total, ids)
+    volume = insert(merged, total_rest, ids, *slabs)
     return volume, evidence.reshape(N)
 
 

time: 153 us -> 156 us (1.020)
  the two profiles are of different devices: /device:TPU:8 before, /device:TPU:128 now
where the time goes in v1:
time: 156 us
  starting transfers between devices  59.9 us (38%)
  waiting for transfers between devices  51.6 us (33%)
  Pallas kernels  35.5 us (23%)
  local copies, waits for them, and re-layouts  5.42 us (3%)
  other arithmetic  2.35 us (2%)
    ppermute x28, waiting for transfers between devices, send(): return lax.ppermute(value, 'img', pairs(dz, dx, dc))  47.7 us
    ppermute x28, starting transfers between devices, send(): return lax.ppermute(value, 'img', pairs(dz, dx, dc))  40.2 us
    all_to_all x2, starting transfers between devices, all_to_all_z(): lax.all_to_all(value, 'img', split_axis=0, concat_axis=0, tiled=True, axi...  15.1 us
    pallas_call x2, Pallas kernels, insert(): pl.pallas_call(insert_kernel, in_specs=[VMEM] * (3 + len(slabs)), out_spe...  10.7 us
    pallas_call x2, Pallas kernels, partial_sums(): pl.pallas_call(lambda *refs: partial_kernel(z_first, *refs), in_specs=[SM...  9.86 us
    pallas_call x1, Pallas kernels, score_all(): pl.pallas_call(score_kernel, in_specs=[SMEM, SMEM] + [VMEM] * (Z + X + 4)...  8.25 us
    pallas_call x2, Pallas kernels, shifted_images(): pl.pallas_call(shift_kernel, in_specs=[VMEM, VMEM], out_specs=[VMEM, VMEM...  5.51 us
    ppermute x3, starting transfers between devices, exchange_refs(): lax.ppermute(value, 'ref', [(r, (r + k) % REFS) for r in range(REFS)])  4.62 us
  transfers between devices with their start and end apart: 33, of which 20 were waited for; matrix products, arithmetic and copies ran while one was open for 2% of the time, Pallas kernels for 4%

profile of v1, /device:TPU:128, one launch (start us, length us, event | category | flops | bytes accessed | tf_op | source)
XLA Modules:
  0.0 155.7 jit_solution(14593282770818597321)
XLA Ops:
  1.7 3.1 %collective-permute-start.1 = (bf16[2,8,2560]{2,1,0:T(8,128)(2,1)S(1)}, bf16[2,8,2560]{2,1,0:T(8,128)(2,1)S(1)}, u32[]{:S(2)}, u32[]{:S(2)}) collective-permute-start(bf16[2,8,2560]{2,1,0:T(8,128)(2,1)S(1)} %get-tuple-element.47), channel_id=1, source_target_pairs={{0,16},{4,20},{8,24},{12,28},{16,0},{20,4},{24,8},{28,12},{32,48},... | collective-permute-start | bytes 245768 | tf_op jit(solution)/shard_map/ppermute | solution.py:373
  16.4 7.2 %all-to-all-start = ((bf16[8,2,8,1664]{3,2,1,0:T(8,128)(2,1)}), bf16[8,2,8,1664]{3,2,1,0:T(8,128)(2,1)S(1)}, u32[]{:S(2)}, u32[]{:S(2)}) async-start(bf16[8,2,8,1664]{3,2,1,0:T(8,128)(2,1)} %prepare.1), calls=%async_computation | async-start | bytes 851968 | tf_op jit(solution)/shard_map/all_to_all | solution.py:377
  25.6 13.8 %collective-permute-done.3.refs_1_ = bf16[4,2,8,2560]{3,2,1,0:T(8,128)(2,1)} collective-permute-done((bf16[4,2,8,2560]{3,2,1,0:T(8,128)(2,1)S(1)}, bf16[4,2,8,2560]{3,2,1,0:T(8,128)(2,1)}, u32[]{:S(2)}, u32[]{:S(2)}) %collective-permute-start.3) | collective-permute-done | bytes 327712 | tf_op jit(solution)/shard_map/ppermute | solution.py:373
  39.4 2.7 %collective-permute-start.4 = (bf16[4,2,8,2560]{3,2,1,0:T(8,128)(2,1)}, bf16[4,2,8,2560]{3,2,1,0:T(8,128)(2,1)}, u32[]{:S(2)}, u32[]{:S(2)}) collective-permute-start(bf16[4,2,8,2560]{3,2,1,0:T(8,128)(2,1)} %collective-permute-done.3.refs_1_), channel_id=1, source_target_pairs={{0,224},{4,228},{8,232},{12,236},{16,240},{20,244},{24,248},{28,25... | collective-permute-start | bytes 983048 | tf_op jit(solution)/shard_map/ppermute | solution.py:373
  43.2 2.6 %collective-permute-start.11 = (bf16[8,2,8,1664]{3,2,1,0:T(8,128)(2,1)S(1)}, bf16[8,2,8,1664]{3,2,1,0:T(8,128)(2,1)S(1)}, u32[]{:S(2)}, u32[]{:S(2)}) collective-permute-start(bf16[8,2,8,1664]{3,2,1,0:T(8,128)(2,1)S(1)} %all-to-all-done.refs_8_), channel_id=1, source_target_pairs={{0,16},{4,20},{8,24},{12,28},{16,0},{20,4},{24,8},{28,12},{32,48},... | collective-permute-start | bytes 1277960 | tf_op jit(solution)/shard_map/ppermute | solution.py:373
  45.8 2.6 %collective-permute-done.4.refs_2_ = bf16[4,2,8,2560]{3,2,1,0:T(8,128)(2,1)} collective-permute-done((bf16[4,2,8,2560]{3,2,1,0:T(8,128)(2,1)}, bf16[4,2,8,2560]{3,2,1,0:T(8,128)(2,1)}, u32[]{:S(2)}, u32[]{:S(2)}) %collective-permute-start.4) | collective-permute-done | bytes 327712 | tf_op jit(solution)/shard_map/ppermute | solution.py:373
  56.4 3.5 %shift.3 = (bf16[5,256,2048]{2,1,0:T(8,128)(2,1)S(1)}, bf16[5,256,2048]{2,1,0:T(8,128)(2,1)S(1)}) custom-call(f32[8,2048]{1,0:T(8,128)S(1)} %copy-done.5, bf16[256,4096]{1,0:T(8,128)(2,1)} %collective-permute-done.13.image_ref), custom_call_target="tpu_custom_call" | custom-call | flops 12582912 | bytes 12582912 | tf_op jit(solution)/shard_map/shift/pallas_call | solution.py:102
  60.0 3.4 %collective-permute-done.11.refs_10_ = bf16[8,2,8,1664]{3,2,1,0:T(8,128)(2,1)S(1)} collective-permute-done((bf16[8,2,8,1664]{3,2,1,0:T(8,128)(2,1)S(1)}, bf16[8,2,8,1664]{3,2,1,0:T(8,128)(2,1)S(1)}, u32[]{:S(2)}, u32[]{:S(2)}) %collective-permute-start.11) | collective-permute-done | bytes 426016 | tf_op jit(solution)/shard_map/ppermute | solution.py:373
  63.5 8.2 %scores.1 = (f32[2,256,1280]{2,1,0:T(8,128)S(1)}, f32[8,256]{1,0:T(8,128)S(1)}) custom-call(s32[2,512]{1,0:T(2,128)S(1)} %constant_dynamic-slice_fusion.sig_ref.refs_0_, s32[4]{0:T(128)S(1)} %pad_add_fusion.pos_ref.refs_1_, bf16[4,2,8,2560]{3,2,1,0:T(8,128)(2,1)S(1)} %pad_maximum_fusion.refs_0_, bf16[4,2,8,2560]{3,2,1,0:T(8,128)(2,1)} %collective-permute-done.3.refs_1_, ...), custom_call_target="tpu_custom_call" | custom-call | flops 5368709120 | bytes 29360128 | tf_op jit(solution)/shard_map/scores/pallas_call | solution.py:174
  73.1 3.0 %collective-permute-start.17 = (f32[8,256]{1,0:T(8,128)S(1)}, f32[8,256]{1,0:T(8,128)S(1)}, u32[]{:S(2)}, u32[]{:S(2)}) collective-permute-start(f32[8,256]{1,0:T(8,128)S(1)} %merge.1.refs_3_.bound_ref), channel_id=1, source_target_pairs={{0,3},{1,0},{2,1},{3,2},{4,7},{5,4},{6,5},{7,6},{8,11},{9,8},{10,9... | collective-permute-start | bytes 24584 | tf_op jit(solution)/shard_map/ppermute | solution.py:434
  77.7 3.5 %collective-permute-done.16.refs_5_ = f32[8,256]{1,0:T(8,128)S(1)} collective-permute-done((f32[8,256]{1,0:T(8,128)S(1)}, f32[8,256]{1,0:T(8,128)S(1)}, u32[]{:S(2)}, u32[]{:S(2)}) %collective-permute-start.16) | collective-permute-done | bytes 8224 | tf_op jit(solution)/shard_map/ppermute | solution.py:434
  81.6 6.1 %partial_first.1 = (f32[512,2560]{1,0:T(8,128)S(1)}, bf16[2,256,1280]{2,1,0:T(8,128)(2,1)S(1)}, f32[1,256]{1,0:T(1,128)}) custom-call(s32[2,512]{1,0:T(2,128)S(1)} %constant_dynamic-slice_fusion.sig_ref.refs_0_, s32[4]{0:T(128)S(1)} %pad_add_fusion.pos_ref.refs_1_, f32[2,256,1280]{2,1,0:T(8,128)S(1)} %get-tuple-element.24.refs_2_, ...), custom_call_target="tpu_custom_call" | custom-call | flops 2684354560 | bytes 16777216 | tf_op jit(solution)/shard_map/partial_first/pallas_call | solution.py:279
  87.7 3.7 %partial_rest.1 = f32[512,1536]{1,0:T(8,128)S(1)} custom-call(s32[2,512]{1,0:T(2,128)S(1)} %constant_dynamic-slice_fusion.sig_ref.refs_0_, s32[4]{0:T(128)S(1)} %pad_add_fusion.pos_ref.refs_1_, bf16[2,256,1280]{2,1,0:T(8,128)(2,1)S(1)} %get-tuple-element.25.refs_2_, f32[8,256]{1,0:T(8,128)S(1)} %merge.1.refs_3_.bound_ref, ...), custom_call_target="tpu_custom_call" | custom-call | flops 2684354560 | bytes 16777216 | tf_op jit(solution)/shard_map/partial_rest/pallas_call | solution.py:279
  94.1 2.7 %collective-permute-start.20 = (f16[8,2,8,1536]{3,2,1,0:T(8,128)(2,1)S(1)}, f16[8,2,8,1536]{3,2,1,0:T(8,128)(2,1)S(1)}, u32[]{:S(2)}, u32[]{:S(2)}) collective-permute-start(f16[8,2,8,1536]{3,2,1,0:T(8,128)(2,1)S(1)} %bitcast.54), channel_id=1, source_target_pairs={{0,24},{4,28},{8,0},{12,4},{16,8},{20,12},{24,16},{28,20},{32,56},... | collective-permute-start | bytes 1179656 | tf_op jit(solution)/shard_map/ppermute | solution.py:373
  98.8 3.2 %collective-permute-start.25 = (f16[4,2,8,2560]{3,2,1,0:T(8,128)(2,1)S(1)}, f16[4,2,8,2560]{3,2,1,0:T(8,128)(2,1)S(1)}, u32[]{:S(2)}, u32[]{:S(2)}) collective-permute-start(f16[4,2,8,2560]{3,2,1,0:T(8,128)(2,1)S(1)} %bitcast.55), channel_id=1, source_target_pairs={{0,224},{4,228},{8,232},{12,236},{16,240},{20,244},{24,248},{28,25... | collective-permute-start | bytes 983048 | tf_op jit(solution)/shard_map/ppermute | solution.py:373
  103.4 3.2 %collective-permute-done.25 = f16[4,2,8,2560]{3,2,1,0:T(8,128)(2,1)S(1)} collective-permute-done((f16[4,2,8,2560]{3,2,1,0:T(8,128)(2,1)S(1)}, f16[4,2,8,2560]{3,2,1,0:T(8,128)(2,1)S(1)}, u32[]{:S(2)}, u32[]{:S(2)}) %collective-permute-start.25) | collective-permute-done | bytes 327712 | tf_op jit(solution)/shard_map/ppermute | solution.py:373
  106.7 3.8 %collective-permute-start.26 = (f16[4,2,8,2560]{3,2,1,0:T(8,128)(2,1)S(1)}, f16[4,2,8,2560]{3,2,1,0:T(8,128)(2,1)S(1)}, u32[]{:S(2)}, u32[]{:S(2)}) collective-permute-start(f16[4,2,8,2560]{3,2,1,0:T(8,128)(2,1)S(1)} %add_convert_fusion.2), channel_id=1, source_target_pairs={{0,224},{4,228},{8,232},{12,236},{16,240},{20,244},{24,248},{28,25... | collective-permute-start | bytes 983048 | tf_op jit(solution)/shard_map/ppermute | solution.py:373
  112.0 3.4 %collective-permute-done.26 = f16[4,2,8,2560]{3,2,1,0:T(8,128)(2,1)S(1)} collective-permute-done((f16[4,2,8,2560]{3,2,1,0:T(8,128)(2,1)S(1)}, f16[4,2,8,2560]{3,2,1,0:T(8,128)(2,1)S(1)}, u32[]{:S(2)}, u32[]{:S(2)}) %collective-permute-start.26) | collective-permute-done | bytes 327712 | tf_op jit(solution)/shard_map/ppermute | solution.py:373
  115.5 3.8 %collective-permute-start.27 = (f16[4,2,8,2560]{3,2,1,0:T(8,128)(2,1)S(1)}, f16[4,2,8,2560]{3,2,1,0:T(8,128)(2,1)S(1)}, u32[]{:S(2)}, u32[]{:S(2)}) collective-permute-start(f16[4,2,8,2560]{3,2,1,0:T(8,128)(2,1)S(1)} %add_convert_fusion.1), channel_id=1, source_target_pairs={{0,224},{4,228},{8,232},{12,236},{16,240},{20,244},{24,248},{28,25... | collective-permute-start | bytes 983048 | tf_op jit(solution)/shard_map/ppermute | solution.py:373
  121.9 7.9 %all-to-all-start.1 = ((f16[8,2,8,1536]{3,2,1,0:T(8,128)(2,1)}), f16[8,2,8,1536]{3,2,1,0:T(8,128)(2,1)S(1)}, u32[]{:S(2)}, u32[]{:S(2)}) async-start(f16[8,2,8,1536]{3,2,1,0:T(8,128)(2,1)} %add_convert_fusion), calls=%async_computation.1 | async-start | bytes 786432 | tf_op jit(solution)/shard_map/all_to_all | solution.py:377
  129.7 5.7 %collective-permute-done.24 = f16[4,2,8,2560]{3,2,1,0:T(8,128)(2,1)S(1)} collective-permute-done((f16[4,2,8,2560]{3,2,1,0:T(8,128)(2,1)S(1)}, f16[4,2,8,2560]{3,2,1,0:T(8,128)(2,1)S(1)}, u32[]{:S(2)}, u32[]{:S(2)}) %collective-permute-start.24) | collective-permute-done | bytes 327712 | tf_op jit(solution)/shard_map/ppermute | solution.py:373
  142.1 2.8 %collective-permute-done.29 = f16[2,8,2560]{2,1,0:T(8,128)(2,1)S(1)} collective-permute-done((f16[2,8,2560]{2,1,0:T(8,128)(2,1)S(1)}, f16[2,8,2560]{2,1,0:T(8,128)(2,1)S(1)}, u32[]{:S(2)}, u32[]{:S(2)}) %collective-permute-start.29) | collective-permute-done | bytes 81952 | tf_op jit(solution)/shard_map/ppermute | solution.py:373
  144.9 6.5 %insert_first.1 = (f32[32,128]{1,0:T(8,128)S(1)}, f32[32,128]{1,0:T(8,128)S(1)}) custom-call(f32[8,256]{1,0:T(8,128)S(1)} %merge.1.refs_3_.bound_ref, f32[16,2560]{1,0:T(8,128)S(1)} %fusion.3.w_ref, s32[16,2048]{1,0:T(8,128)S(1)} %bitcast.44), custom_call_target="tpu_custom_call" | custom-call | flops 536870912 | bytes 524288 | tf_op jit(solution)/shard_map/insert_first/pallas_call | solution.py:343
  151.5 4.2 %insert_rest.1 = f32[2,4096]{1,0:T(2,128)} custom-call(f32[8,256]{1,0:T(8,128)S(1)} %merge.1.refs_3_.bound_ref, f32[16,1536]{1,0:T(8,128)S(1)} %bitcast.43, s32[16,2048]{1,0:T(8,128)S(1)} %bitcast.45, f32[32,128]{1,0:T(8,128)S(1)} %get-tuple-element.27.refs_0_, f32[32,128]{1,0:T(8,128)S(1)} %get-tuple-element.28.refs_1_), custom_call_target="tpu_custom_call" | custom-call | flops 536870912 | bytes 524288 | tf_op jit(solution)/shard_map/insert_rest/pallas_call | solution.py:343
  (86 shorter events, 43.9 us)
Async XLA Ops:
  0.7 53.8 %collective-permute-start.13 = (bf16[256,4096]{1,0:T(8,128)(2,1)}, bf16[256,4096]{1,0:T(8,128)(2,1)}, u32[]{:S(2)}, u32[]{:S(2)}) collective-permute-start(bf16[256,4096]{1,0:T(8,128)(2,1)} %image_ref.3), channel_id=1, source_target_pairs={{0,4},{4,0},{8,12},{12,8},{16,20},{20,16},{24,28},{28,24},{32,36},... | collective-permute-start | bytes 6291464 | tf_op jit(solution)/shard_map/ppermute | solution.py:373
  1.7 6.4 %collective-permute-start.1 = (bf16[2,8,2560]{2,1,0:T(8,128)(2,1)S(1)}, bf16[2,8,2560]{2,1,0:T(8,128)(2,1)S(1)}, u32[]{:S(2)}, u32[]{:S(2)}) collective-permute-start(bf16[2,8,2560]{2,1,0:T(8,128)(2,1)S(1)} %get-tuple-element.47), channel_id=1, source_target_pairs={{0,16},{4,20},{8,24},{12,28},{16,0},{20,4},{24,8},{28,12},{32,48},... | collective-permute-start | bytes 245768 | tf_op jit(solution)/shard_map/ppermute | solution.py:373
  11.6 12.5 %collective-permute-start.6 = (bf16[4,2,8,2560]{3,2,1,0:T(8,128)(2,1)S(1)}, bf16[4,2,8,2560]{3,2,1,0:T(8,128)(2,1)S(1)}, u32[]{:S(2)}, u32[]{:S(2)}) collective-permute-start(bf16[4,2,8,2560]{3,2,1,0:T(8,128)(2,1)S(1)} %pad_maximum_fusion.refs_0_), channel_id=1, source_target_pairs={{0,32},{4,36},{8,40},{12,44},{16,48},{20,52},{24,56},{28,60},{32,6... | collective-permute-start | bytes 983048 | tf_op jit(solution)/shard_map/ppermute | solution.py:373
  16.4 25.7 %all-to-all-start = ((bf16[8,2,8,1664]{3,2,1,0:T(8,128)(2,1)}), bf16[8,2,8,1664]{3,2,1,0:T(8,128)(2,1)S(1)}, u32[]{:S(2)}, u32[]{:S(2)}) async-start(bf16[8,2,8,1664]{3,2,1,0:T(8,128)(2,1)} %prepare.1), calls=%async_computation | async-start | bytes 851968 | tf_op jit(solution)/shard_map/all_to_all | solution.py:377
  23.6 15.8 %collective-permute-start.3 = (bf16[4,2,8,2560]{3,2,1,0:T(8,128)(2,1)S(1)}, bf16[4,2,8,2560]{3,2,1,0:T(8,128)(2,1)}, u32[]{:S(2)}, u32[]{:S(2)}) collective-permute-start(bf16[4,2,8,2560]{3,2,1,0:T(8,128)(2,1)S(1)} %pad_maximum_fusion.refs_0_), channel_id=1, source_target_pairs={{0,224},{4,228},{8,232},{12,236},{16,240},{20,244},{24,248},{28,25... | collective-permute-start | bytes 983048 | tf_op jit(solution)/shard_map/ppermute | solution.py:373
  24.2 17.9 %collective-permute-start.7 = (bf16[4,2,8,2560]{3,2,1,0:T(8,128)(2,1)S(1)}, bf16[4,2,8,2560]{3,2,1,0:T(8,128)(2,1)}, u32[]{:S(2)}, u32[]{:S(2)}) collective-permute-start(bf16[4,2,8,2560]{3,2,1,0:T(8,128)(2,1)S(1)} %collective-permute-done.6.refs_7_), channel_id=1, source_target_pairs={{0,32},{4,36},{8,40},{12,44},{16,48},{20,52},{24,56},{28,60},{32,6... | collective-permute-start | bytes 983048 | tf_op jit(solution)/shard_map/ppermute | solution.py:373
  39.4 9.1 %collective-permute-start.4 = (bf16[4,2,8,2560]{3,2,1,0:T(8,128)(2,1)}, bf16[4,2,8,2560]{3,2,1,0:T(8,128)(2,1)}, u32[]{:S(2)}, u32[]{:S(2)}) collective-permute-start(bf16[4,2,8,2560]{3,2,1,0:T(8,128)(2,1)} %collective-permute-done.3.refs_1_), channel_id=1, source_target_pairs={{0,224},{4,228},{8,232},{12,236},{16,240},{20,244},{24,248},{28,25... | collective-permute-start | bytes 983048 | tf_op jit(solution)/shard_map/ppermute | solution.py:373
  42.1 9.8 %collective-permute-start.8 = (bf16[4,2,8,2560]{3,2,1,0:T(8,128)(2,1)}, bf16[4,2,8,2560]{3,2,1,0:T(8,128)(2,1)}, u32[]{:S(2)}, u32[]{:S(2)}) collective-permute-start(bf16[4,2,8,2560]{3,2,1,0:T(8,128)(2,1)} %collective-permute-done.7.refs_6_), channel_id=1, source_target_pairs={{0,32},{4,36},{8,40},{12,44},{16,48},{20,52},{24,56},{28,60},{32,6... | collective-permute-start | bytes 983048 | tf_op jit(solution)/shard_map/ppermute | solution.py:373
  42.1 17.9 %collective-permute-start.12 = (bf16[8,2,8,1664]{3,2,1,0:T(8,128)(2,1)S(1)}, bf16[8,2,8,1664]{3,2,1,0:T(8,128)(2,1)S(1)}, u32[]{:S(2)}, u32[]{:S(2)}) collective-permute-start(bf16[8,2,8,1664]{3,2,1,0:T(8,128)(2,1)S(1)} %all-to-all-done.refs_8_), channel_id=1, source_target_pairs={{0,8},{4,12},{8,16},{12,20},{16,24},{20,28},{24,0},{28,4},{32,40},... | collective-permute-start | bytes 1277960 | tf_op jit(solution)/shard_map/ppermute | solution.py:373
  43.2 20.2 %collective-permute-start.11 = (bf16[8,2,8,1664]{3,2,1,0:T(8,128)(2,1)S(1)}, bf16[8,2,8,1664]{3,2,1,0:T(8,128)(2,1)S(1)}, u32[]{:S(2)}, u32[]{:S(2)}) collective-permute-start(bf16[8,2,8,1664]{3,2,1,0:T(8,128)(2,1)S(1)} %all-to-all-done.refs_8_), channel_id=1, source_target_pairs={{0,16},{4,20},{8,24},{12,28},{16,0},{20,4},{24,8},{28,12},{32,48},... | collective-permute-start | bytes 1277960 | tf_op jit(solution)/shard_map/ppermute | solution.py:373
  48.5 15.0 %collective-permute-start.10 = (bf16[8,2,8,1664]{3,2,1,0:T(8,128)(2,1)S(1)}, bf16[8,2,8,1664]{3,2,1,0:T(8,128)(2,1)S(1)}, u32[]{:S(2)}, u32[]{:S(2)}) collective-permute-start(bf16[8,2,8,1664]{3,2,1,0:T(8,128)(2,1)S(1)} %all-to-all-done.refs_8_), channel_id=1, source_target_pairs={{0,24},{4,28},{8,0},{12,4},{16,8},{20,12},{24,16},{28,20},{32,56},... | collective-permute-start | bytes 1277960 | tf_op jit(solution)/shard_map/ppermute | solution.py:373
  51.9 8.1 %collective-permute-start.5 = (bf16[4,2,8,2560]{3,2,1,0:T(8,128)(2,1)}, bf16[4,2,8,2560]{3,2,1,0:T(8,128)(2,1)S(1)}, u32[]{:S(2)}, u32[]{:S(2)}) collective-permute-start(bf16[4,2,8,2560]{3,2,1,0:T(8,128)(2,1)} %collective-permute-done.4.refs_2_), channel_id=1, source_target_pairs={{0,224},{4,228},{8,232},{12,236},{16,240},{20,244},{24,248},{28,25... | collective-permute-start | bytes 983048 | tf_op jit(solution)/shard_map/ppermute | solution.py:373
  54.4 9.1 %collective-permute-start.9 = (bf16[4,2,8,2560]{3,2,1,0:T(8,128)(2,1)}, bf16[4,2,8,2560]{3,2,1,0:T(8,128)(2,1)S(1)}, u32[]{:S(2)}, u32[]{:S(2)}) collective-permute-start(bf16[4,2,8,2560]{3,2,1,0:T(8,128)(2,1)} %collective-permute-done.8.refs_5_), channel_id=1, source_target_pairs={{0,32},{4,36},{8,40},{12,44},{16,48},{20,52},{24,56},{28,60},{32,6... | collective-permute-start | bytes 983048 | tf_op jit(solution)/shard_map/ppermute | solution.py:373
  93.8 9.4 %collective-permute-start.21 = (f16[4,2,8,2560]{3,2,1,0:T(8,128)(2,1)S(1)}, f16[4,2,8,2560]{3,2,1,0:T(8,128)(2,1)S(1)}, u32[]{:S(2)}, u32[]{:S(2)}) collective-permute-start(f16[4,2,8,2560]{3,2,1,0:T(8,128)(2,1)S(1)} %bitcast.56), channel_id=1, source_target_pairs={{0,32},{4,36},{8,40},{12,44},{16,48},{20,52},{24,56},{28,60},{32,6... | collective-permute-start | bytes 983048 | tf_op jit(solution)/shard_map/ppermute | solution.py:373
  94.1 26.8 %collective-permute-start.20 = (f16[8,2,8,1536]{3,2,1,0:T(8,128)(2,1)S(1)}, f16[8,2,8,1536]{3,2,1,0:T(8,128)(2,1)S(1)}, u32[]{:S(2)}, u32[]{:S(2)}) collective-permute-start(f16[8,2,8,1536]{3,2,1,0:T(8,128)(2,1)S(1)} %bitcast.54), channel_id=1, source_target_pairs={{0,24},{4,28},{8,0},{12,4},{16,8},{20,12},{24,16},{28,20},{32,56},... | collective-permute-start | bytes 1179656 | tf_op jit(solution)/shard_map/ppermute | solution.py:373
  96.8 24.0 %collective-permute-start.18 = (f16[8,2,8,1536]{3,2,1,0:T(8,128)(2,1)S(1)}, f16[8,2,8,1536]{3,2,1,0:T(8,128)(2,1)S(1)}, u32[]{:S(2)}, u32[]{:S(2)}) collective-permute-start(f16[8,2,8,1536]{3,2,1,0:T(8,128)(2,1)S(1)} %bitcast.53), channel_id=1, source_target_pairs={{0,8},{4,12},{8,16},{12,20},{16,24},{20,28},{24,0},{28,4},{32,40},... | collective-permute-start | bytes 1179656 | tf_op jit(solution)/shard_map/ppermute | solution.py:373
  96.8 24.1 %collective-permute-start.19 = (f16[8,2,8,1536]{3,2,1,0:T(8,128)(2,1)S(1)}, f16[8,2,8,1536]{3,2,1,0:T(8,128)(2,1)S(1)}, u32[]{:S(2)}, u32[]{:S(2)}) collective-permute-start(f16[8,2,8,1536]{3,2,1,0:T(8,128)(2,1)S(1)} %bitcast.52), channel_id=1, source_target_pairs={{0,16},{4,20},{8,24},{12,28},{16,0},{20,4},{24,8},{28,12},{32,48},... | collective-permute-start | bytes 1179656 | tf_op jit(solution)/shard_map/ppermute | solution.py:373
  98.8 7.8 %collective-permute-start.25 = (f16[4,2,8,2560]{3,2,1,0:T(8,128)(2,1)S(1)}, f16[4,2,8,2560]{3,2,1,0:T(8,128)(2,1)S(1)}, u32[]{:S(2)}, u32[]{:S(2)}) collective-permute-start(f16[4,2,8,2560]{3,2,1,0:T(8,128)(2,1)S(1)} %bitcast.55), channel_id=1, source_target_pairs={{0,224},{4,228},{8,232},{12,236},{16,240},{20,244},{24,248},{28,25... | collective-permute-start | bytes 983048 | tf_op jit(solution)/shard_map/ppermute | solution.py:373
  103.3 8.5 %collective-permute-start.22 = (f16[4,2,8,2560]{3,2,1,0:T(8,128)(2,1)S(1)}, f16[4,2,8,2560]{3,2,1,0:T(8,128)(2,1)S(1)}, u32[]{:S(2)}, u32[]{:S(2)}) collective-permute-start(f16[4,2,8,2560]{3,2,1,0:T(8,128)(2,1)S(1)} %add_convert_fusion.5), channel_id=1, source_target_pairs={{0,32},{4,36},{8,40},{12,44},{16,48},{20,52},{24,56},{28,60},{32,6... | collective-permute-start | bytes 983048 | tf_op jit(solution)/shard_map/ppermute | solution.py:373
  106.7 8.7 %collective-permute-start.26 = (f16[4,2,8,2560]{3,2,1,0:T(8,128)(2,1)S(1)}, f16[4,2,8,2560]{3,2,1,0:T(8,128)(2,1)S(1)}, u32[]{:S(2)}, u32[]{:S(2)}) collective-permute-start(f16[4,2,8,2560]{3,2,1,0:T(8,128)(2,1)S(1)} %add_convert_fusion.2), channel_id=1, source_target_pairs={{0,224},{4,228},{8,232},{12,236},{16,240},{20,244},{24,248},{28,25... | collective-permute-start | bytes 983048 | tf_op jit(solution)/shard_map/ppermute | solution.py:373
  111.9 8.8 %collective-permute-start.23 = (f16[4,2,8,2560]{3,2,1,0:T(8,128)(2,1)S(1)}, f16[4,2,8,2560]{3,2,1,0:T(8,128)(2,1)S(1)}, u32[]{:S(2)}, u32[]{:S(2)}) collective-permute-start(f16[4,2,8,2560]{3,2,1,0:T(8,128)(2,1)S(1)} %add_convert_fusion.4), channel_id=1, source_target_pairs={{0,32},{4,36},{8,40},{12,44},{16,48},{20,52},{24,56},{28,60},{32,6... | collective-permute-start | bytes 983048 | tf_op jit(solution)/shard_map/ppermute | solution.py:373
  115.5 14.2 %collective-permute-start.27 = (f16[4,2,8,2560]{3,2,1,0:T(8,128)(2,1)S(1)}, f16[4,2,8,2560]{3,2,1,0:T(8,128)(2,1)S(1)}, u32[]{:S(2)}, u32[]{:S(2)}) collective-permute-start(f16[4,2,8,2560]{3,2,1,0:T(8,128)(2,1)S(1)} %add_convert_fusion.1), channel_id=1, source_target_pairs={{0,224},{4,228},{8,232},{12,236},{16,240},{20,244},{24,248},{28,25... | collective-permute-start | bytes 983048 | tf_op jit(solution)/shard_map/ppermute | solution.py:373
  120.8 14.7 %collective-permute-start.24 = (f16[4,2,8,2560]{3,2,1,0:T(8,128)(2,1)S(1)}, f16[4,2,8,2560]{3,2,1,0:T(8,128)(2,1)S(1)}, u32[]{:S(2)}, u32[]{:S(2)}) collective-permute-start(f16[4,2,8,2560]{3,2,1,0:T(8,128)(2,1)S(1)} %add_convert_fusion.3), channel_id=1, source_target_pairs={{0,32},{4,36},{8,40},{12,44},{16,48},{20,52},{24,56},{28,60},{32,6... | collective-permute-start | bytes 983048 | tf_op jit(solution)/shard_map/ppermute | solution.py:373
  121.9 18.5 %all-to-all-start.1 = ((f16[8,2,8,1536]{3,2,1,0:T(8,128)(2,1)}), f16[8,2,8,1536]{3,2,1,0:T(8,128)(2,1)S(1)}, u32[]{:S(2)}, u32[]{:S(2)}) async-start(f16[8,2,8,1536]{3,2,1,0:T(8,128)(2,1)} %add_convert_fusion), calls=%async_computation.1 | async-start | bytes 786432 | tf_op jit(solution)/shard_map/all_to_all | solution.py:377
  (17 other events, 192.9 us)

commit v2 on v1

--- a/solution.py
+++ b/solution.py
@@ -25,6 +25,10 @@
 SPLIT = 2560
 REST = FEATURES - SPLIT
 BORDER = SPLIT - PIX
+UNIT = REST + EXTRA
+MESSAGE = X * SPLIT + UNIT
+EARLY = (0, 1, 2, 6, 7)
+LATE = (3, 4, 5)
 
 
 def shift_tables():
@@ -56,12 +60,9 @@
         top = jnp.maximum(top, jnp.abs(image_ref[i * 16 : i * 16 + 16, :]))
     largest = jnp.max(top.astype(jnp.float32), axis=0, keepdims=True)
     largest = jnp.max(largest, axis=1, keepdims=True)
-    spread = jnp.broadcast_to(largest, (8, EXTRA)).astype(jnp.bfloat16)
+    out_ref[:, :, 0:REST] = proj_ref[:, :, SPLIT:]
     for b in range(2):
-        row = proj_ref[b, :, SPLIT:]
-        for k in range(Z):
-            out_ref[k, b, :, 0:REST] = row
-            out_ref[k, b, :, REST:] = spread
+        out_ref[b, :, REST:] = jnp.broadcast_to(largest, (8, EXTRA)).astype(jnp.bfloat16)
 
 
 def prepare(images, projections):
@@ -69,10 +70,44 @@
         prepare_kernel,
         in_specs=[VMEM, VMEM],
         out_specs=VMEM,
-        out_shape=jax.ShapeDtypeStruct((Z, 2, 8, REST + EXTRA), jnp.bfloat16),
-        compiler_params=limit(4),
+        out_shape=pltpu.VMEM((2, 8, UNIT), jnp.bfloat16),
+        compiler_params=limit(2),
         name="prepare",
     )(in_vmem(images), in_vmem(projections))
+
+
+def assemble_kernel(*refs):
+    *parts, out_ref = refs
+    for k, part in enumerate(parts):
+        out_ref[:, :, k * SPLIT : k * SPLIT + part.shape[2]] = part[...]
+
+
+def assemble(row, unit):
+    return pl.pallas_call(
+        assemble_kernel,
+        in_specs=[VMEM] * (X + 1),
+        out_specs=VMEM,
+        out_shape=pltpu.VMEM((2, 8, MESSAGE), jnp.bfloat16),
+        compiler_params=limit(2),
+        name="assemble",
+    )(*[in_vmem(v) for v in (*row, unit)])
+
+
+def pick_kernel(*refs):
+    *messages, out_ref = refs
+    for k, message in enumerate(messages):
+        out_ref[k] = message[:, :, X * SPLIT :]
+
+
+def pick(messages):
+    return pl.pallas_call(
+        pick_kernel,
+        in_specs=[VMEM] * len(messages),
+        out_specs=VMEM,
+        out_shape=pltpu.VMEM((len(messages), 2, 8, UNIT), jnp.bfloat16),
+        compiler_params=limit(2),
+        name="pick",
+    )(*[in_vmem(v) for v in messages])
 
 
 def shift_kernel(table_ref, image_ref, out_re, out_im):
@@ -120,39 +155,79 @@
     return sig_ref[row, at], sig_ref[row, at + 1], zz
 
 
-def score_kernel(sig_ref, pos_ref, *refs):
-    by_z = refs[:Z]
-    by_x = refs[Z : Z + X]
-    sh = refs[Z + X : Z + X + 4]
-    st_ref, stat_ref = refs[Z + X + 4 : Z + X + 6]
-    sel, acc, mask = refs[Z + X + 6 :]
+DIMS = (((1,), (1,)), ((), ()))
+
+
+def score_first_kernel(sig_ref, pos_ref, *refs):
+    messages, sh, (acc_ref, sel) = refs[:Z], refs[Z : Z + 4], refs[Z + 4 :]
+    for q in range(2):
+        for o in range(RUNS):
+            dz, dx = o // X, o % X
+            _, second, _ = run_entry(sig_ref, pos_ref, q, dz, dx)
+            sel[o] = messages[dz][second, :, dx * SPLIT : (dx + 1) * SPLIT]
+        acc_ref[q] = lax.dot_general(
+            sh[2 * q][...].reshape(ROWS, PIX),
+            sel[:, :, 0:PIX].reshape(COLS, PIX),
+            DIMS,
+            preferred_element_type=jnp.float32,
+        )
+        acc_ref[q] += lax.dot_general(
+            sh[2 * q + 1][:, :, 0:BORDER].reshape(ROWS, BORDER),
+            sel[:, :, PIX:].reshape(COLS, BORDER),
+            DIMS,
+            preferred_element_type=jnp.float32,
+        )
+
+
+def score_first(sig, pos, messages, shifted):
+    return pl.pallas_call(
+        score_first_kernel,
+        in_specs=[SMEM, SMEM] + [VMEM] * (Z + 4),
+        out_specs=VMEM,
+        out_shape=pltpu.VMEM((2, ROWS, COLS), jnp.float32),
+        scratch_shapes=[pltpu.VMEM((RUNS, 8, SPLIT), jnp.bfloat16)],
+        compiler_params=limit(8),
+        cost_estimate=pl.CostEstimate(
+            flops=4 * ROWS * COLS * SPLIT, bytes_accessed=16 * 1024 * 1024, transcendentals=0
+        ),
+        name="score_first",
+    )(sig, pos, *[in_vmem(v) for v in messages], *[in_vmem(v) for v in shifted])
+
+
+def score_rest_kernel(sig_ref, pos_ref, *refs):
+    messages, batches = refs[:Z], refs[Z : Z + 6]
+    sh, acc = refs[Z + 6 : Z + 8], refs[Z + 8]
+    st_ref, stat_ref, sel, work, mask = refs[Z + 9 :]
+
+    def unit(dz, dx, second, at):
+        if dx == 0:
+            return messages[dz][second, :, X * SPLIT + at.start : X * SPLIT + at.stop]
+        early = dz in EARLY
+        place = (EARLY if early else LATE).index(dz)
+        return batches[dx - 1 if early else dx + 2][place, second, :, at]
+
     stat_ref[...] = jnp.zeros_like(stat_ref)
+    largest = jnp.zeros((8, EXTRA), jnp.float32)
+    for o in range(RUNS):
+        top = unit(o // X, o % X, 0, slice(REST, UNIT))
+        largest = jnp.maximum(largest, top.astype(jnp.float32))
+    stat_ref[4:5, 0:EXTRA] = jnp.max(largest, axis=0, keepdims=True)
     for q in range(2):
-        for dz in range(Z):
-            for dx in range(X):
-                o = dz * X + dx
-                first, second, zz = run_entry(sig_ref, pos_ref, q, dz, dx)
-                sel[q, o, :, 0:SPLIT] = by_z[dz][dx, second]
-                sel[q, o, :, SPLIT:] = by_x[dx][zz, second, :, 0:REST]
-                live = (first + second).astype(jnp.float32)
-                mask[q, o * 8 : o * 8 + 8, :] = jnp.full((8, 128), live, jnp.float32)
-    dims = (((1,), (1,)), ((), ()))
-    for q in range(2):
-        for half in range(2):
-            part = lax.dot_general(
-                sh[2 * q + half][...].reshape(ROWS, PIX),
-                sel[q, :, :, half * PIX : (half + 1) * PIX].reshape(COLS, PIX),
-                dims,
-                preferred_element_type=jnp.float32,
-            )
-            if half == 0:
-                acc[...] = part
-            else:
-                acc[...] += part
-        live = mask[q, :, 0:1] > 0.5
+        for o in range(RUNS):
+            first, second, _ = run_entry(sig_ref, pos_ref, q, o // X, o % X)
+            sel[o] = unit(o // X, o % X, second, slice(0, REST))
+            live = (first + second).astype(jnp.float32)
+            mask[o * 8 : o * 8 + 8, :] = jnp.full((8, 128), live, jnp.float32)
+        work[...] = acc[q] + lax.dot_general(
+            sh[q][:, :, BORDER:].reshape(ROWS, REST),
+            sel[...].reshape(COLS, REST),
+            DIMS,
+            preferred_element_type=jnp.float32,
+        )
+        live = mask[:, 0:1] > 0.5
         top = jnp.full((1, N), NEGATIVE, jnp.float32)
         for t in range(SHIFTS):
-            s = acc[t * N : (t + 1) * N, :].T * SCALE
+            s = work[t * N : (t + 1) * N, :].T * SCALE
             s = jnp.where(live, s, NEGATIVE)
             st_ref[q, :, t * N : (t + 1) * N] = s
             top = jnp.maximum(top, jnp.max(s, axis=0, keepdims=True))
@@ -163,33 +238,32 @@
             total = total + jnp.sum(e, axis=0, keepdims=True)
         stat_ref[q : q + 1, :] = top
         stat_ref[2 + q : 3 + q, :] = total
-    largest = jnp.zeros((8, EXTRA), jnp.float32)
-    for dx in range(X):
-        for zz in range(Z):
-            largest = jnp.maximum(largest, by_x[dx][zz, 0, :, REST:].astype(jnp.float32))
-    stat_ref[4:5, 0:EXTRA] = jnp.max(largest, axis=0, keepdims=True)
-
-
-def score_all(sig, pos, by_z, by_x, shifted):
-    return pl.pallas_call(
-        score_kernel,
-        in_specs=[SMEM, SMEM] + [VMEM] * (Z + X + 4),
+
+
+def score_rest(sig, pos, messages, batches, shifted, acc):
+    return pl.pallas_call(
+        score_rest_kernel,
+        in_specs=[SMEM, SMEM] + [VMEM] * (Z + 9),
         out_specs=[VMEM, VMEM],
         out_shape=[
             pltpu.VMEM((2, COLS, ROWS), jnp.float32),
             pltpu.VMEM((8, N), jnp.float32),
         ],
         scratch_shapes=[
-            pltpu.VMEM((2, RUNS, 8, FEATURES), jnp.bfloat16),
+            pltpu.VMEM((RUNS, 8, REST), jnp.bfloat16),
             pltpu.VMEM((ROWS, COLS), jnp.float32),
-            pltpu.VMEM((2, COLS, 128), jnp.float32),
+            pltpu.VMEM((COLS, 128), jnp.float32),
         ],
         compiler_params=limit(8),
         cost_estimate=pl.CostEstimate(
-            flops=4 * ROWS * COLS * FEATURES, bytes_accessed=28 * 1024 * 1024, transcendentals=2 * ROWS * COLS
+            flops=4 * ROWS * COLS * REST, bytes_accessed=16 * 1024 * 1024, transcendentals=2 * ROWS * COLS
         ),
-        name="scores",
-    )(sig, pos, *[in_vmem(v) for v in by_z], *[in_vmem(v) for v in by_x], *[in_vmem(v) for v in shifted])
+        name="score_rest",
+    )(
+        sig,
+        pos,
+        *[in_vmem(v) for v in (*messages, *batches, shifted[1], shifted[3], acc)],
+    )
 
 
 def merge_kernel(stat_ref, other_ref, out_ref):
@@ -218,25 +292,28 @@
 
 def partial_kernel(z_first, sig_ref, pos_ref, *refs):
     if z_first:
-        st_ref, *every = refs[:5]
-        images, (out_ref, w_ref, ev_ref) = refs[5:9], refs[9:]
+        st_ref, every = refs[:2]
+        images, (out_ref, w_ref, ev_ref) = refs[2:6], refs[6:]
         for q in range(2):
-            tops = [r[q : q + 1, :] for r in every]
+            tops = [every[k, q : q + 1, :] for k in range(REFS)]
             top = jnp.maximum(jnp.maximum(tops[0], tops[1]), jnp.maximum(tops[2], tops[3]))
-            total = sum(r[2 + q : 3 + q, :] * jnp.exp(t - top) for r, t in zip(every, tops))
+            total = sum(
+                every[k, 2 + q : 3 + q, :] * jnp.exp(tops[k] - top) for k in range(REFS)
+            )
             evidence = top + jnp.log(total)
             if q == 0:
                 ev_ref[...] = evidence
             for t in range(SHIFTS):
                 s = st_ref[q, :, t * N : (t + 1) * N]
                 w_ref[q, :, t * N : (t + 1) * N] = jnp.exp(s - evidence).astype(jnp.bfloat16)
-        bound_ref = every[0]
+        bound = every[0, 4:5, 0:1]
         tiles = ((0, 0, PIX // PTILE), (PIX, 1, BORDER // PTILE))
     else:
         w_ref, bound_ref = refs[:2]
+        bound = bound_ref[4:5, 0:1]
         images, (out_ref,) = refs[2:6], refs[6:]
         tiles = ((-BORDER, 1, PIX // PTILE),)
-    scale = HEADROOM / bound_ref[4:5, 0:1]
+    scale = HEADROOM / bound
     entries = [
         [run_entry(sig_ref, pos_ref, q, dz, dx) for dz in range(Z) for dx in range(X)]
         for q in range(2)
@@ -294,7 +371,7 @@
 
 def insert_kernel(bound_ref, w_ref, ins_ref, *refs):
     scale = bound_ref[4:5, 0:1] * (1.0 / HEADROOM)
-    rest = len(refs) == 3
+    rest = len(refs) == 1
 
     def add(acc, i, at, at_ids, width):
         row = pl.ds(i, 1)
@@ -316,16 +393,11 @@
 
     empty = jnp.zeros((2 * HIGH, LOW), jnp.float32)
     if rest:
-        re_ref, im_ref, out_ref = refs
         step = lambda i, acc: add(acc, i, slice(0, REST), slice(BORDER, PIX), REST)
-        acc = lax.fori_loop(0, 16, step, empty, unroll=2)
-        slab = im_ref[...] + acc[:HIGH] + acc[HIGH:]
-        for h in range(HIGH):
-            at = slice(h * LOW, (h + 1) * LOW)
-            out_ref[0:1, at] = re_ref[h : h + 1, :]
-            out_ref[1:2, at] = slab[h : h + 1, :]
+        acc = lax.fori_loop(0, 16, step, empty)
+        refs[0][...] = acc[:HIGH] + acc[HIGH:]
     else:
-        re_ref, im_ref = refs
+        slab_ref, out_ref = refs
 
         def step(i, both):
             re, im = both
@@ -334,23 +406,33 @@
             return re, im
 
         re, im = lax.fori_loop(0, 16, step, (empty, empty))
-        re_ref[...] = re[:HIGH] + re[HIGH:]
-        im_ref[...] = im[:HIGH] + im[HIGH:]
-
-
-def insert(bound, weighted, insertion, *slabs):
-    slab = jax.ShapeDtypeStruct((HIGH, LOW), jnp.float32)
+        re = re[:HIGH] + re[HIGH:]
+        im = slab_ref[...] + im[:HIGH] + im[HIGH:]
+        for h in range(HIGH):
+            at = slice(h * LOW, (h + 1) * LOW)
+            out_ref[0:1, at] = re[h : h + 1, :]
+            out_ref[1:2, at] = im[h : h + 1, :]
+
+
+def insert_call(shape, *args):
     return pl.pallas_call(
         insert_kernel,
-        in_specs=[VMEM] * (3 + len(slabs)),
-        out_specs=VMEM if slabs else [VMEM, VMEM],
-        out_shape=jax.ShapeDtypeStruct((2, VOX), jnp.float32) if slabs else [slab, slab],
+        in_specs=[VMEM] * len(args),
+        out_specs=VMEM,
+        out_shape=jax.ShapeDtypeStruct(shape, jnp.float32),
         compiler_params=limit(8),
         cost_estimate=pl.CostEstimate(
             flops=4 * HIGH * LOW * 16 * PIX, bytes_accessed=512 * 1024, transcendentals=0
         ),
-        name="insert_rest" if slabs else "insert_first",
-    )(bound, weighted.reshape(16, weighted.shape[-1]), insertion, *slabs)
+    )(*args)
+
+
+def insert_rest(bound, weighted, insertion):
+    return insert_call((HIGH, LOW), bound, weighted.reshape(16, REST), insertion)
+
+
+def insert_first(bound, weighted, insertion, slab):
+    return insert_call((2, VOX), bound, weighted.reshape(16, SPLIT), insertion, slab)
 
 
 def img_index(z, x, c):
@@ -379,22 +461,23 @@
     )
 
 
-def gather_x_first(unit):
-    row = jnp.stack([unit, send(unit, dx=-1), send(unit, dx=-2), send(unit, dx=1)])
-    out = {0: row}
-    ahead = behind = row
+def gather(projections, unit):
+    mine = projections[:, :, :SPLIT]
+    row = [mine, send(mine, dx=-1), send(mine, dx=-2), send(mine, dx=1)]
+    ahead = behind = assemble(row, unit)
+    messages = {0: ahead}
     for k in range(1, Z // 2 + 1):
         behind = send(behind, dz=1)
-        out[Z - k] = behind
+        messages[Z - k] = behind
         if k < Z // 2:
             ahead = send(ahead, dz=-1)
-            out[k] = ahead
-    return [out[k] for k in range(Z)]
-
-
-def gather_z_first(copies):
-    column = all_to_all_z(copies)
-    return [column, send(column, dx=-1), send(column, dx=-2), send(column, dx=1)]
+            messages[k] = ahead
+    batches = []
+    for places in (EARLY, LATE):
+        column = pick([messages[k] for k in places])
+        for dx in (-1, -2, 1):
+            batches.append(send(column, dx=dx))
+    return [messages[k] for k in range(Z)], batches
 
 
 def wide(value):
@@ -429,10 +512,7 @@
 
 
 def exchange_refs(value):
-    out = [value]
-    for k in range(1, REFS):
-        out.append(lax.ppermute(value, "ref", [(r, (r + k) % REFS) for r in range(REFS)]))
-    return out
+    return lax.all_gather(value, "ref")
 
 
 def one_device(particles, projections, significance, insertion):
@@ -444,24 +524,24 @@
     table = jnp.asarray(shift_tables())
 
     mate = send(particles, dc=1)
-    by_z = gather_x_first(projections[:, :, :SPLIT])
-    copies = prepare(particles, projections)
-    copies, pos, sig = lax.optimization_barrier((copies, pos, sig))
-    by_x = gather_z_first(copies)
+    unit = prepare(particles, projections)
+    unit, pos, sig = lax.optimization_barrier((unit, pos, sig))
+    messages, batches = gather(projections, unit)
     own_re, own_im = shifted_images(table, particles)
     mate_re, mate_im = shifted_images(table, mate)
 
     shifted = (own_re, own_im, mate_re, mate_im)
-    scores, stats = score_all(sig, pos, by_z, by_x, shifted)
+    acc = score_first(sig, pos, messages, shifted)
+    scores, stats = score_rest(sig, pos, messages, batches, shifted, acc)
     merged = merge(stats, send(stats, dc=1))
     every = exchange_refs(merged)
-    sums, weights, evidence = partial_sums(True, sig, pos, (scores, *every), shifted)
+    sums, weights, evidence = partial_sums(True, sig, pos, (scores, every), shifted)
     (sums_rest,) = partial_sums(False, sig, pos, (weights, merged), shifted)
     total = scatter_z_first(sums.reshape(Z, X, 2, 8, SPLIT))
     total_rest = scatter_x_first(sums_rest.reshape(X, Z, 2, 8, REST))
     ids = insertion.reshape(16, PIX)
-    slabs = insert(merged, total, ids)
-    volume = insert(merged, total_rest, ids, *slabs)
+    slab = insert_rest(merged, total_rest, ids)
+    volume = insert_first(merged, total, ids, slab)
     return volume, evidence.reshape(N)
 
 

time: 156 us -> 160 us (1.026)
  the two profiles are of different devices: /device:TPU:128 before, /device:TPU:8 now
where the time goes in v2:
time: 160 us; the launch traced here: 158 us
  starting transfers between devices  53.4 us (33%)
  waiting for transfers between devices  46.4 us (29%)
  Pallas kernels  36.7 us (23%)
  blocking collectives  12.1 us (8%)
  local copies, waits for them, and re-layouts  5.59 us (3%)
  other arithmetic  2.33 us (1%)
    ppermute x31, starting transfers between devices, send(): return lax.ppermute(value, 'img', pairs(dz, dx, dc))  47.5 us
    ppermute x31, waiting for transfers between devices, send(): return lax.ppermute(value, 'img', pairs(dz, dx, dc))  42.7 us
    all_gather x1, blocking collectives, exchange_refs(): return lax.all_gather(value, 'ref')  12.1 us
    pallas_call x2, Pallas kernels, insert_call(): pl.pallas_call(insert_kernel, in_specs=[VMEM] * len(args), out_specs=VMEM...  12.1 us
    pallas_call x2, Pallas kernels, partial_sums(): pl.pallas_call(lambda *refs: partial_kernel(z_first, *refs), in_specs=[SM...  9.87 us
    all_to_all x1, starting transfers between devices, all_to_all_z(): lax.all_to_all(value, 'img', split_axis=0, concat_axis=0, tiled=True, axi...  5.88 us
    pallas_call x2, Pallas kernels, shifted_images(): pl.pallas_call(shift_kernel, in_specs=[VMEM, VMEM], out_specs=[VMEM, VMEM...  5.5 us
    pallas_call x1, Pallas kernels, score_first(): pl.pallas_call(score_first_kernel, in_specs=[SMEM, SMEM] + [VMEM] * (Z +...  4.52 us
  transfers between devices with their start and end apart: 32, of which 14 were waited for; matrix products, arithmetic and copies ran while one was open for 2% of the time, Pallas kernels for 10%

profile of v2, /device:TPU:8, one launch (start us, length us, event | category | flops | bytes accessed | tf_op | source)
XLA Modules:
  0.0 157.5 jit_solution(7156337238474447949)
XLA Ops:
  3.1 2.7 %collective-permute-start.1 = (bf16[2,8,2560]{2,1,0:T(8,128)(2,1)S(1)}, bf16[2,8,2560]{2,1,0:T(8,128)(2,1)S(1)}, u32[]{:S(2)}, u32[]{:S(2)}) collective-permute-start(bf16[2,8,2560]{2,1,0:T(8,128)(2,1)S(1)} %slice.71.refs_0_), channel_id=1, source_target_pairs={{0,16},{4,20},{8,24},{12,28},{16,0},{20,4},{24,8},{28,12},{32,48},... | collective-permute-start | bytes 245768 | tf_op jit(solution)/shard_map/ppermute | solution.py:455
  12.5 4.0 %collective-permute-start.3 = (bf16[2,8,11904]{2,1,0:T(8,128)(2,1)S(1)}, bf16[2,8,11904]{2,1,0:T(8,128)(2,1)S(1)}, u32[]{:S(2)}, u32[]{:S(2)}) collective-permute-start(bf16[2,8,11904]{2,1,0:T(8,128)(2,1)S(1)} %assemble.1.refs_0_), channel_id=1, source_target_pairs={{0,224},{4,228},{8,232},{12,236},{16,240},{20,244},{24,248},{28,25... | collective-permute-start | bytes 1142792 | tf_op jit(solution)/shard_map/ppermute | solution.py:455
  16.5 8.6 %collective-permute-done.6.refs_4_.refs_7_ = bf16[2,8,11904]{2,1,0:T(8,128)(2,1)S(1)} collective-permute-done((bf16[2,8,11904]{2,1,0:T(8,128)(2,1)S(1)}, bf16[2,8,11904]{2,1,0:T(8,128)(2,1)S(1)}, u32[]{:S(2)}, u32[]{:S(2)}) %collective-permute-start.6) | collective-permute-done | bytes 380960 | tf_op jit(solution)/shard_map/ppermute | solution.py:455
  25.1 3.2 %collective-permute-start.4 = (bf16[2,8,11904]{2,1,0:T(8,128)(2,1)S(1)}, bf16[2,8,11904]{2,1,0:T(8,128)(2,1)S(1)}, u32[]{:S(2)}, u32[]{:S(2)}) collective-permute-start(bf16[2,8,11904]{2,1,0:T(8,128)(2,1)S(1)} %collective-permute-done.3.refs_1_), channel_id=1, source_target_pairs={{0,224},{4,228},{8,232},{12,236},{16,240},{20,244},{24,248},{28,25... | collective-permute-start | bytes 1142792 | tf_op jit(solution)/shard_map/ppermute | solution.py:455
  28.3 7.8 %collective-permute-done.7.refs_3_.refs_6_ = bf16[2,8,11904]{2,1,0:T(8,128)(2,1)S(1)} collective-permute-done((bf16[2,8,11904]{2,1,0:T(8,128)(2,1)S(1)}, bf16[2,8,11904]{2,1,0:T(8,128)(2,1)S(1)}, u32[]{:S(2)}, u32[]{:S(2)}) %collective-permute-start.7) | collective-permute-done | bytes 380960 | tf_op jit(solution)/shard_map/ppermute | solution.py:455
  36.1 3.2 %collective-permute-start.5 = (bf16[2,8,11904]{2,1,0:T(8,128)(2,1)S(1)}, bf16[2,8,11904]{2,1,0:T(8,128)(2,1)S(1)}, u32[]{:S(2)}, u32[]{:S(2)}) collective-permute-start(bf16[2,8,11904]{2,1,0:T(8,128)(2,1)S(1)} %collective-permute-done.4.refs_2_), channel_id=1, source_target_pairs={{0,224},{4,228},{8,232},{12,236},{16,240},{20,244},{24,248},{28,25... | collective-permute-start | bytes 1142792 | tf_op jit(solution)/shard_map/ppermute | solution.py:455
  39.3 6.9 %collective-permute-done.8.refs_2_.refs_5_ = bf16[2,8,11904]{2,1,0:T(8,128)(2,1)S(1)} collective-permute-done((bf16[2,8,11904]{2,1,0:T(8,128)(2,1)S(1)}, bf16[2,8,11904]{2,1,0:T(8,128)(2,1)S(1)}, u32[]{:S(2)}, u32[]{:S(2)}) %collective-permute-start.8) | collective-permute-done | bytes 380960 | tf_op jit(solution)/shard_map/ppermute | solution.py:455
  57.3 3.5 %shift.3 = (bf16[5,256,2048]{2,1,0:T(8,128)(2,1)S(1)}, bf16[5,256,2048]{2,1,0:T(8,128)(2,1)S(1)}) custom-call(f32[8,2048]{1,0:T(8,128)S(1)} %copy-done.5, bf16[256,4096]{1,0:T(8,128)(2,1)} %collective-permute-done.16.image_ref), custom_call_target="tpu_custom_call" | custom-call | flops 12582912 | bytes 12582912 | tf_op jit(solution)/shard_map/shift/pallas_call | solution.py:137
  60.9 2.8 %collective-permute-start.13 = (bf16[3,2,8,1664]{3,2,1,0:T(8,128)(2,1)S(1)}, bf16[3,2,8,1664]{3,2,1,0:T(8,128)(2,1)S(1)}, u32[]{:S(2)}, u32[]{:S(2)}) collective-permute-start(bf16[3,2,8,1664]{3,2,1,0:T(8,128)(2,1)S(1)} %pick.3), channel_id=1, source_target_pairs={{0,24},{4,28},{8,0},{12,4},{16,8},{20,12},{24,16},{28,20},{32,56},... | collective-permute-start | bytes 479240 | tf_op jit(solution)/shard_map/ppermute | solution.py:455
  63.6 4.5 %score_first.1.refs_16_ = f32[2,1280,256]{2,1,0:T(8,128)S(1)} custom-call(s32[2,512]{1,0:T(2,128)S(1)} %constant_dynamic-slice_fusion.sig_ref.refs_0_, s32[4]{0:T(128)S(1)} %pad_add_fusion.pos_ref.refs_1_, bf16[2,8,11904]{2,1,0:T(8,128)(2,1)S(1)} %assemble.1.refs_0_, bf16[2,8,11904]{2,1,0:T(8,128)(2,1)S(1)} %collective-permute-done.3.refs_1_, ...), custom_call_target="tpu_custom_call" | custom-call | flops 3355443200 | bytes 16777216 | tf_op jit(solution)/shard_map/score_first/pallas_call | solution.py:183
  68.4 4.3 %score_rest.1 = (f32[2,256,1280]{2,1,0:T(8,128)S(1)}, f32[8,256]{1,0:T(8,128)S(1)}) custom-call(s32[2,512]{1,0:T(2,128)S(1)} %constant_dynamic-slice_fusion.sig_ref.refs_0_, s32[4]{0:T(128)S(1)} %pad_add_fusion.pos_ref.refs_1_, bf16[2,8,11904]{2,1,0:T(8,128)(2,1)S(1)} %assemble.1.refs_0_, bf16[2,8,11904]{2,1,0:T(8,128)(2,1)S(1)} %collective-permute-done.3.refs_1_, ...), custom_call_target="tpu_custom_call" | custom-call | flops 2013265920 | bytes 16777216 | tf_op jit(solution)/shard_map/score_rest/pallas_call | solution.py:244
  74.0 12.1 %all-gather = f32[32,256]{1,0:T(8,128)S(1)} all-gather(f32[8,256]{1,0:T(8,128)S(1)} %merge.1.refs_3_.bound_ref), channel_id=2, replica_groups=mesh['img'=64,'ref'=4] {'ref'}, dimensions={0}, use_global_device_ids=true | all-gather | bytes 40960 | tf_op jit(solution)/shard_map/all_gather | solution.py:515
  86.2 6.1 %partial_first.1 = (f32[512,2560]{1,0:T(8,128)S(1)}, bf16[2,256,1280]{2,1,0:T(8,128)(2,1)S(1)}, f32[1,256]{1,0:T(1,128)}) custom-call(s32[2,512]{1,0:T(2,128)S(1)} %constant_dynamic-slice_fusion.sig_ref.refs_0_, s32[4]{0:T(128)S(1)} %pad_add_fusion.pos_ref.refs_1_, f32[2,256,1280]{2,1,0:T(8,128)S(1)} %get-tuple-element.22.refs_2_, ...), custom_call_target="tpu_custom_call" | custom-call | flops 2684354560 | bytes 16777216 | tf_op jit(solution)/shard_map/partial_first/pallas_call | solution.py:356
  92.3 3.7 %partial_rest.1 = f32[512,1536]{1,0:T(8,128)S(1)} custom-call(s32[2,512]{1,0:T(2,128)S(1)} %constant_dynamic-slice_fusion.sig_ref.refs_0_, s32[4]{0:T(128)S(1)} %pad_add_fusion.pos_ref.refs_1_, bf16[2,256,1280]{2,1,0:T(8,128)(2,1)S(1)} %get-tuple-element.24.refs_2_, f32[8,256]{1,0:T(8,128)S(1)} %merge.1.refs_3_.bound_ref, ...), custom_call_target="tpu_custom_call" | custom-call | flops 2684354560 | bytes 16777216 | tf_op jit(solution)/shard_map/partial_rest/pallas_call | solution.py:356
  103.4 3.2 %collective-permute-start.22 = (f16[4,2,8,2560]{3,2,1,0:T(8,128)(2,1)S(1)}, f16[4,2,8,2560]{3,2,1,0:T(8,128)(2,1)S(1)}, u32[]{:S(2)}, u32[]{:S(2)}) collective-permute-start(f16[4,2,8,2560]{3,2,1,0:T(8,128)(2,1)S(1)} %bitcast.52), channel_id=1, source_target_pairs={{0,224},{4,228},{8,232},{12,236},{16,240},{20,244},{24,248},{28,25... | collective-permute-start | bytes 983048 | tf_op jit(solution)/shard_map/ppermute | solution.py:455
  107.4 4.2 %collective-permute-done.22 = f16[4,2,8,2560]{3,2,1,0:T(8,128)(2,1)S(1)} collective-permute-done((f16[4,2,8,2560]{3,2,1,0:T(8,128)(2,1)S(1)}, f16[4,2,8,2560]{3,2,1,0:T(8,128)(2,1)S(1)}, u32[]{:S(2)}, u32[]{:S(2)}) %collective-permute-start.22) | collective-permute-done | bytes 327712 | tf_op jit(solution)/shard_map/ppermute | solution.py:455
  111.7 3.8 %collective-permute-start.23 = (f16[4,2,8,2560]{3,2,1,0:T(8,128)(2,1)S(1)}, f16[4,2,8,2560]{3,2,1,0:T(8,128)(2,1)S(1)}, u32[]{:S(2)}, u32[]{:S(2)}) collective-permute-start(f16[4,2,8,2560]{3,2,1,0:T(8,128)(2,1)S(1)} %add_convert_fusion.2), channel_id=1, source_target_pairs={{0,224},{4,228},{8,232},{12,236},{16,240},{20,244},{24,248},{28,25... | collective-permute-start | bytes 983048 | tf_op jit(solution)/shard_map/ppermute | solution.py:455
  116.5 5.2 %collective-permute-done.23 = f16[4,2,8,2560]{3,2,1,0:T(8,128)(2,1)S(1)} collective-permute-done((f16[4,2,8,2560]{3,2,1,0:T(8,128)(2,1)S(1)}, f16[4,2,8,2560]{3,2,1,0:T(8,128)(2,1)S(1)}, u32[]{:S(2)}, u32[]{:S(2)}) %collective-permute-start.23) | collective-permute-done | bytes 327712 | tf_op jit(solution)/shard_map/ppermute | solution.py:455
  121.8 3.4 %collective-permute-start.24 = (f16[4,2,8,2560]{3,2,1,0:T(8,128)(2,1)S(1)}, f16[4,2,8,2560]{3,2,1,0:T(8,128)(2,1)S(1)}, u32[]{:S(2)}, u32[]{:S(2)}) collective-permute-start(f16[4,2,8,2560]{3,2,1,0:T(8,128)(2,1)S(1)} %add_convert_fusion.1), channel_id=1, source_target_pairs={{0,224},{4,228},{8,232},{12,236},{16,240},{20,244},{24,248},{28,25... | collective-permute-start | bytes 983048 | tf_op jit(solution)/shard_map/ppermute | solution.py:455
  127.5 5.9 %all-to-all-start = ((f16[8,2,8,1536]{3,2,1,0:T(8,128)(2,1)}), f16[8,2,8,1536]{3,2,1,0:T(8,128)(2,1)S(1)}, u32[]{:S(2)}, u32[]{:S(2)}) async-start(f16[8,2,8,1536]{3,2,1,0:T(8,128)(2,1)} %add_convert_fusion), calls=%async_computation | async-start | bytes 786432 | tf_op jit(solution)/shard_map/all_to_all | solution.py:459
  133.4 3.1 %collective-permute-done.21 = f16[4,2,8,2560]{3,2,1,0:T(8,128)(2,1)S(1)} collective-permute-done((f16[4,2,8,2560]{3,2,1,0:T(8,128)(2,1)S(1)}, f16[4,2,8,2560]{3,2,1,0:T(8,128)(2,1)S(1)}, u32[]{:S(2)}, u32[]{:S(2)}) %collective-permute-start.21) | collective-permute-done | bytes 327712 | tf_op jit(solution)/shard_map/ppermute | solution.py:455
  141.6 3.7 %all-to-all-done = f16[8,2,8,1536]{3,2,1,0:T(8,128)(2,1)S(1)} async-done(((f16[8,2,8,1536]{3,2,1,0:T(8,128)(2,1)}), f16[8,2,8,1536]{3,2,1,0:T(8,128)(2,1)S(1)}, u32[]{:S(2)}, u32[]{:S(2)}) %all-to-all-start) | async-done | bytes 393248 | tf_op jit(solution)/shard_map/all_to_all | solution.py:459
  145.3 4.9 %shard_map.68.refs_0_ = f32[32,128]{1,0:T(8,128)S(1)} custom-call(f32[8,256]{1,0:T(8,128)S(1)} %merge.1.refs_3_.bound_ref, f32[16,1536]{1,0:T(8,128)S(1)} %bitcast.40, s32[16,2048]{1,0:T(8,128)S(1)} %bitcast.41), custom_call_target="tpu_custom_call" | custom-call | flops 536870912 | bytes 524288 | tf_op jit(solution)/shard_map/pallas_call | solution.py:418
  150.3 7.2 %shard_map.69 = f32[2,4096]{1,0:T(2,128)} custom-call(f32[8,256]{1,0:T(8,128)S(1)} %merge.1.refs_3_.bound_ref, f32[16,2560]{1,0:T(8,128)S(1)} %fusion.3.w_ref, s32[16,2048]{1,0:T(8,128)S(1)} %bitcast.42, f32[32,128]{1,0:T(8,128)S(1)} %shard_map.68.refs_0_), custom_call_target="tpu_custom_call" | custom-call | flops 536870912 | bytes 524288 | tf_op jit(solution)/shard_map/pallas_call | solution.py:418
  (88 shorter events, 38.3 us)
Async XLA Ops:
  0.6 55.0 %collective-permute-start.16 = (bf16[256,4096]{1,0:T(8,128)(2,1)}, bf16[256,4096]{1,0:T(8,128)(2,1)}, u32[]{:S(2)}, u32[]{:S(2)}) collective-permute-start(bf16[256,4096]{1,0:T(8,128)(2,1)} %image_ref.3), channel_id=1, source_target_pairs={{0,4},{4,0},{8,12},{12,8},{16,20},{20,16},{24,28},{28,24},{32,36},... | collective-permute-start | bytes 6291464 | tf_op jit(solution)/shard_map/ppermute | solution.py:455
  10.5 14.6 %collective-permute-start.6 = (bf16[2,8,11904]{2,1,0:T(8,128)(2,1)S(1)}, bf16[2,8,11904]{2,1,0:T(8,128)(2,1)S(1)}, u32[]{:S(2)}, u32[]{:S(2)}) collective-permute-start(bf16[2,8,11904]{2,1,0:T(8,128)(2,1)S(1)} %assemble.1.refs_0_), channel_id=1, source_target_pairs={{0,32},{4,36},{8,40},{12,44},{16,48},{20,52},{24,56},{28,60},{32,6... | collective-permute-start | bytes 1142792 | tf_op jit(solution)/shard_map/ppermute | solution.py:455
  12.5 12.6 %collective-permute-start.3 = (bf16[2,8,11904]{2,1,0:T(8,128)(2,1)S(1)}, bf16[2,8,11904]{2,1,0:T(8,128)(2,1)S(1)}, u32[]{:S(2)}, u32[]{:S(2)}) collective-permute-start(bf16[2,8,11904]{2,1,0:T(8,128)(2,1)S(1)} %assemble.1.refs_0_), channel_id=1, source_target_pairs={{0,224},{4,228},{8,232},{12,236},{16,240},{20,244},{24,248},{28,25... | collective-permute-start | bytes 1142792 | tf_op jit(solution)/shard_map/ppermute | solution.py:455
  25.1 11.0 %collective-permute-start.7 = (bf16[2,8,11904]{2,1,0:T(8,128)(2,1)S(1)}, bf16[2,8,11904]{2,1,0:T(8,128)(2,1)S(1)}, u32[]{:S(2)}, u32[]{:S(2)}) collective-permute-start(bf16[2,8,11904]{2,1,0:T(8,128)(2,1)S(1)} %collective-permute-done.6.refs_4_.refs_7_), channel_id=1, source_target_pairs={{0,32},{4,36},{8,40},{12,44},{16,48},{20,52},{24,56},{28,60},{32,6... | collective-permute-start | bytes 1142792 | tf_op jit(solution)/shard_map/ppermute | solution.py:455
  25.1 11.0 %collective-permute-start.4 = (bf16[2,8,11904]{2,1,0:T(8,128)(2,1)S(1)}, bf16[2,8,11904]{2,1,0:T(8,128)(2,1)S(1)}, u32[]{:S(2)}, u32[]{:S(2)}) collective-permute-start(bf16[2,8,11904]{2,1,0:T(8,128)(2,1)S(1)} %collective-permute-done.3.refs_1_), channel_id=1, source_target_pairs={{0,224},{4,228},{8,232},{12,236},{16,240},{20,244},{24,248},{28,25... | collective-permute-start | bytes 1142792 | tf_op jit(solution)/shard_map/ppermute | solution.py:455
  36.1 10.2 %collective-permute-start.8 = (bf16[2,8,11904]{2,1,0:T(8,128)(2,1)S(1)}, bf16[2,8,11904]{2,1,0:T(8,128)(2,1)S(1)}, u32[]{:S(2)}, u32[]{:S(2)}) collective-permute-start(bf16[2,8,11904]{2,1,0:T(8,128)(2,1)S(1)} %collective-permute-done.7.refs_3_.refs_6_), channel_id=1, source_target_pairs={{0,32},{4,36},{8,40},{12,44},{16,48},{20,52},{24,56},{28,60},{32,6... | collective-permute-start | bytes 1142792 | tf_op jit(solution)/shard_map/ppermute | solution.py:455
  36.1 14.2 %collective-permute-start.5 = (bf16[2,8,11904]{2,1,0:T(8,128)(2,1)S(1)}, bf16[2,8,11904]{2,1,0:T(8,128)(2,1)S(1)}, u32[]{:S(2)}, u32[]{:S(2)}) collective-permute-start(bf16[2,8,11904]{2,1,0:T(8,128)(2,1)S(1)} %collective-permute-done.4.refs_2_), channel_id=1, source_target_pairs={{0,224},{4,228},{8,232},{12,236},{16,240},{20,244},{24,248},{28,25... | collective-permute-start | bytes 1142792 | tf_op jit(solution)/shard_map/ppermute | solution.py:455
  46.2 9.3 %collective-permute-start.9 = (bf16[2,8,11904]{2,1,0:T(8,128)(2,1)S(1)}, bf16[2,8,11904]{2,1,0:T(8,128)(2,1)S(1)}, u32[]{:S(2)}, u32[]{:S(2)}) collective-permute-start(bf16[2,8,11904]{2,1,0:T(8,128)(2,1)S(1)} %collective-permute-done.8.refs_2_.refs_5_), channel_id=1, source_target_pairs={{0,32},{4,36},{8,40},{12,44},{16,48},{20,52},{24,56},{28,60},{32,6... | collective-permute-start | bytes 1142792 | tf_op jit(solution)/shard_map/ppermute | solution.py:455
  46.3 14.6 %collective-permute-start.12 = (bf16[5,2,8,1664]{3,2,1,0:T(8,128)(2,1)S(1)}, bf16[5,2,8,1664]{3,2,1,0:T(8,128)(2,1)S(1)}, u32[]{:S(2)}, u32[]{:S(2)}) collective-permute-start(bf16[5,2,8,1664]{3,2,1,0:T(8,128)(2,1)S(1)} %pick.2), channel_id=1, source_target_pairs={{0,8},{4,12},{8,16},{12,20},{16,24},{20,28},{24,0},{28,4},{32,40},... | collective-permute-start | bytes 798728 | tf_op jit(solution)/shard_map/ppermute | solution.py:455
  48.4 19.8 %collective-permute-start.11 = (bf16[5,2,8,1664]{3,2,1,0:T(8,128)(2,1)S(1)}, bf16[5,2,8,1664]{3,2,1,0:T(8,128)(2,1)S(1)}, u32[]{:S(2)}, u32[]{:S(2)}) collective-permute-start(bf16[5,2,8,1664]{3,2,1,0:T(8,128)(2,1)S(1)} %pick.2), channel_id=1, source_target_pairs={{0,16},{4,20},{8,24},{12,28},{16,0},{20,4},{24,8},{28,12},{32,48},... | collective-permute-start | bytes 798728 | tf_op jit(solution)/shard_map/ppermute | solution.py:455
  50.3 17.9 %collective-permute-start.10 = (bf16[5,2,8,1664]{3,2,1,0:T(8,128)(2,1)S(1)}, bf16[5,2,8,1664]{3,2,1,0:T(8,128)(2,1)S(1)}, u32[]{:S(2)}, u32[]{:S(2)}) collective-permute-start(bf16[5,2,8,1664]{3,2,1,0:T(8,128)(2,1)S(1)} %pick.2), channel_id=1, source_target_pairs={{0,24},{4,28},{8,0},{12,4},{16,8},{20,12},{24,16},{28,20},{32,56},... | collective-permute-start | bytes 798728 | tf_op jit(solution)/shard_map/ppermute | solution.py:455
  55.6 12.6 %collective-permute-start.15 = (bf16[3,2,8,1664]{3,2,1,0:T(8,128)(2,1)S(1)}, bf16[3,2,8,1664]{3,2,1,0:T(8,128)(2,1)S(1)}, u32[]{:S(2)}, u32[]{:S(2)}) collective-permute-start(bf16[3,2,8,1664]{3,2,1,0:T(8,128)(2,1)S(1)} %pick.3), channel_id=1, source_target_pairs={{0,8},{4,12},{8,16},{12,20},{16,24},{20,28},{24,0},{28,4},{32,40},... | collective-permute-start | bytes 479240 | tf_op jit(solution)/shard_map/ppermute | solution.py:455
  55.7 12.5 %collective-permute-start.14 = (bf16[3,2,8,1664]{3,2,1,0:T(8,128)(2,1)S(1)}, bf16[3,2,8,1664]{3,2,1,0:T(8,128)(2,1)S(1)}, u32[]{:S(2)}, u32[]{:S(2)}) collective-permute-start(bf16[3,2,8,1664]{3,2,1,0:T(8,128)(2,1)S(1)} %pick.3), channel_id=1, source_target_pairs={{0,16},{4,20},{8,24},{12,28},{16,0},{20,4},{24,8},{28,12},{32,48},... | collective-permute-start | bytes 479240 | tf_op jit(solution)/shard_map/ppermute | solution.py:455
  99.1 27.4 %collective-permute-start.30 = (f16[8,2,8,1536]{3,2,1,0:T(8,128)(2,1)S(1)}, f16[8,2,8,1536]{3,2,1,0:T(8,128)(2,1)S(1)}, u32[]{:S(2)}, u32[]{:S(2)}) collective-permute-start(f16[8,2,8,1536]{3,2,1,0:T(8,128)(2,1)S(1)} %bitcast.51), channel_id=1, source_target_pairs={{0,24},{4,28},{8,0},{12,4},{16,8},{20,12},{24,16},{28,20},{32,56},... | collective-permute-start | bytes 1179656 | tf_op jit(solution)/shard_map/ppermute | solution.py:455
  101.8 24.7 %collective-permute-start.28 = (f16[8,2,8,1536]{3,2,1,0:T(8,128)(2,1)S(1)}, f16[8,2,8,1536]{3,2,1,0:T(8,128)(2,1)S(1)}, u32[]{:S(2)}, u32[]{:S(2)}) collective-permute-start(f16[8,2,8,1536]{3,2,1,0:T(8,128)(2,1)S(1)} %bitcast.50), channel_id=1, source_target_pairs={{0,8},{4,12},{8,16},{12,20},{16,24},{20,28},{24,0},{28,4},{32,40},... | collective-permute-start | bytes 1179656 | tf_op jit(solution)/shard_map/ppermute | solution.py:455
  101.8 24.7 %collective-permute-start.29 = (f16[8,2,8,1536]{3,2,1,0:T(8,128)(2,1)S(1)}, f16[8,2,8,1536]{3,2,1,0:T(8,128)(2,1)S(1)}, u32[]{:S(2)}, u32[]{:S(2)}) collective-permute-start(f16[8,2,8,1536]{3,2,1,0:T(8,128)(2,1)S(1)} %bitcast.49), channel_id=1, source_target_pairs={{0,16},{4,20},{8,24},{12,28},{16,0},{20,4},{24,8},{28,12},{32,48},... | collective-permute-start | bytes 1179656 | tf_op jit(solution)/shard_map/ppermute | solution.py:455
  111.7 10.0 %collective-permute-start.23 = (f16[4,2,8,2560]{3,2,1,0:T(8,128)(2,1)S(1)}, f16[4,2,8,2560]{3,2,1,0:T(8,128)(2,1)S(1)}, u32[]{:S(2)}, u32[]{:S(2)}) collective-permute-start(f16[4,2,8,2560]{3,2,1,0:T(8,128)(2,1)S(1)} %add_convert_fusion.2), channel_id=1, source_target_pairs={{0,224},{4,228},{8,232},{12,236},{16,240},{20,244},{24,248},{28,25... | collective-permute-start | bytes 983048 | tf_op jit(solution)/shard_map/ppermute | solution.py:455
  116.4 9.9 %collective-permute-start.20 = (f16[4,2,8,2560]{3,2,1,0:T(8,128)(2,1)S(1)}, f16[4,2,8,2560]{3,2,1,0:T(8,128)(2,1)S(1)}, u32[]{:S(2)}, u32[]{:S(2)}) collective-permute-start(f16[4,2,8,2560]{3,2,1,0:T(8,128)(2,1)S(1)} %add_convert_fusion.4), channel_id=1, source_target_pairs={{0,32},{4,36},{8,40},{12,44},{16,48},{20,52},{24,56},{28,60},{32,6... | collective-permute-start | bytes 983048 | tf_op jit(solution)/shard_map/ppermute | solution.py:455
  121.8 11.5 %collective-permute-start.24 = (f16[4,2,8,2560]{3,2,1,0:T(8,128)(2,1)S(1)}, f16[4,2,8,2560]{3,2,1,0:T(8,128)(2,1)S(1)}, u32[]{:S(2)}, u32[]{:S(2)}) collective-permute-start(f16[4,2,8,2560]{3,2,1,0:T(8,128)(2,1)S(1)} %add_convert_fusion.1), channel_id=1, source_target_pairs={{0,224},{4,228},{8,232},{12,236},{16,240},{20,244},{24,248},{28,25... | collective-permute-start | bytes 983048 | tf_op jit(solution)/shard_map/ppermute | solution.py:455
  126.4 10.1 %collective-permute-start.21 = (f16[4,2,8,2560]{3,2,1,0:T(8,128)(2,1)S(1)}, f16[4,2,8,2560]{3,2,1,0:T(8,128)(2,1)S(1)}, u32[]{:S(2)}, u32[]{:S(2)}) collective-permute-start(f16[4,2,8,2560]{3,2,1,0:T(8,128)(2,1)S(1)} %add_convert_fusion.3), channel_id=1, source_target_pairs={{0,32},{4,36},{8,40},{12,44},{16,48},{20,52},{24,56},{28,60},{32,6... | collective-permute-start | bytes 983048 | tf_op jit(solution)/shard_map/ppermute | solution.py:455
  127.5 17.8 %all-to-all-start = ((f16[8,2,8,1536]{3,2,1,0:T(8,128)(2,1)}), f16[8,2,8,1536]{3,2,1,0:T(8,128)(2,1)S(1)}, u32[]{:S(2)}, u32[]{:S(2)}) async-start(f16[8,2,8,1536]{3,2,1,0:T(8,128)(2,1)} %add_convert_fusion), calls=%async_computation | async-start | bytes 786432 | tf_op jit(solution)/shard_map/all_to_all | solution.py:459
  136.7 13.6 %collective-permute-start.25 = (f16[2,8,2560]{2,1,0:T(8,128)(2,1)S(1)}, f16[2,8,2560]{2,1,0:T(8,128)(2,1)S(1)}, u32[]{:S(2)}, u32[]{:S(2)}) collective-permute-start(f16[2,8,2560]{2,1,0:T(8,128)(2,1)S(1)} %get-tuple-element.39), channel_id=1, source_target_pairs={{0,8},{4,12},{8,16},{12,20},{16,24},{20,28},{24,0},{28,4},{32,40},... | collective-permute-start | bytes 245768 | tf_op jit(solution)/shard_map/ppermute | solution.py:455
  139.4 10.9 %collective-permute-start.27 = (f16[2,8,2560]{2,1,0:T(8,128)(2,1)S(1)}, f16[2,8,2560]{2,1,0:T(8,128)(2,1)S(1)}, u32[]{:S(2)}, u32[]{:S(2)}) collective-permute-start(f16[2,8,2560]{2,1,0:T(8,128)(2,1)S(1)} %get-tuple-element.40), channel_id=1, source_target_pairs={{0,24},{4,28},{8,0},{12,4},{16,8},{20,12},{24,16},{28,20},{32,56},... | collective-permute-start | bytes 245768 | tf_op jit(solution)/shard_map/ppermute | solution.py:455
  140.0 10.3 %collective-permute-start.26 = (f16[2,8,2560]{2,1,0:T(8,128)(2,1)S(1)}, f16[2,8,2560]{2,1,0:T(8,128)(2,1)S(1)}, u32[]{:S(2)}, u32[]{:S(2)}) collective-permute-start(f16[2,8,2560]{2,1,0:T(8,128)(2,1)S(1)} %get-tuple-element.41), channel_id=1, source_target_pairs={{0,16},{4,20},{8,24},{12,28},{16,0},{20,4},{24,8},{28,12},{32,48},... | collective-permute-start | bytes 245768 | tf_op jit(solution)/shard_map/ppermute | solution.py:455
  (16 other events, 174.6 us)

commit v3 on v2

--- a/solution.py
+++ b/solution.py
@@ -110,48 +110,49 @@
     )(*[in_vmem(v) for v in messages])
 
 
-def shift_kernel(table_ref, image_ref, out_re, out_im):
-    for j in range(PIX // LANES):
-        at = slice(j * LANES, (j + 1) * LANES)
-        at_im = slice(PIX + j * LANES, PIX + (j + 1) * LANES)
-        tables = [table_ref[k : k + 1, at] for k in range(4)]
-
-        @pl.loop(0, N // 16)
-        def _(i):
-            rows = pl.ds(pl.multiple_of(i * 16, 16), 16)
-            re_in, im_in = image_ref[rows, at], image_ref[rows, at_im]
-            out_re[0, rows, at] = re_in
-            out_im[0, rows, at] = im_in
-            re, im = re_in.astype(jnp.float32), im_in.astype(jnp.float32)
-            for k in range(2):
-                c, s = tables[2 * k], tables[2 * k + 1]
-                rc, rs, ic, is_ = re * c, re * s, im * c, im * s
-                out_re[1 + 2 * k, rows, at] = (rc - is_).astype(jnp.bfloat16)
-                out_im[1 + 2 * k, rows, at] = (rs + ic).astype(jnp.bfloat16)
-                out_re[2 + 2 * k, rows, at] = (rc + is_).astype(jnp.bfloat16)
-                out_im[2 + 2 * k, rows, at] = (ic - rs).astype(jnp.bfloat16)
-
-
-def shifted_images(table, images):
-    shape = pltpu.VMEM((SHIFTS, N, PIX), jnp.bfloat16)
+def shift_kernel(table_ref, own_ref, mate_ref, out_re, out_im):
+    for q, image_ref in enumerate((own_ref, mate_ref)):
+        for j in range(PIX // LANES):
+            at = slice(j * LANES, (j + 1) * LANES)
+            at_im = slice(PIX + j * LANES, PIX + (j + 1) * LANES)
+            tables = [table_ref[k : k + 1, at] for k in range(4)]
+
+            @pl.loop(0, N // 16)
+            def _(i):
+                rows = pl.ds(pl.multiple_of(i * 16, 16), 16)
+                re_in, im_in = image_ref[rows, at], image_ref[rows, at_im]
+                out_re[q, 0, rows, at] = re_in
+                out_im[q, 0, rows, at] = im_in
+                re, im = re_in.astype(jnp.float32), im_in.astype(jnp.float32)
+                for k in range(2):
+                    c, s = tables[2 * k], tables[2 * k + 1]
+                    rc, rs, ic, is_ = re * c, re * s, im * c, im * s
+                    out_re[q, 1 + 2 * k, rows, at] = (rc - is_).astype(jnp.bfloat16)
+                    out_im[q, 1 + 2 * k, rows, at] = (rs + ic).astype(jnp.bfloat16)
+                    out_re[q, 2 + 2 * k, rows, at] = (rc + is_).astype(jnp.bfloat16)
+                    out_im[q, 2 + 2 * k, rows, at] = (ic - rs).astype(jnp.bfloat16)
+
+
+def shifted_images(table, own, mate):
+    shape = pltpu.VMEM((2, SHIFTS, N, PIX), jnp.bfloat16)
     return pl.pallas_call(
         shift_kernel,
-        in_specs=[VMEM, VMEM],
+        in_specs=[VMEM] * 3,
         out_specs=[VMEM, VMEM],
         out_shape=[shape, shape],
         compiler_params=limit(4),
         cost_estimate=pl.CostEstimate(
-            flops=24 * N * PIX, bytes_accessed=12 * 1024 * 1024, transcendentals=0
+            flops=48 * N * PIX, bytes_accessed=24 * 1024 * 1024, transcendentals=0
         ),
         name="shift",
-    )(in_vmem(table), in_vmem(images))
+    )(in_vmem(table), in_vmem(own), in_vmem(mate))
 
 
 def run_entry(sig_ref, pos_ref, q, dz, dx):
     zz = lax.rem(pos_ref[0] + dz, Z)
     xx = lax.rem(pos_ref[1] + dx, X)
     at = (((zz * X + xx) * CORES + pos_ref[2]) * REFS + pos_ref[3]) * 2
-    row = pos_ref[2] if q == 0 else 1 - pos_ref[2]
+    row = lax.rem(pos_ref[2] + q, 2)
     return sig_ref[row, at], sig_ref[row, at + 1], zz
 
 
@@ -159,20 +160,22 @@
 
 
 def score_first_kernel(sig_ref, pos_ref, *refs):
-    messages, sh, (acc_ref, sel) = refs[:Z], refs[Z : Z + 4], refs[Z + 4 :]
-    for q in range(2):
+    messages, (re_ref, im_ref, acc_ref, sel) = refs[:Z], refs[Z:]
+
+    @pl.loop(0, 2)
+    def _(q):
         for o in range(RUNS):
             dz, dx = o // X, o % X
             _, second, _ = run_entry(sig_ref, pos_ref, q, dz, dx)
             sel[o] = messages[dz][second, :, dx * SPLIT : (dx + 1) * SPLIT]
         acc_ref[q] = lax.dot_general(
-            sh[2 * q][...].reshape(ROWS, PIX),
+            re_ref[q].reshape(ROWS, PIX),
             sel[:, :, 0:PIX].reshape(COLS, PIX),
             DIMS,
             preferred_element_type=jnp.float32,
         )
         acc_ref[q] += lax.dot_general(
-            sh[2 * q + 1][:, :, 0:BORDER].reshape(ROWS, BORDER),
+            im_ref[q, :, :, 0:BORDER].reshape(ROWS, BORDER),
             sel[:, :, PIX:].reshape(COLS, BORDER),
             DIMS,
             preferred_element_type=jnp.float32,
@@ -182,7 +185,7 @@
 def score_first(sig, pos, messages, shifted):
     return pl.pallas_call(
         score_first_kernel,
-        in_specs=[SMEM, SMEM] + [VMEM] * (Z + 4),
+        in_specs=[SMEM, SMEM] + [VMEM] * (Z + 2),
         out_specs=VMEM,
         out_shape=pltpu.VMEM((2, ROWS, COLS), jnp.float32),
         scratch_shapes=[pltpu.VMEM((RUNS, 8, SPLIT), jnp.bfloat16)],
@@ -196,8 +199,8 @@
 
 def score_rest_kernel(sig_ref, pos_ref, *refs):
     messages, batches = refs[:Z], refs[Z : Z + 6]
-    sh, acc = refs[Z + 6 : Z + 8], refs[Z + 8]
-    st_ref, stat_ref, sel, work, mask = refs[Z + 9 :]
+    im_ref, acc = refs[Z + 6 : Z + 8]
+    st_ref, stat_ref, sel, work, mask = refs[Z + 8 :]
 
     def unit(dz, dx, second, at):
         if dx == 0:
@@ -212,14 +215,16 @@
         top = unit(o // X, o % X, 0, slice(REST, UNIT))
         largest = jnp.maximum(largest, top.astype(jnp.float32))
     stat_ref[4:5, 0:EXTRA] = jnp.max(largest, axis=0, keepdims=True)
-    for q in range(2):
+
+    @pl.loop(0, 2)
+    def _(q):
         for o in range(RUNS):
             first, second, _ = run_entry(sig_ref, pos_ref, q, o // X, o % X)
             sel[o] = unit(o // X, o % X, second, slice(0, REST))
             live = (first + second).astype(jnp.float32)
             mask[o * 8 : o * 8 + 8, :] = jnp.full((8, 128), live, jnp.float32)
         work[...] = acc[q] + lax.dot_general(
-            sh[q][:, :, BORDER:].reshape(ROWS, REST),
+            im_ref[q, :, :, BORDER:].reshape(ROWS, REST),
             sel[...].reshape(COLS, REST),
             DIMS,
             preferred_element_type=jnp.float32,
@@ -236,14 +241,14 @@
             s = st_ref[q, :, t * N : (t + 1) * N]
             e = jnp.where(live, jnp.exp(s - top), 0.0)
             total = total + jnp.sum(e, axis=0, keepdims=True)
-        stat_ref[q : q + 1, :] = top
-        stat_ref[2 + q : 3 + q, :] = total
+        stat_ref[pl.ds(q, 1), :] = top
+        stat_ref[pl.ds(2 + q, 1), :] = total
 
 
 def score_rest(sig, pos, messages, batches, shifted, acc):
     return pl.pallas_call(
         score_rest_kernel,
-        in_specs=[SMEM, SMEM] + [VMEM] * (Z + 9),
+        in_specs=[SMEM, SMEM] + [VMEM] * (Z + 8),
         out_specs=[VMEM, VMEM],
         out_shape=[
             pltpu.VMEM((2, COLS, ROWS), jnp.float32),
@@ -262,7 +267,7 @@
     )(
         sig,
         pos,
-        *[in_vmem(v) for v in (*messages, *batches, shifted[1], shifted[3], acc)],
+        *[in_vmem(v) for v in (*messages, *batches, shifted[1], acc)],
     )
 
 
@@ -292,41 +297,36 @@
 
 def partial_kernel(z_first, sig_ref, pos_ref, *refs):
     if z_first:
-        st_ref, every = refs[:2]
-        images, (out_ref, w_ref, ev_ref) = refs[2:6], refs[6:]
+        w_ref, bound_ref, image_ref, out_ref = refs
+        bound = bound_ref[4:5, 0:1]
+    else:
+        st_ref, *every = refs[:5]
+        image_ref, out_ref, w_ref, ev_ref = refs[5:]
         for q in range(2):
-            tops = [every[k, q : q + 1, :] for k in range(REFS)]
+            tops = [r[q : q + 1, :] for r in every]
             top = jnp.maximum(jnp.maximum(tops[0], tops[1]), jnp.maximum(tops[2], tops[3]))
-            total = sum(
-                every[k, 2 + q : 3 + q, :] * jnp.exp(tops[k] - top) for k in range(REFS)
-            )
+            total = sum(r[2 + q : 3 + q, :] * jnp.exp(t - top) for r, t in zip(every, tops))
             evidence = top + jnp.log(total)
             if q == 0:
                 ev_ref[...] = evidence
             for t in range(SHIFTS):
                 s = st_ref[q, :, t * N : (t + 1) * N]
                 w_ref[q, :, t * N : (t + 1) * N] = jnp.exp(s - evidence).astype(jnp.bfloat16)
-        bound = every[0, 4:5, 0:1]
-        tiles = ((0, 0, PIX // PTILE), (PIX, 1, BORDER // PTILE))
-    else:
-        w_ref, bound_ref = refs[:2]
-        bound = bound_ref[4:5, 0:1]
-        images, (out_ref,) = refs[2:6], refs[6:]
-        tiles = ((-BORDER, 1, PIX // PTILE),)
+        bound = every[0][4:5, 0:1]
     scale = HEADROOM / bound
     entries = [
         [run_entry(sig_ref, pos_ref, q, dz, dx) for dz in range(Z) for dx in range(X)]
         for q in range(2)
     ]
 
-    def one_tile(offset, half, i):
-        at_in = pl.ds(pl.multiple_of(i * PTILE, PTILE), PTILE)
-        at = pl.ds(pl.multiple_of(offset + i * PTILE, PTILE), PTILE)
+    @pl.loop(0, PIX // PTILE)
+    def _(i):
+        at = pl.ds(pl.multiple_of(i * PTILE, PTILE), PTILE)
         for q in range(2):
             value = (
                 jnp.dot(
                     w_ref[q],
-                    images[2 * q + half][:, :, at_in].reshape(ROWS, PTILE),
+                    image_ref[q, :, :, at].reshape(ROWS, PTILE),
                     preferred_element_type=jnp.float32,
                 )
                 * scale
@@ -343,27 +343,23 @@
                 else:
                     out_ref[rows, at] += block
 
-    for offset, half, count in tiles:
-        start = max(0, -offset) // PTILE
-        pl.loop(start, count)(lambda i, offset=offset, half=half: one_tile(offset, half, i))
-
-
-def partial_sums(z_first, sig, pos, weights, shifted):
-    out_shape = [pltpu.VMEM((2 * COLS, SPLIT if z_first else REST), jnp.float32)]
-    if z_first:
+
+def partial_sums(z_first, sig, pos, weights, images):
+    out_shape = [pltpu.VMEM((2 * COLS, PIX), jnp.float32)]
+    if not z_first:
         out_shape.append(pltpu.VMEM((2, COLS, ROWS), jnp.bfloat16))
         out_shape.append(jax.ShapeDtypeStruct((1, N), jnp.float32))
     return pl.pallas_call(
         lambda *refs: partial_kernel(z_first, *refs),
-        in_specs=[SMEM, SMEM] + [VMEM] * (len(weights) + 4),
+        in_specs=[SMEM, SMEM] + [VMEM] * (len(weights) + 1),
         out_specs=[VMEM] * len(out_shape),
         out_shape=out_shape,
         compiler_params=limit(4),
         cost_estimate=pl.CostEstimate(
             flops=2 * ROWS * COLS * FEATURES, bytes_accessed=16 * 1024 * 1024, transcendentals=0
         ),
-        name="partial_first" if z_first else "partial_rest",
-    )(sig, pos, *[in_vmem(v) for v in weights], *[in_vmem(v) for v in shifted])
+        name="partial_re" if z_first else "partial_im",
+    )(sig, pos, *[in_vmem(v) for v in weights], in_vmem(images))
 
 
 HIGH, LOW = 32, 128
@@ -371,68 +367,50 @@
 
 def insert_kernel(bound_ref, w_ref, ins_ref, *refs):
     scale = bound_ref[4:5, 0:1] * (1.0 / HEADROOM)
-    rest = len(refs) == 1
-
-    def add(acc, i, at, at_ids, width):
+    high_ids = lax.broadcasted_iota(jnp.int32, (HIGH, PIX), 0)
+    low_ids = lax.broadcasted_iota(jnp.int32, (LOW, PIX), 0)
+
+    def step(i, acc):
         row = pl.ds(i, 1)
-        ids = ins_ref[row, at_ids]
+        ids = ins_ref[row, :]
         high = lax.shift_right_logical(ids, 7)
         low = lax.bitwise_and(ids, LOW - 1)
-        value = w_ref[row, at] * scale
+        value = w_ref[row, :] * scale
         head = value.astype(jnp.bfloat16).astype(jnp.float32)
         tail = value - head
-        here = high == lax.broadcasted_iota(jnp.int32, (HIGH, width), 0)
+        here = high == high_ids
         rows = jnp.concatenate(
             [jnp.where(here, head, 0.0), jnp.where(here, tail, 0.0)], axis=0
         ).astype(jnp.bfloat16)
-        there = low == lax.broadcasted_iota(jnp.int32, (LOW, width), 0)
-        table = jnp.where(there, 1.0, 0.0).astype(jnp.bfloat16)
-        return acc + lax.dot_general(
-            rows, table, (((1,), (1,)), ((), ())), preferred_element_type=jnp.float32
-        )
+        table = jnp.where(low == low_ids, 1.0, 0.0).astype(jnp.bfloat16)
+        return acc + lax.dot_general(rows, table, DIMS, preferred_element_type=jnp.float32)
 
     empty = jnp.zeros((2 * HIGH, LOW), jnp.float32)
-    if rest:
-        step = lambda i, acc: add(acc, i, slice(0, REST), slice(BORDER, PIX), REST)
-        acc = lax.fori_loop(0, 16, step, empty)
-        refs[0][...] = acc[:HIGH] + acc[HIGH:]
+    acc = lax.fori_loop(0, 16, step, empty, unroll=1 if len(refs) == 1 else 4)
+    slab = acc[:HIGH] + acc[HIGH:]
+    if len(refs) == 1:
+        refs[0][...] = slab
     else:
-        slab_ref, out_ref = refs
-
-        def step(i, both):
-            re, im = both
-            re = add(re, i, slice(0, PIX), slice(0, PIX), PIX)
-            im = add(im, i, slice(PIX, SPLIT), slice(0, BORDER), BORDER)
-            return re, im
-
-        re, im = lax.fori_loop(0, 16, step, (empty, empty))
-        re = re[:HIGH] + re[HIGH:]
-        im = slab_ref[...] + im[:HIGH] + im[HIGH:]
+        im_ref, out_ref = refs
         for h in range(HIGH):
             at = slice(h * LOW, (h + 1) * LOW)
-            out_ref[0:1, at] = re[h : h + 1, :]
-            out_ref[1:2, at] = im[h : h + 1, :]
-
-
-def insert_call(shape, *args):
+            out_ref[0:1, at] = slab[h : h + 1, :]
+            out_ref[1:2, at] = im_ref[h : h + 1, :]
+
+
+def insert(bound, weighted, insertion, *im):
+    shape = (2, VOX) if im else (HIGH, LOW)
     return pl.pallas_call(
         insert_kernel,
-        in_specs=[VMEM] * len(args),
+        in_specs=[VMEM] * (3 + len(im)),
         out_specs=VMEM,
         out_shape=jax.ShapeDtypeStruct(shape, jnp.float32),
         compiler_params=limit(8),
         cost_estimate=pl.CostEstimate(
             flops=4 * HIGH * LOW * 16 * PIX, bytes_accessed=512 * 1024, transcendentals=0
         ),
-    )(*args)
-
-
-def insert_rest(bound, weighted, insertion):
-    return insert_call((HIGH, LOW), bound, weighted.reshape(16, REST), insertion)
-
-
-def insert_first(bound, weighted, insertion, slab):
-    return insert_call((2, VOX), bound, weighted.reshape(16, SPLIT), insertion, slab)
+        name="insert_re" if im else "insert_im",
+    )(bound, weighted.reshape(16, PIX), insertion, *im)
 
 
 def img_index(z, x, c):
@@ -512,7 +490,10 @@
 
 
 def exchange_refs(value):
-    return lax.all_gather(value, "ref")
+    out = [value]
+    for k in range(1, REFS):
+        out.append(lax.ppermute(value, "ref", [(r, (r + k) % REFS) for r in range(REFS)]))
+    return out
 
 
 def one_device(particles, projections, significance, insertion):
@@ -527,21 +508,19 @@
     unit = prepare(particles, projections)
     unit, pos, sig = lax.optimization_barrier((unit, pos, sig))
     messages, batches = gather(projections, unit)
-    own_re, own_im = shifted_images(table, particles)
-    mate_re, mate_im = shifted_images(table, mate)
-
-    shifted = (own_re, own_im, mate_re, mate_im)
+    shifted = shifted_images(table, particles, mate)
+
     acc = score_first(sig, pos, messages, shifted)
     scores, stats = score_rest(sig, pos, messages, batches, shifted, acc)
     merged = merge(stats, send(stats, dc=1))
     every = exchange_refs(merged)
-    sums, weights, evidence = partial_sums(True, sig, pos, (scores, every), shifted)
-    (sums_rest,) = partial_sums(False, sig, pos, (weights, merged), shifted)
-    total = scatter_z_first(sums.reshape(Z, X, 2, 8, SPLIT))
-    total_rest = scatter_x_first(sums_rest.reshape(X, Z, 2, 8, REST))
+    sums_im, weights, evidence = partial_sums(False, sig, pos, (scores, *every), shifted[1])
+    (sums_re,) = partial_sums(True, sig, pos, (weights, merged), shifted[0])
+    total_im = scatter_x_first(sums_im.reshape(X, Z, 2, 8, PIX))
+    total_re = scatter_z_first(sums_re.reshape(Z, X, 2, 8, PIX))
     ids = insertion.reshape(16, PIX)
-    slab = insert_rest(merged, total_rest, ids)
-    volume = insert_first(merged, total, ids, slab)
+    slab = insert(merged, total_im, ids)
+    volume = insert(merged, total_re, ids, slab)
     return volume, evidence.reshape(N)
 
 

time: 160 us -> 152 us (0.950); the launches traced: 158 us -> 151 us
  blocking collectives: 12.1 us -> 0 us
  waiting for transfers between devices: 46.4 us -> 52.7 us
  starting transfers between devices: 53.4 us -> 56 us
  Pallas kernels: 36.7 us -> 34.9 us
    all_gather x1 -> x0, blocking collectives: 12.1 us -> none  [exchange_refs(): return lax.all_gather(value, 'ref')]
    ppermute x0 -> x3, starting transfers between devices: none -> 4.96 us  [exchange_refs(): lax.ppermute(value, 'ref', [(r, (r + k) % REFS) for r in range(REFS)])]
    ppermute x31, waiting for transfers between devices: 42.7 us -> 46.2 us  [send(): return lax.ppermute(value, 'img', pairs(dz, dx, dc))]
    pallas_call x5 -> x4, Pallas kernels: 21.9 us -> 19.4 us  [the longest x2 9.72 us: insert(): pl.pallas_call(insert_kernel, in_specs=[VMEM] * (3 + len(im)), out_specs=...]
    ppermute x0 -> x3, waiting for transfers between devices: none -> 1.75 us  [exchange_refs(): lax.ppermute(value, 'ref', [(r, (r + k) % REFS) for r in range(REFS)])]
    ppermute x31, starting transfers between devices: 47.5 us -> 45.8 us  [send(): return lax.ppermute(value, 'img', pairs(dz, dx, dc))]
    unnamed x14 -> x12, local copies, waits for them, and re-layouts: 3.92 us -> 2.51 us
  transfers between devices with their start and end apart: 32 -> 35, of which waited for: 14 -> 18; matrix products, arithmetic and copies ran while one was open for 2% -> 2% of each run, Pallas kernels for 10% -> 7%
where the time goes in v3:
time: 152 us; the launch traced here: 151 us
  starting transfers between devices  56 us (37%)
  waiting for transfers between devices  52.7 us (35%)
  Pallas kernels  34.9 us (23%)
  local copies, waits for them, and re-layouts  4.22 us (3%)
  other arithmetic  2.48 us (2%)
    ppermute x31, waiting for transfers between devices, send(): return lax.ppermute(value, 'img', pairs(dz, dx, dc))  46.2 us
    ppermute x31, starting transfers between devices, send(): return lax.ppermute(value, 'img', pairs(dz, dx, dc))  45.8 us
    pallas_call x2, Pallas kernels, partial_sums(): pl.pallas_call(lambda *refs: partial_kernel(z_first, *refs), in_specs=[SM...  10.2 us
    pallas_call x2, Pallas kernels, insert(): pl.pallas_call(insert_kernel, in_specs=[VMEM] * (3 + len(im)), out_specs=...  9.72 us
    pallas_call x1, Pallas kernels, shifted_images(): pl.pallas_call(shift_kernel, in_specs=[VMEM] * 3, out_specs=[VMEM, VMEM],...  5.49 us
    all_to_all x1, starting transfers between devices, all_to_all_z(): lax.all_to_all(value, 'img', split_axis=0, concat_axis=0, tiled=True, axi...  5.25 us
    ppermute x3, starting transfers between devices, exchange_refs(): lax.ppermute(value, 'ref', [(r, (r + k) % REFS) for r in range(REFS)])  4.96 us
    pallas_call x1, Pallas kernels, score_first(): pl.pallas_call(score_first_kernel, in_specs=[SMEM, SMEM] + [VMEM] * (Z +...  4.76 us
  transfers between devices with their start and end apart: 35, of which 18 were waited for; matrix products, arithmetic and copies ran while one was open for 2% of the time, Pallas kernels for 7%

profile of v3, /device:TPU:8, one launch (start us, length us, event | category | flops | bytes accessed | tf_op | source)
XLA Modules:
  0.0 151.2 jit_solution(29948600127661844)
XLA Ops:
  12.5 4.0 %collective-permute-start.3 = (bf16[2,8,11904]{2,1,0:T(8,128)(2,1)S(1)}, bf16[2,8,11904]{2,1,0:T(8,128)(2,1)S(1)}, u32[]{:S(2)}, u32[]{:S(2)}) collective-permute-start(bf16[2,8,11904]{2,1,0:T(8,128)(2,1)S(1)} %assemble.1.refs_0_), channel_id=1, source_target_pairs={{0,224},{4,228},{8,232},{12,236},{16,240},{20,244},{24,248},{28,25... | collective-permute-start | bytes 1142792 | tf_op jit(solution)/shard_map/ppermute | solution.py:433
  16.5 8.6 %collective-permute-done.6.refs_4_.refs_7_ = bf16[2,8,11904]{2,1,0:T(8,128)(2,1)S(1)} collective-permute-done((bf16[2,8,11904]{2,1,0:T(8,128)(2,1)S(1)}, bf16[2,8,11904]{2,1,0:T(8,128)(2,1)S(1)}, u32[]{:S(2)}, u32[]{:S(2)}) %collective-permute-start.6) | collective-permute-done | bytes 380960 | tf_op jit(solution)/shard_map/ppermute | solution.py:433
  25.1 3.2 %collective-permute-start.4 = (bf16[2,8,11904]{2,1,0:T(8,128)(2,1)S(1)}, bf16[2,8,11904]{2,1,0:T(8,128)(2,1)S(1)}, u32[]{:S(2)}, u32[]{:S(2)}) collective-permute-start(bf16[2,8,11904]{2,1,0:T(8,128)(2,1)S(1)} %collective-permute-done.3.refs_1_), channel_id=1, source_target_pairs={{0,224},{4,228},{8,232},{12,236},{16,240},{20,244},{24,248},{28,25... | collective-permute-start | bytes 1142792 | tf_op jit(solution)/shard_map/ppermute | solution.py:433
  28.3 7.8 %collective-permute-done.7.refs_3_.refs_6_ = bf16[2,8,11904]{2,1,0:T(8,128)(2,1)S(1)} collective-permute-done((bf16[2,8,11904]{2,1,0:T(8,128)(2,1)S(1)}, bf16[2,8,11904]{2,1,0:T(8,128)(2,1)S(1)}, u32[]{:S(2)}, u32[]{:S(2)}) %collective-permute-start.7) | collective-permute-done | bytes 380960 | tf_op jit(solution)/shard_map/ppermute | solution.py:433
  36.1 3.2 %collective-permute-start.5 = (bf16[2,8,11904]{2,1,0:T(8,128)(2,1)S(1)}, bf16[2,8,11904]{2,1,0:T(8,128)(2,1)S(1)}, u32[]{:S(2)}, u32[]{:S(2)}) collective-permute-start(bf16[2,8,11904]{2,1,0:T(8,128)(2,1)S(1)} %collective-permute-done.4.refs_2_), channel_id=1, source_target_pairs={{0,224},{4,228},{8,232},{12,236},{16,240},{20,244},{24,248},{28,25... | collective-permute-start | bytes 1142792 | tf_op jit(solution)/shard_map/ppermute | solution.py:433
  39.3 6.9 %collective-permute-done.8.refs_2_.refs_5_ = bf16[2,8,11904]{2,1,0:T(8,128)(2,1)S(1)} collective-permute-done((bf16[2,8,11904]{2,1,0:T(8,128)(2,1)S(1)}, bf16[2,8,11904]{2,1,0:T(8,128)(2,1)S(1)}, u32[]{:S(2)}, u32[]{:S(2)}) %collective-permute-start.8) | collective-permute-done | bytes 380960 | tf_op jit(solution)/shard_map/ppermute | solution.py:433
  50.8 4.8 %collective-permute-done.9.refs_1_.refs_4_ = bf16[2,8,11904]{2,1,0:T(8,128)(2,1)S(1)} collective-permute-done((bf16[2,8,11904]{2,1,0:T(8,128)(2,1)S(1)}, bf16[2,8,11904]{2,1,0:T(8,128)(2,1)S(1)}, u32[]{:S(2)}, u32[]{:S(2)}) %collective-permute-start.9) | collective-permute-done | bytes 380960 | tf_op jit(solution)/shard_map/ppermute | solution.py:433
  57.3 5.5 %shift.1 = (bf16[2,5,256,2048]{3,2,1,0:T(8,128)(2,1)S(1)}, bf16[2,5,256,2048]{3,2,1,0:T(8,128)(2,1)S(1)}) custom-call(f32[8,2048]{1,0:T(8,128)S(1)} %copy-done.4, bf16[256,4096]{1,0:T(8,128)(2,1)S(1)} %copy-done.2, bf16[256,4096]{1,0:T(8,128)(2,1)} %collective-permute-done.16.mate_ref), custom_call_target="tpu_custom_call" | custom-call | flops 25165824 | bytes 25165824 | tf_op jit(solution)/shard_map/shift/pallas_call | solution.py:138
  65.6 4.8 %score_first.1.refs_15_ = f32[2,1280,256]{2,1,0:T(8,128)S(1)} custom-call(s32[2,512]{1,0:T(2,128)S(1)} %constant_dynamic-slice_fusion.sig_ref.refs_0_, s32[4]{0:T(128)S(1)} %pad_add_fusion.pos_ref.refs_1_, bf16[2,8,11904]{2,1,0:T(8,128)(2,1)S(1)} %assemble.1.refs_0_, bf16[2,8,11904]{2,1,0:T(8,128)(2,1)S(1)} %collective-permute-done.3.refs_1_, ...), custom_call_target="tpu_custom_call" | custom-call | flops 3355443200 | bytes 16777216 | tf_op jit(solution)/shard_map/score_first/pallas_call | solution.py:186
  70.4 4.2 %score_rest.1 = (f32[2,256,1280]{2,1,0:T(8,128)S(1)}, f32[8,256]{1,0:T(8,128)S(1)}) custom-call(s32[2,512]{1,0:T(2,128)S(1)} %constant_dynamic-slice_fusion.sig_ref.refs_0_, s32[4]{0:T(128)S(1)} %pad_add_fusion.pos_ref.refs_1_, bf16[2,8,11904]{2,1,0:T(8,128)(2,1)S(1)} %assemble.1.refs_0_, bf16[2,8,11904]{2,1,0:T(8,128)(2,1)S(1)} %collective-permute-done.3.refs_1_, ...), custom_call_target="tpu_custom_call" | custom-call | flops 2013265920 | bytes 16777216 | tf_op jit(solution)/shard_map/score_rest/pallas_call | solution.py:249
  82.7 5.5 %partial_im.1 = (f32[512,2048]{1,0:T(8,128)S(1)}, bf16[2,256,1280]{2,1,0:T(8,128)(2,1)S(1)}, f32[1,256]{1,0:T(1,128)}) custom-call(s32[2,512]{1,0:T(2,128)S(1)} %constant_dynamic-slice_fusion.sig_ref.refs_0_, s32[4]{0:T(128)S(1)} %pad_add_fusion.pos_ref.refs_1_, f32[2,256,1280]{2,1,0:T(8,128)S(1)} %get-tuple-element.18.refs_2_, ...), custom_call_target="tpu_custom_call" | custom-call | flops 2684354560 | bytes 16777216 | tf_op jit(solution)/shard_map/partial_im/pallas_call | solution.py:352
  88.7 4.7 %partial_re.1 = f32[512,2048]{1,0:T(8,128)S(1)} custom-call(s32[2,512]{1,0:T(2,128)S(1)} %constant_dynamic-slice_fusion.sig_ref.refs_0_, s32[4]{0:T(128)S(1)} %pad_add_fusion.pos_ref.refs_1_, bf16[2,256,1280]{2,1,0:T(8,128)(2,1)S(1)} %get-tuple-element.19.refs_2_, f32[8,256]{1,0:T(8,128)S(1)} %merge.1.refs_3_.bound_ref, ...), custom_call_target="tpu_custom_call" | custom-call | flops 2684354560 | bytes 16777216 | tf_op jit(solution)/shard_map/partial_re/pallas_call | solution.py:352
  98.6 3.2 %collective-permute-start.25 = (f16[4,2,8,2048]{3,2,1,0:T(8,128)(2,1)S(1)}, f16[4,2,8,2048]{3,2,1,0:T(8,128)(2,1)S(1)}, u32[]{:S(2)}, u32[]{:S(2)}) collective-permute-start(f16[4,2,8,2048]{3,2,1,0:T(8,128)(2,1)S(1)} %bitcast.50), channel_id=1, source_target_pairs={{0,224},{4,228},{8,232},{12,236},{16,240},{20,244},{24,248},{28,25... | collective-permute-start | bytes 786440 | tf_op jit(solution)/shard_map/ppermute | solution.py:433
  102.6 3.1 %collective-permute-done.25 = f16[4,2,8,2048]{3,2,1,0:T(8,128)(2,1)S(1)} collective-permute-done((f16[4,2,8,2048]{3,2,1,0:T(8,128)(2,1)S(1)}, f16[4,2,8,2048]{3,2,1,0:T(8,128)(2,1)S(1)}, u32[]{:S(2)}, u32[]{:S(2)}) %collective-permute-start.25) | collective-permute-done | bytes 262176 | tf_op jit(solution)/shard_map/ppermute | solution.py:433
  105.8 3.8 %collective-permute-start.26 = (f16[4,2,8,2048]{3,2,1,0:T(8,128)(2,1)S(1)}, f16[4,2,8,2048]{3,2,1,0:T(8,128)(2,1)S(1)}, u32[]{:S(2)}, u32[]{:S(2)}) collective-permute-start(f16[4,2,8,2048]{3,2,1,0:T(8,128)(2,1)S(1)} %add_convert_fusion.2), channel_id=1, source_target_pairs={{0,224},{4,228},{8,232},{12,236},{16,240},{20,244},{24,248},{28,25... | collective-permute-start | bytes 786440 | tf_op jit(solution)/shard_map/ppermute | solution.py:433
  110.3 3.3 %collective-permute-done.26 = f16[4,2,8,2048]{3,2,1,0:T(8,128)(2,1)S(1)} collective-permute-done((f16[4,2,8,2048]{3,2,1,0:T(8,128)(2,1)S(1)}, f16[4,2,8,2048]{3,2,1,0:T(8,128)(2,1)S(1)}, u32[]{:S(2)}, u32[]{:S(2)}) %collective-permute-start.26) | collective-permute-done | bytes 262176 | tf_op jit(solution)/shard_map/ppermute | solution.py:433
  113.6 3.8 %collective-permute-start.27 = (f16[4,2,8,2048]{3,2,1,0:T(8,128)(2,1)S(1)}, f16[4,2,8,2048]{3,2,1,0:T(8,128)(2,1)S(1)}, u32[]{:S(2)}, u32[]{:S(2)}) collective-permute-start(f16[4,2,8,2048]{3,2,1,0:T(8,128)(2,1)S(1)} %add_convert_fusion.1), channel_id=1, source_target_pairs={{0,224},{4,228},{8,232},{12,236},{16,240},{20,244},{24,248},{28,25... | collective-permute-start | bytes 786440 | tf_op jit(solution)/shard_map/ppermute | solution.py:433
  118.0 2.9 %collective-permute-done.31 = f16[8,2,8,2048]{3,2,1,0:T(8,128)(2,1)S(1)} collective-permute-done((f16[8,2,8,2048]{3,2,1,0:T(8,128)(2,1)S(1)}, f16[8,2,8,2048]{3,2,1,0:T(8,128)(2,1)S(1)}, u32[]{:S(2)}, u32[]{:S(2)}) %collective-permute-start.31) | collective-permute-done | bytes 524320 | tf_op jit(solution)/shard_map/ppermute | solution.py:433
  122.1 5.2 %all-to-all-start = ((f16[8,2,8,2048]{3,2,1,0:T(8,128)(2,1)}), f16[8,2,8,2048]{3,2,1,0:T(8,128)(2,1)S(1)}, u32[]{:S(2)}, u32[]{:S(2)}) async-start(f16[8,2,8,2048]{3,2,1,0:T(8,128)(2,1)} %add_convert_fusion), calls=%async_computation | async-start | bytes 1048576 | tf_op jit(solution)/shard_map/all_to_all | solution.py:437
  128.0 2.9 %collective-permute-start.30 = (f16[2,8,2048]{2,1,0:T(8,128)(2,1)S(1)}, f16[2,8,2048]{2,1,0:T(8,128)(2,1)S(1)}, u32[]{:S(2)}, u32[]{:S(2)}) collective-permute-start(f16[2,8,2048]{2,1,0:T(8,128)(2,1)S(1)} %get-tuple-element.36), channel_id=1, source_target_pairs={{0,24},{4,28},{8,0},{12,4},{16,8},{20,12},{24,16},{28,20},{32,56},... | collective-permute-start | bytes 196616 | tf_op jit(solution)/shard_map/ppermute | solution.py:433
  133.4 3.3 %collective-permute-done.29 = f16[2,8,2048]{2,1,0:T(8,128)(2,1)S(1)} collective-permute-done((f16[2,8,2048]{2,1,0:T(8,128)(2,1)S(1)}, f16[2,8,2048]{2,1,0:T(8,128)(2,1)S(1)}, u32[]{:S(2)}, u32[]{:S(2)}) %collective-permute-start.29) | collective-permute-done | bytes 65568 | tf_op jit(solution)/shard_map/ppermute | solution.py:433
  136.7 4.8 %all-to-all-done = f16[8,2,8,2048]{3,2,1,0:T(8,128)(2,1)S(1)} async-done(((f16[8,2,8,2048]{3,2,1,0:T(8,128)(2,1)}), f16[8,2,8,2048]{3,2,1,0:T(8,128)(2,1)S(1)}, u32[]{:S(2)}, u32[]{:S(2)}) %all-to-all-start) | async-done | bytes 524320 | tf_op jit(solution)/shard_map/all_to_all | solution.py:437
  141.5 5.6 %insert_im.1.refs_0_ = f32[32,128]{1,0:T(8,128)S(1)} custom-call(f32[8,256]{1,0:T(8,128)S(1)} %merge.1.refs_3_.bound_ref, f32[16,2048]{1,0:T(8,128)S(1)} %bitcast.37, s32[16,2048]{1,0:T(8,128)S(1)} %bitcast.38), custom_call_target="tpu_custom_call" | custom-call | flops 536870912 | bytes 524288 | tf_op jit(solution)/shard_map/insert_im/pallas_call | solution.py:403
  147.1 4.2 %insert_re.1 = f32[2,4096]{1,0:T(2,128)} custom-call(f32[8,256]{1,0:T(8,128)S(1)} %merge.1.refs_3_.bound_ref, f32[16,2048]{1,0:T(8,128)S(1)} %fusion.3.w_ref, s32[16,2048]{1,0:T(8,128)S(1)} %bitcast.39, f32[32,128]{1,0:T(8,128)S(1)} %insert_im.1.refs_0_), custom_call_target="tpu_custom_call" | custom-call | flops 536870912 | bytes 524288 | tf_op jit(solution)/shard_map/insert_re/pallas_call | solution.py:403
  (89 shorter events, 41.1 us)
Async XLA Ops:
  0.6 55.0 %collective-permute-start.16 = (bf16[256,4096]{1,0:T(8,128)(2,1)}, bf16[256,4096]{1,0:T(8,128)(2,1)}, u32[]{:S(2)}, u32[]{:S(2)}) collective-permute-start(bf16[256,4096]{1,0:T(8,128)(2,1)} %own_ref.1), channel_id=1, source_target_pairs={{0,4},{4,0},{8,12},{12,8},{16,20},{20,16},{24,28},{28,24},{32,36},... | collective-permute-start | bytes 6291464 | tf_op jit(solution)/shard_map/ppermute | solution.py:433
  1.6 8.5 %collective-permute-start.2 = (bf16[2,8,2560]{2,1,0:T(8,128)(2,1)S(1)}, bf16[2,8,2560]{2,1,0:T(8,128)(2,1)S(1)}, u32[]{:S(2)}, u32[]{:S(2)}) collective-permute-start(bf16[2,8,2560]{2,1,0:T(8,128)(2,1)S(1)} %slice.71.refs_0_), channel_id=1, source_target_pairs={{0,8},{4,12},{8,16},{12,20},{16,24},{20,28},{24,0},{28,4},{32,40},... | collective-permute-start | bytes 245768 | tf_op jit(solution)/shard_map/ppermute | solution.py:433
  10.5 14.6 %collective-permute-start.6 = (bf16[2,8,11904]{2,1,0:T(8,128)(2,1)S(1)}, bf16[2,8,11904]{2,1,0:T(8,128)(2,1)S(1)}, u32[]{:S(2)}, u32[]{:S(2)}) collective-permute-start(bf16[2,8,11904]{2,1,0:T(8,128)(2,1)S(1)} %assemble.1.refs_0_), channel_id=1, source_target_pairs={{0,32},{4,36},{8,40},{12,44},{16,48},{20,52},{24,56},{28,60},{32,6... | collective-permute-start | bytes 1142792 | tf_op jit(solution)/shard_map/ppermute | solution.py:433
  12.5 12.6 %collective-permute-start.3 = (bf16[2,8,11904]{2,1,0:T(8,128)(2,1)S(1)}, bf16[2,8,11904]{2,1,0:T(8,128)(2,1)S(1)}, u32[]{:S(2)}, u32[]{:S(2)}) collective-permute-start(bf16[2,8,11904]{2,1,0:T(8,128)(2,1)S(1)} %assemble.1.refs_0_), channel_id=1, source_target_pairs={{0,224},{4,228},{8,232},{12,236},{16,240},{20,244},{24,248},{28,25... | collective-permute-start | bytes 1142792 | tf_op jit(solution)/shard_map/ppermute | solution.py:433
  25.1 11.0 %collective-permute-start.7 = (bf16[2,8,11904]{2,1,0:T(8,128)(2,1)S(1)}, bf16[2,8,11904]{2,1,0:T(8,128)(2,1)S(1)}, u32[]{:S(2)}, u32[]{:S(2)}) collective-permute-start(bf16[2,8,11904]{2,1,0:T(8,128)(2,1)S(1)} %collective-permute-done.6.refs_4_.refs_7_), channel_id=1, source_target_pairs={{0,32},{4,36},{8,40},{12,44},{16,48},{20,52},{24,56},{28,60},{32,6... | collective-permute-start | bytes 1142792 | tf_op jit(solution)/shard_map/ppermute | solution.py:433
  25.1 11.0 %collective-permute-start.4 = (bf16[2,8,11904]{2,1,0:T(8,128)(2,1)S(1)}, bf16[2,8,11904]{2,1,0:T(8,128)(2,1)S(1)}, u32[]{:S(2)}, u32[]{:S(2)}) collective-permute-start(bf16[2,8,11904]{2,1,0:T(8,128)(2,1)S(1)} %collective-permute-done.3.refs_1_), channel_id=1, source_target_pairs={{0,224},{4,228},{8,232},{12,236},{16,240},{20,244},{24,248},{28,25... | collective-permute-start | bytes 1142792 | tf_op jit(solution)/shard_map/ppermute | solution.py:433
  36.1 10.2 %collective-permute-start.8 = (bf16[2,8,11904]{2,1,0:T(8,128)(2,1)S(1)}, bf16[2,8,11904]{2,1,0:T(8,128)(2,1)S(1)}, u32[]{:S(2)}, u32[]{:S(2)}) collective-permute-start(bf16[2,8,11904]{2,1,0:T(8,128)(2,1)S(1)} %collective-permute-done.7.refs_3_.refs_6_), channel_id=1, source_target_pairs={{0,32},{4,36},{8,40},{12,44},{16,48},{20,52},{24,56},{28,60},{32,6... | collective-permute-start | bytes 1142792 | tf_op jit(solution)/shard_map/ppermute | solution.py:433
  36.1 12.2 %collective-permute-start.5 = (bf16[2,8,11904]{2,1,0:T(8,128)(2,1)S(1)}, bf16[2,8,11904]{2,1,0:T(8,128)(2,1)S(1)}, u32[]{:S(2)}, u32[]{:S(2)}) collective-permute-start(bf16[2,8,11904]{2,1,0:T(8,128)(2,1)S(1)} %collective-permute-done.4.refs_2_), channel_id=1, source_target_pairs={{0,224},{4,228},{8,232},{12,236},{16,240},{20,244},{24,248},{28,25... | collective-permute-start | bytes 1142792 | tf_op jit(solution)/shard_map/ppermute | solution.py:433
  46.2 9.3 %collective-permute-start.9 = (bf16[2,8,11904]{2,1,0:T(8,128)(2,1)S(1)}, bf16[2,8,11904]{2,1,0:T(8,128)(2,1)S(1)}, u32[]{:S(2)}, u32[]{:S(2)}) collective-permute-start(bf16[2,8,11904]{2,1,0:T(8,128)(2,1)S(1)} %collective-permute-done.8.refs_2_.refs_5_), channel_id=1, source_target_pairs={{0,32},{4,36},{8,40},{12,44},{16,48},{20,52},{24,56},{28,60},{32,6... | collective-permute-start | bytes 1142792 | tf_op jit(solution)/shard_map/ppermute | solution.py:433
  46.3 16.5 %collective-permute-start.12 = (bf16[5,2,8,1664]{3,2,1,0:T(8,128)(2,1)S(1)}, bf16[5,2,8,1664]{3,2,1,0:T(8,128)(2,1)S(1)}, u32[]{:S(2)}, u32[]{:S(2)}) collective-permute-start(bf16[5,2,8,1664]{3,2,1,0:T(8,128)(2,1)S(1)} %pick.2), channel_id=1, source_target_pairs={{0,8},{4,12},{8,16},{12,20},{16,24},{20,28},{24,0},{28,4},{32,40},... | collective-permute-start | bytes 798728 | tf_op jit(solution)/shard_map/ppermute | solution.py:433
  46.4 24.0 %collective-permute-start.11 = (bf16[5,2,8,1664]{3,2,1,0:T(8,128)(2,1)S(1)}, bf16[5,2,8,1664]{3,2,1,0:T(8,128)(2,1)S(1)}, u32[]{:S(2)}, u32[]{:S(2)}) collective-permute-start(bf16[5,2,8,1664]{3,2,1,0:T(8,128)(2,1)S(1)} %pick.2), channel_id=1, source_target_pairs={{0,16},{4,20},{8,24},{12,28},{16,0},{20,4},{24,8},{28,12},{32,48},... | collective-permute-start | bytes 798728 | tf_op jit(solution)/shard_map/ppermute | solution.py:433
  48.3 22.1 %collective-permute-start.10 = (bf16[5,2,8,1664]{3,2,1,0:T(8,128)(2,1)S(1)}, bf16[5,2,8,1664]{3,2,1,0:T(8,128)(2,1)S(1)}, u32[]{:S(2)}, u32[]{:S(2)}) collective-permute-start(bf16[5,2,8,1664]{3,2,1,0:T(8,128)(2,1)S(1)} %pick.2), channel_id=1, source_target_pairs={{0,24},{4,28},{8,0},{12,4},{16,8},{20,12},{24,16},{28,20},{32,56},... | collective-permute-start | bytes 798728 | tf_op jit(solution)/shard_map/ppermute | solution.py:433
  55.6 14.8 %collective-permute-start.15 = (bf16[3,2,8,1664]{3,2,1,0:T(8,128)(2,1)S(1)}, bf16[3,2,8,1664]{3,2,1,0:T(8,128)(2,1)S(1)}, u32[]{:S(2)}, u32[]{:S(2)}) collective-permute-start(bf16[3,2,8,1664]{3,2,1,0:T(8,128)(2,1)S(1)} %pick.3), channel_id=1, source_target_pairs={{0,8},{4,12},{8,16},{12,20},{16,24},{20,28},{24,0},{28,4},{32,40},... | collective-permute-start | bytes 479240 | tf_op jit(solution)/shard_map/ppermute | solution.py:433
  55.7 14.7 %collective-permute-start.14 = (bf16[3,2,8,1664]{3,2,1,0:T(8,128)(2,1)S(1)}, bf16[3,2,8,1664]{3,2,1,0:T(8,128)(2,1)S(1)}, u32[]{:S(2)}, u32[]{:S(2)}) collective-permute-start(bf16[3,2,8,1664]{3,2,1,0:T(8,128)(2,1)S(1)} %pick.3), channel_id=1, source_target_pairs={{0,16},{4,20},{8,24},{12,28},{16,0},{20,4},{24,8},{28,12},{32,48},... | collective-permute-start | bytes 479240 | tf_op jit(solution)/shard_map/ppermute | solution.py:433
  94.2 8.2 %collective-permute-start.21 = (f16[4,2,8,2048]{3,2,1,0:T(8,128)(2,1)S(1)}, f16[4,2,8,2048]{3,2,1,0:T(8,128)(2,1)S(1)}, u32[]{:S(2)}, u32[]{:S(2)}) collective-permute-start(f16[4,2,8,2048]{3,2,1,0:T(8,128)(2,1)S(1)} %bitcast.51), channel_id=1, source_target_pairs={{0,32},{4,36},{8,40},{12,44},{16,48},{20,52},{24,56},{28,60},{32,6... | collective-permute-start | bytes 786440 | tf_op jit(solution)/shard_map/ppermute | solution.py:433
  94.5 23.5 %collective-permute-start.33 = (f16[8,2,8,2048]{3,2,1,0:T(8,128)(2,1)S(1)}, f16[8,2,8,2048]{3,2,1,0:T(8,128)(2,1)S(1)}, u32[]{:S(2)}, u32[]{:S(2)}) collective-permute-start(f16[8,2,8,2048]{3,2,1,0:T(8,128)(2,1)S(1)} %bitcast.49), channel_id=1, source_target_pairs={{0,24},{4,28},{8,0},{12,4},{16,8},{20,12},{24,16},{28,20},{32,56},... | collective-permute-start | bytes 1572872 | tf_op jit(solution)/shard_map/ppermute | solution.py:433
  96.2 24.7 %collective-permute-start.31 = (f16[8,2,8,2048]{3,2,1,0:T(8,128)(2,1)S(1)}, f16[8,2,8,2048]{3,2,1,0:T(8,128)(2,1)S(1)}, u32[]{:S(2)}, u32[]{:S(2)}) collective-permute-start(f16[8,2,8,2048]{3,2,1,0:T(8,128)(2,1)S(1)} %bitcast.48), channel_id=1, source_target_pairs={{0,8},{4,12},{8,16},{12,20},{16,24},{20,28},{24,0},{28,4},{32,40},... | collective-permute-start | bytes 1572872 | tf_op jit(solution)/shard_map/ppermute | solution.py:433
  96.6 24.3 %collective-permute-start.32 = (f16[8,2,8,2048]{3,2,1,0:T(8,128)(2,1)S(1)}, f16[8,2,8,2048]{3,2,1,0:T(8,128)(2,1)S(1)}, u32[]{:S(2)}, u32[]{:S(2)}) collective-permute-start(f16[8,2,8,2048]{3,2,1,0:T(8,128)(2,1)S(1)} %bitcast.47), channel_id=1, source_target_pairs={{0,16},{4,20},{8,24},{12,28},{16,0},{20,4},{24,8},{28,12},{32,48},... | collective-permute-start | bytes 1572872 | tf_op jit(solution)/shard_map/ppermute | solution.py:433
  102.5 7.7 %collective-permute-start.22 = (f16[4,2,8,2048]{3,2,1,0:T(8,128)(2,1)S(1)}, f16[4,2,8,2048]{3,2,1,0:T(8,128)(2,1)S(1)}, u32[]{:S(2)}, u32[]{:S(2)}) collective-permute-start(f16[4,2,8,2048]{3,2,1,0:T(8,128)(2,1)S(1)} %add_convert_fusion.5), channel_id=1, source_target_pairs={{0,32},{4,36},{8,40},{12,44},{16,48},{20,52},{24,56},{28,60},{32,6... | collective-permute-start | bytes 786440 | tf_op jit(solution)/shard_map/ppermute | solution.py:433
  105.8 7.8 %collective-permute-start.26 = (f16[4,2,8,2048]{3,2,1,0:T(8,128)(2,1)S(1)}, f16[4,2,8,2048]{3,2,1,0:T(8,128)(2,1)S(1)}, u32[]{:S(2)}, u32[]{:S(2)}) collective-permute-start(f16[4,2,8,2048]{3,2,1,0:T(8,128)(2,1)S(1)} %add_convert_fusion.2), channel_id=1, source_target_pairs={{0,224},{4,228},{8,232},{12,236},{16,240},{20,244},{24,248},{28,25... | collective-permute-start | bytes 786440 | tf_op jit(solution)/shard_map/ppermute | solution.py:433
  110.2 7.7 %collective-permute-start.23 = (f16[4,2,8,2048]{3,2,1,0:T(8,128)(2,1)S(1)}, f16[4,2,8,2048]{3,2,1,0:T(8,128)(2,1)S(1)}, u32[]{:S(2)}, u32[]{:S(2)}) collective-permute-start(f16[4,2,8,2048]{3,2,1,0:T(8,128)(2,1)S(1)} %add_convert_fusion.4), channel_id=1, source_target_pairs={{0,32},{4,36},{8,40},{12,44},{16,48},{20,52},{24,56},{28,60},{32,6... | collective-permute-start | bytes 786440 | tf_op jit(solution)/shard_map/ppermute | solution.py:433
  113.6 13.7 %collective-permute-start.27 = (f16[4,2,8,2048]{3,2,1,0:T(8,128)(2,1)S(1)}, f16[4,2,8,2048]{3,2,1,0:T(8,128)(2,1)S(1)}, u32[]{:S(2)}, u32[]{:S(2)}) collective-permute-start(f16[4,2,8,2048]{3,2,1,0:T(8,128)(2,1)S(1)} %add_convert_fusion.1), channel_id=1, source_target_pairs={{0,224},{4,228},{8,232},{12,236},{16,240},{20,244},{24,248},{28,25... | collective-permute-start | bytes 786440 | tf_op jit(solution)/shard_map/ppermute | solution.py:433
  117.9 9.5 %collective-permute-start.24 = (f16[4,2,8,2048]{3,2,1,0:T(8,128)(2,1)S(1)}, f16[4,2,8,2048]{3,2,1,0:T(8,128)(2,1)S(1)}, u32[]{:S(2)}, u32[]{:S(2)}) collective-permute-start(f16[4,2,8,2048]{3,2,1,0:T(8,128)(2,1)S(1)} %add_convert_fusion.3), channel_id=1, source_target_pairs={{0,32},{4,36},{8,40},{12,44},{16,48},{20,52},{24,56},{28,60},{32,6... | collective-permute-start | bytes 786440 | tf_op jit(solution)/shard_map/ppermute | solution.py:433
  122.1 19.3 %all-to-all-start = ((f16[8,2,8,2048]{3,2,1,0:T(8,128)(2,1)}), f16[8,2,8,2048]{3,2,1,0:T(8,128)(2,1)S(1)}, u32[]{:S(2)}, u32[]{:S(2)}) async-start(f16[8,2,8,2048]{3,2,1,0:T(8,128)(2,1)} %add_convert_fusion), calls=%async_computation | async-start | bytes 1048576 | tf_op jit(solution)/shard_map/all_to_all | solution.py:437
  (17 other events, 184.1 us)

commit v4 on v3

--- a/solution.py
+++ b/solution.py
@@ -22,7 +22,7 @@
 SCALE = 2.0 / math.sqrt(FEATURES)
 HEADROOM = 2.5
 EXTRA = 128
-SPLIT = 2560
+SPLIT = 2304
 REST = FEATURES - SPLIT
 BORDER = SPLIT - PIX
 UNIT = REST + EXTRA
@@ -485,8 +485,8 @@
 
 def scatter_x_first(parts):
     arrived = [send(narrow(parts[k]), dx=k) for k in range(1, X)]
-    column = parts[0] + wide(arrived[0]) + wide(arrived[1]) + wide(arrived[2])
-    return jnp.sum(wide(all_to_all_z(narrow(column))), axis=0)
+    column = narrow(parts[0] + wide(arrived[0]) + wide(arrived[1]) + wide(arrived[2]))
+    return jnp.sum(wide(all_to_all_z(column)), axis=0)
 
 
 def exchange_refs(value):

time: 152 us -> 151 us (level)
  starting transfers between devices: 56 us -> 53.1 us
  waiting for transfers between devices: 52.7 us -> 54.4 us
    ppermute x31, starting transfers between devices: 45.8 us -> 42.6 us  [send(): return lax.ppermute(value, 'img', pairs(dz, dx, dc))]
    ppermute x31, waiting for transfers between devices: 46.2 us -> 47.8 us  [send(): return lax.ppermute(value, 'img', pairs(dz, dx, dc))]
  transfers between devices with their start and end apart: 35 -> 35, of which waited for: 18 -> 19; matrix products, arithmetic and copies ran while one was open for 2% -> 2% of each run, Pallas kernels for 7% -> 7%
where the time goes in v4:
time: 151 us; the launch traced here: 150 us
  waiting for transfers between devices  54.4 us (36%)
  starting transfers between devices  53.1 us (35%)
  Pallas kernels  34.8 us (23%)
  local copies, waits for them, and re-layouts  4.3 us (3%)
  other arithmetic  2.44 us (2%)
    ppermute x31, waiting for transfers between devices, send(): return lax.ppermute(value, 'img', pairs(dz, dx, dc))  47.8 us
    ppermute x31, starting transfers between devices, send(): return lax.ppermute(value, 'img', pairs(dz, dx, dc))  42.6 us
    pallas_call x2, Pallas kernels, partial_sums(): pl.pallas_call(lambda *refs: partial_kernel(z_first, *refs), in_specs=[SM...  10.2 us
    pallas_call x2, Pallas kernels, insert(): pl.pallas_call(insert_kernel, in_specs=[VMEM] * (3 + len(im)), out_specs=...  9.72 us
    all_to_all x1, starting transfers between devices, all_to_all_z(): lax.all_to_all(value, 'img', split_axis=0, concat_axis=0, tiled=True, axi...  5.52 us
    pallas_call x1, Pallas kernels, shifted_images(): pl.pallas_call(shift_kernel, in_specs=[VMEM] * 3, out_specs=[VMEM, VMEM],...  5.49 us
    ppermute x3, starting transfers between devices, exchange_refs(): lax.ppermute(value, 'ref', [(r, (r + k) % REFS) for r in range(REFS)])  4.94 us
    all_to_all x1, waiting for transfers between devices, all_to_all_z(): lax.all_to_all(value, 'img', split_axis=0, concat_axis=0, tiled=True, axi...  4.84 us
  transfers between devices with their start and end apart: 35, of which 19 were waited for; matrix products, arithmetic and copies ran while one was open for 2% of the time, Pallas kernels for 7%

profile of v4, /device:TPU:8, one launch (start us, length us, event | category | flops | bytes accessed | tf_op | source)
XLA Modules:
  0.0 150.0 jit_solution(12089641624353318754)
XLA Ops:
  3.1 2.7 %collective-permute-start.1 = (bf16[2,8,2304]{2,1,0:T(8,128)(2,1)S(1)}, bf16[2,8,2304]{2,1,0:T(8,128)(2,1)S(1)}, u32[]{:S(2)}, u32[]{:S(2)}) collective-permute-start(bf16[2,8,2304]{2,1,0:T(8,128)(2,1)S(1)} %slice.71.refs_0_), channel_id=1, source_target_pairs={{0,16},{4,20},{8,24},{12,28},{16,0},{20,4},{24,8},{28,12},{32,48},... | collective-permute-start | bytes 221192 | tf_op jit(solution)/shard_map/ppermute | solution.py:433
  12.2 4.0 %collective-permute-start.3 = (bf16[2,8,11136]{2,1,0:T(8,128)(2,1)S(1)}, bf16[2,8,11136]{2,1,0:T(8,128)(2,1)S(1)}, u32[]{:S(2)}, u32[]{:S(2)}) collective-permute-start(bf16[2,8,11136]{2,1,0:T(8,128)(2,1)S(1)} %assemble.1.refs_0_), channel_id=1, source_target_pairs={{0,224},{4,228},{8,232},{12,236},{16,240},{20,244},{24,248},{28,25... | collective-permute-start | bytes 1069064 | tf_op jit(solution)/shard_map/ppermute | solution.py:433
  16.3 8.0 %collective-permute-done.6.refs_4_.refs_7_ = bf16[2,8,11136]{2,1,0:T(8,128)(2,1)S(1)} collective-permute-done((bf16[2,8,11136]{2,1,0:T(8,128)(2,1)S(1)}, bf16[2,8,11136]{2,1,0:T(8,128)(2,1)S(1)}, u32[]{:S(2)}, u32[]{:S(2)}) %collective-permute-start.6) | collective-permute-done | bytes 356384 | tf_op jit(solution)/shard_map/ppermute | solution.py:433
  24.3 3.2 %collective-permute-start.4 = (bf16[2,8,11136]{2,1,0:T(8,128)(2,1)S(1)}, bf16[2,8,11136]{2,1,0:T(8,128)(2,1)S(1)}, u32[]{:S(2)}, u32[]{:S(2)}) collective-permute-start(bf16[2,8,11136]{2,1,0:T(8,128)(2,1)S(1)} %collective-permute-done.3.refs_1_), channel_id=1, source_target_pairs={{0,224},{4,228},{8,232},{12,236},{16,240},{20,244},{24,248},{28,25... | collective-permute-start | bytes 1069064 | tf_op jit(solution)/shard_map/ppermute | solution.py:433
  27.5 7.3 %collective-permute-done.7.refs_3_.refs_6_ = bf16[2,8,11136]{2,1,0:T(8,128)(2,1)S(1)} collective-permute-done((bf16[2,8,11136]{2,1,0:T(8,128)(2,1)S(1)}, bf16[2,8,11136]{2,1,0:T(8,128)(2,1)S(1)}, u32[]{:S(2)}, u32[]{:S(2)}) %collective-permute-start.7) | collective-permute-done | bytes 356384 | tf_op jit(solution)/shard_map/ppermute | solution.py:433
  34.8 3.2 %collective-permute-start.5 = (bf16[2,8,11136]{2,1,0:T(8,128)(2,1)S(1)}, bf16[2,8,11136]{2,1,0:T(8,128)(2,1)S(1)}, u32[]{:S(2)}, u32[]{:S(2)}) collective-permute-start(bf16[2,8,11136]{2,1,0:T(8,128)(2,1)S(1)} %collective-permute-done.4.refs_2_), channel_id=1, source_target_pairs={{0,224},{4,228},{8,232},{12,236},{16,240},{20,244},{24,248},{28,25... | collective-permute-start | bytes 1069064 | tf_op jit(solution)/shard_map/ppermute | solution.py:433
  38.0 6.4 %collective-permute-done.8.refs_2_.refs_5_ = bf16[2,8,11136]{2,1,0:T(8,128)(2,1)S(1)} collective-permute-done((bf16[2,8,11136]{2,1,0:T(8,128)(2,1)S(1)}, bf16[2,8,11136]{2,1,0:T(8,128)(2,1)S(1)}, u32[]{:S(2)}, u32[]{:S(2)}) %collective-permute-start.8) | collective-permute-done | bytes 356384 | tf_op jit(solution)/shard_map/ppermute | solution.py:433
  48.8 4.4 %collective-permute-done.9.refs_1_.refs_4_ = bf16[2,8,11136]{2,1,0:T(8,128)(2,1)S(1)} collective-permute-done((bf16[2,8,11136]{2,1,0:T(8,128)(2,1)S(1)}, bf16[2,8,11136]{2,1,0:T(8,128)(2,1)S(1)}, u32[]{:S(2)}, u32[]{:S(2)}) %collective-permute-start.9) | collective-permute-done | bytes 356384 | tf_op jit(solution)/shard_map/ppermute | solution.py:433
  54.9 5.5 %shift.1 = (bf16[2,5,256,2048]{3,2,1,0:T(8,128)(2,1)S(1)}, bf16[2,5,256,2048]{3,2,1,0:T(8,128)(2,1)S(1)}) custom-call(f32[8,2048]{1,0:T(8,128)S(1)} %copy-done.4, bf16[256,4096]{1,0:T(8,128)(2,1)S(1)} %copy-done.2, bf16[256,4096]{1,0:T(8,128)(2,1)} %collective-permute-done.16.mate_ref), custom_call_target="tpu_custom_call" | custom-call | flops 25165824 | bytes 25165824 | tf_op jit(solution)/shard_map/shift/pallas_call | solution.py:138
  63.2 4.4 %score_first.1.refs_15_ = f32[2,1280,256]{2,1,0:T(8,128)S(1)} custom-call(s32[2,512]{1,0:T(2,128)S(1)} %constant_dynamic-slice_fusion.sig_ref.refs_0_, s32[4]{0:T(128)S(1)} %pad_add_fusion.pos_ref.refs_1_, bf16[2,8,11136]{2,1,0:T(8,128)(2,1)S(1)} %assemble.1.refs_0_, bf16[2,8,11136]{2,1,0:T(8,128)(2,1)S(1)} %collective-permute-done.3.refs_1_, ...), custom_call_target="tpu_custom_call" | custom-call | flops 3019898880 | bytes 16777216 | tf_op jit(solution)/shard_map/score_first/pallas_call | solution.py:186
  68.3 4.6 %score_rest.1 = (f32[2,256,1280]{2,1,0:T(8,128)S(1)}, f32[8,256]{1,0:T(8,128)S(1)}) custom-call(s32[2,512]{1,0:T(2,128)S(1)} %constant_dynamic-slice_fusion.sig_ref.refs_0_, s32[4]{0:T(128)S(1)} %pad_add_fusion.pos_ref.refs_1_, bf16[2,8,11136]{2,1,0:T(8,128)(2,1)S(1)} %assemble.1.refs_0_, bf16[2,8,11136]{2,1,0:T(8,128)(2,1)S(1)} %collective-permute-done.3.refs_1_, ...), custom_call_target="tpu_custom_call" | custom-call | flops 2348810240 | bytes 16777216 | tf_op jit(solution)/shard_map/score_rest/pallas_call | solution.py:249
  81.0 5.5 %partial_im.1 = (f32[512,2048]{1,0:T(8,128)S(1)}, bf16[2,256,1280]{2,1,0:T(8,128)(2,1)S(1)}, f32[1,256]{1,0:T(1,128)}) custom-call(s32[2,512]{1,0:T(2,128)S(1)} %constant_dynamic-slice_fusion.sig_ref.refs_0_, s32[4]{0:T(128)S(1)} %pad_add_fusion.pos_ref.refs_1_, f32[2,256,1280]{2,1,0:T(8,128)S(1)} %get-tuple-element.18.refs_2_, ...), custom_call_target="tpu_custom_call" | custom-call | flops 2684354560 | bytes 16777216 | tf_op jit(solution)/shard_map/partial_im/pallas_call | solution.py:352
  86.9 4.7 %partial_re.1 = f32[512,2048]{1,0:T(8,128)S(1)} custom-call(s32[2,512]{1,0:T(2,128)S(1)} %constant_dynamic-slice_fusion.sig_ref.refs_0_, s32[4]{0:T(128)S(1)} %pad_add_fusion.pos_ref.refs_1_, bf16[2,256,1280]{2,1,0:T(8,128)(2,1)S(1)} %get-tuple-element.19.refs_2_, f32[8,256]{1,0:T(8,128)S(1)} %merge.1.refs_3_.bound_ref, ...), custom_call_target="tpu_custom_call" | custom-call | flops 2684354560 | bytes 16777216 | tf_op jit(solution)/shard_map/partial_re/pallas_call | solution.py:352
  96.4 3.2 %collective-permute-start.25 = (f16[4,2,8,2048]{3,2,1,0:T(8,128)(2,1)S(1)}, f16[4,2,8,2048]{3,2,1,0:T(8,128)(2,1)S(1)}, u32[]{:S(2)}, u32[]{:S(2)}) collective-permute-start(f16[4,2,8,2048]{3,2,1,0:T(8,128)(2,1)S(1)} %bitcast.50), channel_id=1, source_target_pairs={{0,224},{4,228},{8,232},{12,236},{16,240},{20,244},{24,248},{28,25... | collective-permute-start | bytes 786440 | tf_op jit(solution)/shard_map/ppermute | solution.py:433
  100.8 2.7 %collective-permute-done.25 = f16[4,2,8,2048]{3,2,1,0:T(8,128)(2,1)S(1)} collective-permute-done((f16[4,2,8,2048]{3,2,1,0:T(8,128)(2,1)S(1)}, f16[4,2,8,2048]{3,2,1,0:T(8,128)(2,1)S(1)}, u32[]{:S(2)}, u32[]{:S(2)}) %collective-permute-start.25) | collective-permute-done | bytes 262176 | tf_op jit(solution)/shard_map/ppermute | solution.py:433
  103.6 3.8 %collective-permute-start.26 = (f16[4,2,8,2048]{3,2,1,0:T(8,128)(2,1)S(1)}, f16[4,2,8,2048]{3,2,1,0:T(8,128)(2,1)S(1)}, u32[]{:S(2)}, u32[]{:S(2)}) collective-permute-start(f16[4,2,8,2048]{3,2,1,0:T(8,128)(2,1)S(1)} %add_convert_fusion.2), channel_id=1, source_target_pairs={{0,224},{4,228},{8,232},{12,236},{16,240},{20,244},{24,248},{28,25... | collective-permute-start | bytes 786440 | tf_op jit(solution)/shard_map/ppermute | solution.py:433
  111.3 3.8 %collective-permute-start.27 = (f16[4,2,8,2048]{3,2,1,0:T(8,128)(2,1)S(1)}, f16[4,2,8,2048]{3,2,1,0:T(8,128)(2,1)S(1)}, u32[]{:S(2)}, u32[]{:S(2)}) collective-permute-start(f16[4,2,8,2048]{3,2,1,0:T(8,128)(2,1)S(1)} %add_convert_fusion.1), channel_id=1, source_target_pairs={{0,224},{4,228},{8,232},{12,236},{16,240},{20,244},{24,248},{28,25... | collective-permute-start | bytes 786440 | tf_op jit(solution)/shard_map/ppermute | solution.py:433
  116.2 3.1 %collective-permute-done.31 = f16[8,2,8,2048]{3,2,1,0:T(8,128)(2,1)S(1)} collective-permute-done((f16[8,2,8,2048]{3,2,1,0:T(8,128)(2,1)S(1)}, f16[8,2,8,2048]{3,2,1,0:T(8,128)(2,1)S(1)}, u32[]{:S(2)}, u32[]{:S(2)}) %collective-permute-start.31) | collective-permute-done | bytes 524320 | tf_op jit(solution)/shard_map/ppermute | solution.py:433
  120.5 5.5 %all-to-all-start = ((f16[8,2,8,2048]{3,2,1,0:T(8,128)(2,1)}), f16[8,2,8,2048]{3,2,1,0:T(8,128)(2,1)S(1)}, u32[]{:S(2)}, u32[]{:S(2)}) async-start(f16[8,2,8,2048]{3,2,1,0:T(8,128)(2,1)} %add_convert_fusion), calls=%async_computation | async-start | bytes 1048576 | tf_op jit(solution)/shard_map/all_to_all | solution.py:437
  126.3 3.2 %collective-permute-start.30 = (f16[2,8,2048]{2,1,0:T(8,128)(2,1)S(1)}, f16[2,8,2048]{2,1,0:T(8,128)(2,1)S(1)}, u32[]{:S(2)}, u32[]{:S(2)}) collective-permute-start(f16[2,8,2048]{2,1,0:T(8,128)(2,1)S(1)} %get-tuple-element.36), channel_id=1, source_target_pairs={{0,24},{4,28},{8,0},{12,4},{16,8},{20,12},{24,16},{28,20},{32,56},... | collective-permute-start | bytes 196616 | tf_op jit(solution)/shard_map/ppermute | solution.py:433
  132.1 3.3 %collective-permute-done.29 = f16[2,8,2048]{2,1,0:T(8,128)(2,1)S(1)} collective-permute-done((f16[2,8,2048]{2,1,0:T(8,128)(2,1)S(1)}, f16[2,8,2048]{2,1,0:T(8,128)(2,1)S(1)}, u32[]{:S(2)}, u32[]{:S(2)}) %collective-permute-start.29) | collective-permute-done | bytes 65568 | tf_op jit(solution)/shard_map/ppermute | solution.py:433
  135.3 4.8 %all-to-all-done = f16[8,2,8,2048]{3,2,1,0:T(8,128)(2,1)S(1)} async-done(((f16[8,2,8,2048]{3,2,1,0:T(8,128)(2,1)}), f16[8,2,8,2048]{3,2,1,0:T(8,128)(2,1)S(1)}, u32[]{:S(2)}, u32[]{:S(2)}) %all-to-all-start) | async-done | bytes 524320 | tf_op jit(solution)/shard_map/all_to_all | solution.py:437
  140.3 5.6 %insert_im.1.refs_0_ = f32[32,128]{1,0:T(8,128)S(1)} custom-call(f32[8,256]{1,0:T(8,128)S(1)} %merge.1.refs_3_.bound_ref, f32[16,2048]{1,0:T(8,128)S(1)} %bitcast.37, s32[16,2048]{1,0:T(8,128)S(1)} %bitcast.38), custom_call_target="tpu_custom_call" | custom-call | flops 536870912 | bytes 524288 | tf_op jit(solution)/shard_map/insert_im/pallas_call | solution.py:403
  145.8 4.2 %insert_re.1 = f32[2,4096]{1,0:T(2,128)} custom-call(f32[8,256]{1,0:T(8,128)S(1)} %merge.1.refs_3_.bound_ref, f32[16,2048]{1,0:T(8,128)S(1)} %fusion.3.w_ref, s32[16,2048]{1,0:T(8,128)S(1)} %bitcast.39, f32[32,128]{1,0:T(8,128)S(1)} %insert_im.1.refs_0_), custom_call_target="tpu_custom_call" | custom-call | flops 536870912 | bytes 524288 | tf_op jit(solution)/shard_map/insert_re/pallas_call | solution.py:403
  (89 shorter events, 41.9 us)
Async XLA Ops:
  0.6 52.7 %collective-permute-start.16 = (bf16[256,4096]{1,0:T(8,128)(2,1)}, bf16[256,4096]{1,0:T(8,128)(2,1)}, u32[]{:S(2)}, u32[]{:S(2)}) collective-permute-start(bf16[256,4096]{1,0:T(8,128)(2,1)} %own_ref.1), channel_id=1, source_target_pairs={{0,4},{4,0},{8,12},{12,8},{16,20},{20,16},{24,28},{28,24},{32,36},... | collective-permute-start | bytes 6291464 | tf_op jit(solution)/shard_map/ppermute | solution.py:433
  1.6 8.5 %collective-permute-start.2 = (bf16[2,8,2304]{2,1,0:T(8,128)(2,1)S(1)}, bf16[2,8,2304]{2,1,0:T(8,128)(2,1)S(1)}, u32[]{:S(2)}, u32[]{:S(2)}) collective-permute-start(bf16[2,8,2304]{2,1,0:T(8,128)(2,1)S(1)} %slice.71.refs_0_), channel_id=1, source_target_pairs={{0,8},{4,12},{8,16},{12,20},{16,24},{20,28},{24,0},{28,4},{32,40},... | collective-permute-start | bytes 221192 | tf_op jit(solution)/shard_map/ppermute | solution.py:433
  10.2 14.1 %collective-permute-start.6 = (bf16[2,8,11136]{2,1,0:T(8,128)(2,1)S(1)}, bf16[2,8,11136]{2,1,0:T(8,128)(2,1)S(1)}, u32[]{:S(2)}, u32[]{:S(2)}) collective-permute-start(bf16[2,8,11136]{2,1,0:T(8,128)(2,1)S(1)} %assemble.1.refs_0_), channel_id=1, source_target_pairs={{0,32},{4,36},{8,40},{12,44},{16,48},{20,52},{24,56},{28,60},{32,6... | collective-permute-start | bytes 1069064 | tf_op jit(solution)/shard_map/ppermute | solution.py:433
  12.2 12.1 %collective-permute-start.3 = (bf16[2,8,11136]{2,1,0:T(8,128)(2,1)S(1)}, bf16[2,8,11136]{2,1,0:T(8,128)(2,1)S(1)}, u32[]{:S(2)}, u32[]{:S(2)}) collective-permute-start(bf16[2,8,11136]{2,1,0:T(8,128)(2,1)S(1)} %assemble.1.refs_0_), channel_id=1, source_target_pairs={{0,224},{4,228},{8,232},{12,236},{16,240},{20,244},{24,248},{28,25... | collective-permute-start | bytes 1069064 | tf_op jit(solution)/shard_map/ppermute | solution.py:433
  24.3 10.5 %collective-permute-start.7 = (bf16[2,8,11136]{2,1,0:T(8,128)(2,1)S(1)}, bf16[2,8,11136]{2,1,0:T(8,128)(2,1)S(1)}, u32[]{:S(2)}, u32[]{:S(2)}) collective-permute-start(bf16[2,8,11136]{2,1,0:T(8,128)(2,1)S(1)} %collective-permute-done.6.refs_4_.refs_7_), channel_id=1, source_target_pairs={{0,32},{4,36},{8,40},{12,44},{16,48},{20,52},{24,56},{28,60},{32,6... | collective-permute-start | bytes 1069064 | tf_op jit(solution)/shard_map/ppermute | solution.py:433
  24.3 10.5 %collective-permute-start.4 = (bf16[2,8,11136]{2,1,0:T(8,128)(2,1)S(1)}, bf16[2,8,11136]{2,1,0:T(8,128)(2,1)S(1)}, u32[]{:S(2)}, u32[]{:S(2)}) collective-permute-start(bf16[2,8,11136]{2,1,0:T(8,128)(2,1)S(1)} %collective-permute-done.3.refs_1_), channel_id=1, source_target_pairs={{0,224},{4,228},{8,232},{12,236},{16,240},{20,244},{24,248},{28,25... | collective-permute-start | bytes 1069064 | tf_op jit(solution)/shard_map/ppermute | solution.py:433
  34.8 9.6 %collective-permute-start.8 = (bf16[2,8,11136]{2,1,0:T(8,128)(2,1)S(1)}, bf16[2,8,11136]{2,1,0:T(8,128)(2,1)S(1)}, u32[]{:S(2)}, u32[]{:S(2)}) collective-permute-start(bf16[2,8,11136]{2,1,0:T(8,128)(2,1)S(1)} %collective-permute-done.7.refs_3_.refs_6_), channel_id=1, source_target_pairs={{0,32},{4,36},{8,40},{12,44},{16,48},{20,52},{24,56},{28,60},{32,6... | collective-permute-start | bytes 1069064 | tf_op jit(solution)/shard_map/ppermute | solution.py:433
  34.8 11.5 %collective-permute-start.5 = (bf16[2,8,11136]{2,1,0:T(8,128)(2,1)S(1)}, bf16[2,8,11136]{2,1,0:T(8,128)(2,1)S(1)}, u32[]{:S(2)}, u32[]{:S(2)}) collective-permute-start(bf16[2,8,11136]{2,1,0:T(8,128)(2,1)S(1)} %collective-permute-done.4.refs_2_), channel_id=1, source_target_pairs={{0,224},{4,228},{8,232},{12,236},{16,240},{20,244},{24,248},{28,25... | collective-permute-start | bytes 1069064 | tf_op jit(solution)/shard_map/ppermute | solution.py:433
  44.5 8.8 %collective-permute-start.9 = (bf16[2,8,11136]{2,1,0:T(8,128)(2,1)S(1)}, bf16[2,8,11136]{2,1,0:T(8,128)(2,1)S(1)}, u32[]{:S(2)}, u32[]{:S(2)}) collective-permute-start(bf16[2,8,11136]{2,1,0:T(8,128)(2,1)S(1)} %collective-permute-done.8.refs_2_.refs_5_), channel_id=1, source_target_pairs={{0,32},{4,36},{8,40},{12,44},{16,48},{20,52},{24,56},{28,60},{32,6... | collective-permute-start | bytes 1069064 | tf_op jit(solution)/shard_map/ppermute | solution.py:433
  44.5 18.3 %collective-permute-start.12 = (bf16[5,2,8,1920]{3,2,1,0:T(8,128)(2,1)S(1)}, bf16[5,2,8,1920]{3,2,1,0:T(8,128)(2,1)S(1)}, u32[]{:S(2)}, u32[]{:S(2)}) collective-permute-start(bf16[5,2,8,1920]{3,2,1,0:T(8,128)(2,1)S(1)} %pick.2), channel_id=1, source_target_pairs={{0,8},{4,12},{8,16},{12,20},{16,24},{20,28},{24,0},{28,4},{32,40},... | collective-permute-start | bytes 921608 | tf_op jit(solution)/shard_map/ppermute | solution.py:433
  44.6 23.0 %collective-permute-start.11 = (bf16[5,2,8,1920]{3,2,1,0:T(8,128)(2,1)S(1)}, bf16[5,2,8,1920]{3,2,1,0:T(8,128)(2,1)S(1)}, u32[]{:S(2)}, u32[]{:S(2)}) collective-permute-start(bf16[5,2,8,1920]{3,2,1,0:T(8,128)(2,1)S(1)} %pick.2), channel_id=1, source_target_pairs={{0,16},{4,20},{8,24},{12,28},{16,0},{20,4},{24,8},{28,12},{32,48},... | collective-permute-start | bytes 921608 | tf_op jit(solution)/shard_map/ppermute | solution.py:433
  46.3 21.3 %collective-permute-start.10 = (bf16[5,2,8,1920]{3,2,1,0:T(8,128)(2,1)S(1)}, bf16[5,2,8,1920]{3,2,1,0:T(8,128)(2,1)S(1)}, u32[]{:S(2)}, u32[]{:S(2)}) collective-permute-start(bf16[5,2,8,1920]{3,2,1,0:T(8,128)(2,1)S(1)} %pick.2), channel_id=1, source_target_pairs={{0,24},{4,28},{8,0},{12,4},{16,8},{20,12},{24,16},{28,20},{32,56},... | collective-permute-start | bytes 921608 | tf_op jit(solution)/shard_map/ppermute | solution.py:433
  53.3 14.4 %collective-permute-start.15 = (bf16[3,2,8,1920]{3,2,1,0:T(8,128)(2,1)S(1)}, bf16[3,2,8,1920]{3,2,1,0:T(8,128)(2,1)S(1)}, u32[]{:S(2)}, u32[]{:S(2)}) collective-permute-start(bf16[3,2,8,1920]{3,2,1,0:T(8,128)(2,1)S(1)} %pick.3), channel_id=1, source_target_pairs={{0,8},{4,12},{8,16},{12,20},{16,24},{20,28},{24,0},{28,4},{32,40},... | collective-permute-start | bytes 552968 | tf_op jit(solution)/shard_map/ppermute | solution.py:433
  53.4 14.3 %collective-permute-start.14 = (bf16[3,2,8,1920]{3,2,1,0:T(8,128)(2,1)S(1)}, bf16[3,2,8,1920]{3,2,1,0:T(8,128)(2,1)S(1)}, u32[]{:S(2)}, u32[]{:S(2)}) collective-permute-start(bf16[3,2,8,1920]{3,2,1,0:T(8,128)(2,1)S(1)} %pick.3), channel_id=1, source_target_pairs={{0,16},{4,20},{8,24},{12,28},{16,0},{20,4},{24,8},{28,12},{32,48},... | collective-permute-start | bytes 552968 | tf_op jit(solution)/shard_map/ppermute | solution.py:433
  92.3 8.3 %collective-permute-start.21 = (f16[4,2,8,2048]{3,2,1,0:T(8,128)(2,1)S(1)}, f16[4,2,8,2048]{3,2,1,0:T(8,128)(2,1)S(1)}, u32[]{:S(2)}, u32[]{:S(2)}) collective-permute-start(f16[4,2,8,2048]{3,2,1,0:T(8,128)(2,1)S(1)} %bitcast.51), channel_id=1, source_target_pairs={{0,32},{4,36},{8,40},{12,44},{16,48},{20,52},{24,56},{28,60},{32,6... | collective-permute-start | bytes 786440 | tf_op jit(solution)/shard_map/ppermute | solution.py:433
  92.8 23.4 %collective-permute-start.33 = (f16[8,2,8,2048]{3,2,1,0:T(8,128)(2,1)S(1)}, f16[8,2,8,2048]{3,2,1,0:T(8,128)(2,1)S(1)}, u32[]{:S(2)}, u32[]{:S(2)}) collective-permute-start(f16[8,2,8,2048]{3,2,1,0:T(8,128)(2,1)S(1)} %bitcast.49), channel_id=1, source_target_pairs={{0,24},{4,28},{8,0},{12,4},{16,8},{20,12},{24,16},{28,20},{32,56},... | collective-permute-start | bytes 1572872 | tf_op jit(solution)/shard_map/ppermute | solution.py:433
  94.6 24.7 %collective-permute-start.31 = (f16[8,2,8,2048]{3,2,1,0:T(8,128)(2,1)S(1)}, f16[8,2,8,2048]{3,2,1,0:T(8,128)(2,1)S(1)}, u32[]{:S(2)}, u32[]{:S(2)}) collective-permute-start(f16[8,2,8,2048]{3,2,1,0:T(8,128)(2,1)S(1)} %bitcast.48), channel_id=1, source_target_pairs={{0,8},{4,12},{8,16},{12,20},{16,24},{20,28},{24,0},{28,4},{32,40},... | collective-permute-start | bytes 1572872 | tf_op jit(solution)/shard_map/ppermute | solution.py:433
  94.9 24.5 %collective-permute-start.32 = (f16[8,2,8,2048]{3,2,1,0:T(8,128)(2,1)S(1)}, f16[8,2,8,2048]{3,2,1,0:T(8,128)(2,1)S(1)}, u32[]{:S(2)}, u32[]{:S(2)}) collective-permute-start(f16[8,2,8,2048]{3,2,1,0:T(8,128)(2,1)S(1)} %bitcast.47), channel_id=1, source_target_pairs={{0,16},{4,20},{8,24},{12,28},{16,0},{20,4},{24,8},{28,12},{32,48},... | collective-permute-start | bytes 1572872 | tf_op jit(solution)/shard_map/ppermute | solution.py:433
  100.7 7.7 %collective-permute-start.22 = (f16[4,2,8,2048]{3,2,1,0:T(8,128)(2,1)S(1)}, f16[4,2,8,2048]{3,2,1,0:T(8,128)(2,1)S(1)}, u32[]{:S(2)}, u32[]{:S(2)}) collective-permute-start(f16[4,2,8,2048]{3,2,1,0:T(8,128)(2,1)S(1)} %add_convert_fusion.5), channel_id=1, source_target_pairs={{0,32},{4,36},{8,40},{12,44},{16,48},{20,52},{24,56},{28,60},{32,6... | collective-permute-start | bytes 786440 | tf_op jit(solution)/shard_map/ppermute | solution.py:433
  103.6 7.7 %collective-permute-start.26 = (f16[4,2,8,2048]{3,2,1,0:T(8,128)(2,1)S(1)}, f16[4,2,8,2048]{3,2,1,0:T(8,128)(2,1)S(1)}, u32[]{:S(2)}, u32[]{:S(2)}) collective-permute-start(f16[4,2,8,2048]{3,2,1,0:T(8,128)(2,1)S(1)} %add_convert_fusion.2), channel_id=1, source_target_pairs={{0,224},{4,228},{8,232},{12,236},{16,240},{20,244},{24,248},{28,25... | collective-permute-start | bytes 786440 | tf_op jit(solution)/shard_map/ppermute | solution.py:433
  108.4 7.7 %collective-permute-start.23 = (f16[4,2,8,2048]{3,2,1,0:T(8,128)(2,1)S(1)}, f16[4,2,8,2048]{3,2,1,0:T(8,128)(2,1)S(1)}, u32[]{:S(2)}, u32[]{:S(2)}) collective-permute-start(f16[4,2,8,2048]{3,2,1,0:T(8,128)(2,1)S(1)} %add_convert_fusion.4), channel_id=1, source_target_pairs={{0,32},{4,36},{8,40},{12,44},{16,48},{20,52},{24,56},{28,60},{32,6... | collective-permute-start | bytes 786440 | tf_op jit(solution)/shard_map/ppermute | solution.py:433
  111.3 14.8 %collective-permute-start.27 = (f16[4,2,8,2048]{3,2,1,0:T(8,128)(2,1)S(1)}, f16[4,2,8,2048]{3,2,1,0:T(8,128)(2,1)S(1)}, u32[]{:S(2)}, u32[]{:S(2)}) collective-permute-start(f16[4,2,8,2048]{3,2,1,0:T(8,128)(2,1)S(1)} %add_convert_fusion.1), channel_id=1, source_target_pairs={{0,224},{4,228},{8,232},{12,236},{16,240},{20,244},{24,248},{28,25... | collective-permute-start | bytes 786440 | tf_op jit(solution)/shard_map/ppermute | solution.py:433
  116.1 9.9 %collective-permute-start.24 = (f16[4,2,8,2048]{3,2,1,0:T(8,128)(2,1)S(1)}, f16[4,2,8,2048]{3,2,1,0:T(8,128)(2,1)S(1)}, u32[]{:S(2)}, u32[]{:S(2)}) collective-permute-start(f16[4,2,8,2048]{3,2,1,0:T(8,128)(2,1)S(1)} %add_convert_fusion.3), channel_id=1, source_target_pairs={{0,32},{4,36},{8,40},{12,44},{16,48},{20,52},{24,56},{28,60},{32,6... | collective-permute-start | bytes 786440 | tf_op jit(solution)/shard_map/ppermute | solution.py:433
  120.5 19.7 %all-to-all-start = ((f16[8,2,8,2048]{3,2,1,0:T(8,128)(2,1)}), f16[8,2,8,2048]{3,2,1,0:T(8,128)(2,1)S(1)}, u32[]{:S(2)}, u32[]{:S(2)}) async-start(f16[8,2,8,2048]{3,2,1,0:T(8,128)(2,1)} %add_convert_fusion), calls=%async_computation | async-start | bytes 1048576 | tf_op jit(solution)/shard_map/all_to_all | solution.py:437
  (17 other events, 178.0 us)

commit v5 on v4

--- a/solution.py
+++ b/solution.py
@@ -296,12 +296,12 @@
 
 
 def partial_kernel(z_first, sig_ref, pos_ref, *refs):
-    if z_first:
-        w_ref, bound_ref, image_ref, out_ref = refs
+    if not z_first:
+        w_ref, bound_ref, image_ref, *out_refs = refs
         bound = bound_ref[4:5, 0:1]
     else:
         st_ref, *every = refs[:5]
-        image_ref, out_ref, w_ref, ev_ref = refs[5:]
+        image_ref, *out_refs, w_ref, ev_ref = refs[5:]
         for q in range(2):
             tops = [r[q : q + 1, :] for r in every]
             top = jnp.maximum(jnp.maximum(tops[0], tops[1]), jnp.maximum(tops[2], tops[3]))
@@ -333,7 +333,8 @@
             )
             for o in range(RUNS):
                 _, second, zz = entries[q][o]
-                base = (o if z_first else (o % X) * Z + zz) * 16
+                out_ref = out_refs[o // X if z_first else o % X]
+                base = (o % X if z_first else zz) * 16
                 rows = pl.ds(pl.multiple_of(base + second * 8, 8), 8)
                 block = value[o * 8 : o * 8 + 8, :]
                 if q == 0:
@@ -345,8 +346,9 @@
 
 
 def partial_sums(z_first, sig, pos, weights, images):
-    out_shape = [pltpu.VMEM((2 * COLS, PIX), jnp.float32)]
-    if not z_first:
+    many, rows = (Z, X * 16) if z_first else (X, Z * 16)
+    out_shape = [pltpu.VMEM((rows, PIX), jnp.float32)] * many
+    if z_first:
         out_shape.append(pltpu.VMEM((2, COLS, ROWS), jnp.bfloat16))
         out_shape.append(jax.ShapeDtypeStruct((1, N), jnp.float32))
     return pl.pallas_call(
@@ -391,26 +393,26 @@
     if len(refs) == 1:
         refs[0][...] = slab
     else:
-        im_ref, out_ref = refs
+        re_ref, out_ref = refs
         for h in range(HIGH):
             at = slice(h * LOW, (h + 1) * LOW)
-            out_ref[0:1, at] = slab[h : h + 1, :]
-            out_ref[1:2, at] = im_ref[h : h + 1, :]
-
-
-def insert(bound, weighted, insertion, *im):
-    shape = (2, VOX) if im else (HIGH, LOW)
+            out_ref[0:1, at] = re_ref[h : h + 1, :]
+            out_ref[1:2, at] = slab[h : h + 1, :]
+
+
+def insert(bound, weighted, insertion, *re):
+    shape = (2, VOX) if re else (HIGH, LOW)
     return pl.pallas_call(
         insert_kernel,
-        in_specs=[VMEM] * (3 + len(im)),
+        in_specs=[VMEM] * (3 + len(re)),
         out_specs=VMEM,
         out_shape=jax.ShapeDtypeStruct(shape, jnp.float32),
         compiler_params=limit(8),
         cost_estimate=pl.CostEstimate(
             flops=4 * HIGH * LOW * 16 * PIX, bytes_accessed=512 * 1024, transcendentals=0
         ),
-        name="insert_re" if im else "insert_im",
-    )(bound, weighted.reshape(16, PIX), insertion, *im)
+        name="insert_im" if re else "insert_re",
+    )(bound, weighted.reshape(16, PIX), insertion, *re)
 
 
 def img_index(z, x, c):
@@ -514,13 +516,13 @@
     scores, stats = score_rest(sig, pos, messages, batches, shifted, acc)
     merged = merge(stats, send(stats, dc=1))
     every = exchange_refs(merged)
-    sums_im, weights, evidence = partial_sums(False, sig, pos, (scores, *every), shifted[1])
-    (sums_re,) = partial_sums(True, sig, pos, (weights, merged), shifted[0])
-    total_im = scatter_x_first(sums_im.reshape(X, Z, 2, 8, PIX))
-    total_re = scatter_z_first(sums_re.reshape(Z, X, 2, 8, PIX))
+    *sums_re, weights, evidence = partial_sums(True, sig, pos, (scores, *every), shifted[0])
+    sums_im = partial_sums(False, sig, pos, (weights, merged), shifted[1])
+    total_re = scatter_z_first([v.reshape(X, 2, 8, PIX) for v in sums_re])
+    total_im = scatter_x_first([v.reshape(Z, 2, 8, PIX) for v in sums_im])
     ids = insertion.reshape(16, PIX)
-    slab = insert(merged, total_im, ids)
-    volume = insert(merged, total_re, ids, slab)
+    slab = insert(merged, total_re, ids)
+    volume = insert(merged, total_im, ids, slab)
     return volume, evidence.reshape(N)
 
 

time: 151 us -> 151 us (level)
  waiting for transfers between devices: 54.4 us -> 56.6 us
  starting transfers between devices: 53.1 us -> 51.2 us
    ppermute x31, waiting for transfers between devices: 47.8 us -> 52.1 us  [send(): return lax.ppermute(value, 'img', pairs(dz, dx, dc))]
    all_to_all x1, waiting for transfers between devices: 4.84 us -> 2.8 us  [all_to_all_z(): lax.all_to_all(value, 'img', split_axis=0, concat_axis=0, tiled=True, axi...]
  transfers between devices with their start and end apart: 35 -> 35, of which waited for: 19 -> 16; matrix products, arithmetic and copies ran while one was open for 2% -> 2% of each run, Pallas kernels for 7% -> 14%
where the time goes in v5:
time: 151 us; the launch traced here: 148 us
  waiting for transfers between devices  56.6 us (37%)
  starting transfers between devices  51.2 us (34%)
  Pallas kernels  34.1 us (23%)
  local copies, waits for them, and re-layouts  3.45 us (2%)
  other arithmetic  2.09 us (1%)
    ppermute x31, waiting for transfers between devices, send(): return lax.ppermute(value, 'img', pairs(dz, dx, dc))  52.1 us
    ppermute x31, starting transfers between devices, send(): return lax.ppermute(value, 'img', pairs(dz, dx, dc))  41.3 us
    pallas_call x2, Pallas kernels, insert(): pl.pallas_call(insert_kernel, in_specs=[VMEM] * (3 + len(re)), out_specs=...  9.72 us
    pallas_call x2, Pallas kernels, partial_sums(): pl.pallas_call(lambda *refs: partial_kernel(z_first, *refs), in_specs=[SM...  9.52 us
    pallas_call x1, Pallas kernels, shifted_images(): pl.pallas_call(shift_kernel, in_specs=[VMEM] * 3, out_specs=[VMEM, VMEM],...  5.49 us
    all_to_all x1, starting transfers between devices, all_to_all_z(): lax.all_to_all(value, 'img', split_axis=0, concat_axis=0, tiled=True, axi...  4.97 us
    ppermute x3, starting transfers between devices, exchange_refs(): lax.ppermute(value, 'ref', [(r, (r + k) % REFS) for r in range(REFS)])  4.94 us
    pallas_call x1, Pallas kernels, score_rest(): pl.pallas_call(score_rest_kernel, in_specs=[SMEM, SMEM] + [VMEM] * (Z + 8...  4.56 us
  transfers between devices with their start and end apart: 35, of which 16 were waited for; matrix products, arithmetic and copies ran while one was open for 2% of the time, Pallas kernels for 14%

profile of v5, /device:TPU:8, one launch (start us, length us, event | category | flops | bytes accessed | tf_op | source)
XLA Modules:
  0.0 148.5 jit_solution(7132050166664496580)
XLA Ops:
  12.2 4.0 %collective-permute-start.3 = (bf16[2,8,11136]{2,1,0:T(8,128)(2,1)S(1)}, bf16[2,8,11136]{2,1,0:T(8,128)(2,1)S(1)}, u32[]{:S(2)}, u32[]{:S(2)}) collective-permute-start(bf16[2,8,11136]{2,1,0:T(8,128)(2,1)S(1)} %assemble.1.refs_0_), channel_id=1, source_target_pairs={{0,224},{4,228},{8,232},{12,236},{16,240},{20,244},{24,248},{28,25... | collective-permute-start | bytes 1069064 | tf_op jit(solution)/shard_map/ppermute | solution.py:435
  16.3 8.0 %collective-permute-done.6.refs_4_.refs_7_ = bf16[2,8,11136]{2,1,0:T(8,128)(2,1)S(1)} collective-permute-done((bf16[2,8,11136]{2,1,0:T(8,128)(2,1)S(1)}, bf16[2,8,11136]{2,1,0:T(8,128)(2,1)S(1)}, u32[]{:S(2)}, u32[]{:S(2)}) %collective-permute-start.6) | collective-permute-done | bytes 356384 | tf_op jit(solution)/shard_map/ppermute | solution.py:435
  24.3 3.2 %collective-permute-start.4 = (bf16[2,8,11136]{2,1,0:T(8,128)(2,1)S(1)}, bf16[2,8,11136]{2,1,0:T(8,128)(2,1)S(1)}, u32[]{:S(2)}, u32[]{:S(2)}) collective-permute-start(bf16[2,8,11136]{2,1,0:T(8,128)(2,1)S(1)} %collective-permute-done.3.refs_1_), channel_id=1, source_target_pairs={{0,224},{4,228},{8,232},{12,236},{16,240},{20,244},{24,248},{28,25... | collective-permute-start | bytes 1069064 | tf_op jit(solution)/shard_map/ppermute | solution.py:435
  27.5 7.3 %collective-permute-done.7.refs_3_.refs_6_ = bf16[2,8,11136]{2,1,0:T(8,128)(2,1)S(1)} collective-permute-done((bf16[2,8,11136]{2,1,0:T(8,128)(2,1)S(1)}, bf16[2,8,11136]{2,1,0:T(8,128)(2,1)S(1)}, u32[]{:S(2)}, u32[]{:S(2)}) %collective-permute-start.7) | collective-permute-done | bytes 356384 | tf_op jit(solution)/shard_map/ppermute | solution.py:435
  34.8 3.2 %collective-permute-start.5 = (bf16[2,8,11136]{2,1,0:T(8,128)(2,1)S(1)}, bf16[2,8,11136]{2,1,0:T(8,128)(2,1)S(1)}, u32[]{:S(2)}, u32[]{:S(2)}) collective-permute-start(bf16[2,8,11136]{2,1,0:T(8,128)(2,1)S(1)} %collective-permute-done.4.refs_2_), channel_id=1, source_target_pairs={{0,224},{4,228},{8,232},{12,236},{16,240},{20,244},{24,248},{28,25... | collective-permute-start | bytes 1069064 | tf_op jit(solution)/shard_map/ppermute | solution.py:435
  38.0 6.4 %collective-permute-done.8.refs_2_.refs_5_ = bf16[2,8,11136]{2,1,0:T(8,128)(2,1)S(1)} collective-permute-done((bf16[2,8,11136]{2,1,0:T(8,128)(2,1)S(1)}, bf16[2,8,11136]{2,1,0:T(8,128)(2,1)S(1)}, u32[]{:S(2)}, u32[]{:S(2)}) %collective-permute-start.8) | collective-permute-done | bytes 356384 | tf_op jit(solution)/shard_map/ppermute | solution.py:435
  48.8 4.4 %collective-permute-done.9.refs_1_.refs_4_ = bf16[2,8,11136]{2,1,0:T(8,128)(2,1)S(1)} collective-permute-done((bf16[2,8,11136]{2,1,0:T(8,128)(2,1)S(1)}, bf16[2,8,11136]{2,1,0:T(8,128)(2,1)S(1)}, u32[]{:S(2)}, u32[]{:S(2)}) %collective-permute-start.9) | collective-permute-done | bytes 356384 | tf_op jit(solution)/shard_map/ppermute | solution.py:435
  54.9 5.5 %shift.1 = (bf16[2,5,256,2048]{3,2,1,0:T(8,128)(2,1)S(1)}, bf16[2,5,256,2048]{3,2,1,0:T(8,128)(2,1)S(1)}) custom-call(f32[8,2048]{1,0:T(8,128)S(1)} %copy-done.4, bf16[256,4096]{1,0:T(8,128)(2,1)S(1)} %copy-done.2, bf16[256,4096]{1,0:T(8,128)(2,1)} %collective-permute-done.16.mate_ref), custom_call_target="tpu_custom_call" | custom-call | flops 25165824 | bytes 25165824 | tf_op jit(solution)/shard_map/shift/pallas_call | solution.py:138
  63.2 4.4 %score_first.1.refs_15_ = f32[2,1280,256]{2,1,0:T(8,128)S(1)} custom-call(s32[2,512]{1,0:T(2,128)S(1)} %constant_dynamic-slice_fusion.sig_ref.refs_0_, s32[4]{0:T(128)S(1)} %pad_add_fusion.pos_ref.refs_1_, bf16[2,8,11136]{2,1,0:T(8,128)(2,1)S(1)} %assemble.1.refs_0_, bf16[2,8,11136]{2,1,0:T(8,128)(2,1)S(1)} %collective-permute-done.3.refs_1_, ...), custom_call_target="tpu_custom_call" | custom-call | flops 3019898880 | bytes 16777216 | tf_op jit(solution)/shard_map/score_first/pallas_call | solution.py:186
  68.3 4.6 %score_rest.1 = (f32[2,256,1280]{2,1,0:T(8,128)S(1)}, f32[8,256]{1,0:T(8,128)S(1)}) custom-call(s32[2,512]{1,0:T(2,128)S(1)} %constant_dynamic-slice_fusion.sig_ref.refs_0_, s32[4]{0:T(128)S(1)} %pad_add_fusion.pos_ref.refs_1_, bf16[2,8,11136]{2,1,0:T(8,128)(2,1)S(1)} %assemble.1.refs_0_, bf16[2,8,11136]{2,1,0:T(8,128)(2,1)S(1)} %collective-permute-done.3.refs_1_, ...), custom_call_target="tpu_custom_call" | custom-call | flops 2348810240 | bytes 16777216 | tf_op jit(solution)/shard_map/score_rest/pallas_call | solution.py:249
  81.0 5.2 %partial_re.1 = (f32[64,2048]{1,0:T(8,128)S(1)}, f32[64,2048]{1,0:T(8,128)S(1)}, f32[64,2048]{1,0:T(8,128)S(1)}, f32[64,2048]{1,0:T(8,128)S(1)}, f32[64,2048]{1,...) custom-call(s32[2,512]{1,0:T(2,128)S(1)} %constant_dynamic-slice_fus, ...), custom_call_target="tpu_custom_call" | custom-call | flops 2684354560 | bytes 16777216 | tf_op jit(solution)/shard_map/partial_re/pallas_call | solution.py:354
  86.3 3.3 %collective-permute-start.28 = (f16[4,2,8,2048]{3,2,1,0:T(8,128)(2,1)S(1)}, f16[4,2,8,2048]{3,2,1,0:T(8,128)(2,1)S(1)}, u32[]{:S(2)}, u32[]{:S(2)}) collective-permute-start(f16[4,2,8,2048]{3,2,1,0:T(8,128)(2,1)S(1)} %bitcast.50), channel_id=1, source_target_pairs={{0,224},{4,228},{8,232},{12,236},{16,240},{20,244},{24,248},{28,25... | collective-permute-start | bytes 786440 | tf_op jit(solution)/shard_map/ppermute | solution.py:435
  89.6 4.3 %partial_im.1 = (f32[128,2048]{1,0:T(8,128)S(1)}, f32[128,2048]{1,0:T(8,128)S(1)}, f32[128,2048]{1,0:T(8,128)S(1)}, f32[128,2048]{1,0:T(8,128)S(1)}) custom-call(s32[2,512]{1,0:T(2,128)S(1)} %constant_dynamic-slice_fusion.sig_ref.refs_0_, s32[4]{0:T(128)S(1)} %pad_add_fusion.pos_ref.refs_1_, bf16[2,256,1280]{2,1,0:T(8,128)(2,1)S(1)} %get-tuple-element.30.refs_2_, ...), custom_call_target="tpu_custom_call" | custom-call | flops 2684354560 | bytes 16777216 | tf_op jit(solution)/shard_map/partial_im/pallas_call | solution.py:354
  97.5 3.3 %collective-permute-start.29 = (f16[4,2,8,2048]{3,2,1,0:T(8,128)(2,1)S(1)}, f16[4,2,8,2048]{3,2,1,0:T(8,128)(2,1)S(1)}, u32[]{:S(2)}, u32[]{:S(2)}) collective-permute-start(f16[4,2,8,2048]{3,2,1,0:T(8,128)(2,1)S(1)} %add_convert_fusion.2), channel_id=1, source_target_pairs={{0,224},{4,228},{8,232},{12,236},{16,240},{20,244},{24,248},{28,25... | collective-permute-start | bytes 786440 | tf_op jit(solution)/shard_map/ppermute | solution.py:435
  100.8 4.2 %collective-permute-done.25 = f16[4,2,8,2048]{3,2,1,0:T(8,128)(2,1)S(1)} collective-permute-done((f16[4,2,8,2048]{3,2,1,0:T(8,128)(2,1)S(1)}, f16[4,2,8,2048]{3,2,1,0:T(8,128)(2,1)S(1)}, u32[]{:S(2)}, u32[]{:S(2)}) %collective-permute-start.25) | collective-permute-done | bytes 262176 | tf_op jit(solution)/shard_map/ppermute | solution.py:435
  105.3 3.3 %collective-permute-start.30 = (f16[4,2,8,2048]{3,2,1,0:T(8,128)(2,1)S(1)}, f16[4,2,8,2048]{3,2,1,0:T(8,128)(2,1)S(1)}, u32[]{:S(2)}, u32[]{:S(2)}) collective-permute-start(f16[4,2,8,2048]{3,2,1,0:T(8,128)(2,1)S(1)} %add_convert_fusion.1), channel_id=1, source_target_pairs={{0,224},{4,228},{8,232},{12,236},{16,240},{20,244},{24,248},{28,25... | collective-permute-start | bytes 786440 | tf_op jit(solution)/shard_map/ppermute | solution.py:435
  108.6 4.3 %collective-permute-done.26 = f16[4,2,8,2048]{3,2,1,0:T(8,128)(2,1)S(1)} collective-permute-done((f16[4,2,8,2048]{3,2,1,0:T(8,128)(2,1)S(1)}, f16[4,2,8,2048]{3,2,1,0:T(8,128)(2,1)S(1)}, u32[]{:S(2)}, u32[]{:S(2)}) %collective-permute-start.26) | collective-permute-done | bytes 262176 | tf_op jit(solution)/shard_map/ppermute | solution.py:435
  113.0 7.4 %collective-permute-done.21 = f16[8,2,8,2048]{3,2,1,0:T(8,128)(2,1)S(1)} collective-permute-done((f16[8,2,8,2048]{3,2,1,0:T(8,128)(2,1)S(1)}, f16[8,2,8,2048]{3,2,1,0:T(8,128)(2,1)S(1)}, u32[]{:S(2)}, u32[]{:S(2)}) %collective-permute-start.21) | collective-permute-done | bytes 524320 | tf_op jit(solution)/shard_map/ppermute | solution.py:435
  121.6 5.0 %all-to-all-start = ((f16[8,2,8,2048]{3,2,1,0:T(8,128)(2,1)}), f16[8,2,8,2048]{3,2,1,0:T(8,128)(2,1)S(1)}, u32[]{:S(2)}, u32[]{:S(2)}) async-start(f16[8,2,8,2048]{3,2,1,0:T(8,128)(2,1)} %add_convert_fusion), calls=%async_computation | async-start | bytes 1048576 | tf_op jit(solution)/shard_map/all_to_all | solution.py:439
  126.9 3.2 %collective-permute-start.33 = (f16[2,8,2048]{2,1,0:T(8,128)(2,1)S(1)}, f16[2,8,2048]{2,1,0:T(8,128)(2,1)S(1)}, u32[]{:S(2)}, u32[]{:S(2)}) collective-permute-start(f16[2,8,2048]{2,1,0:T(8,128)(2,1)S(1)} %get-tuple-element.47), channel_id=1, source_target_pairs={{0,24},{4,28},{8,0},{12,4},{16,8},{20,12},{24,16},{28,20},{32,56},... | collective-permute-start | bytes 196616 | tf_op jit(solution)/shard_map/ppermute | solution.py:435
  132.6 3.3 %collective-permute-done.32 = f16[2,8,2048]{2,1,0:T(8,128)(2,1)S(1)} collective-permute-done((f16[2,8,2048]{2,1,0:T(8,128)(2,1)S(1)}, f16[2,8,2048]{2,1,0:T(8,128)(2,1)S(1)}, u32[]{:S(2)}, u32[]{:S(2)}) %collective-permute-start.32) | collective-permute-done | bytes 65568 | tf_op jit(solution)/shard_map/ppermute | solution.py:435
  135.9 5.6 %insert_re.1.refs_0_ = f32[32,128]{1,0:T(8,128)S(1)} custom-call(f32[8,256]{1,0:T(8,128)S(1)} %merge.1.refs_3_.bound_ref, f32[16,2048]{1,0:T(8,128)S(1)} %fusion.3.w_ref, s32[16,2048]{1,0:T(8,128)S(1)} %bitcast.45), custom_call_target="tpu_custom_call" | custom-call | flops 536870912 | bytes 524288 | tf_op jit(solution)/shard_map/insert_re/pallas_call | solution.py:405
  141.5 2.8 %all-to-all-done = f16[8,2,8,2048]{3,2,1,0:T(8,128)(2,1)S(1)} async-done(((f16[8,2,8,2048]{3,2,1,0:T(8,128)(2,1)}), f16[8,2,8,2048]{3,2,1,0:T(8,128)(2,1)S(1)}, u32[]{:S(2)}, u32[]{:S(2)}) %all-to-all-start) | async-done | bytes 524320 | tf_op jit(solution)/shard_map/all_to_all | solution.py:439
  144.3 4.2 %insert_im.1 = f32[2,4096]{1,0:T(2,128)} custom-call(f32[8,256]{1,0:T(8,128)S(1)} %merge.1.refs_3_.bound_ref, f32[16,2048]{1,0:T(8,128)S(1)} %bitcast.44, s32[16,2048]{1,0:T(8,128)S(1)} %bitcast.46, f32[32,128]{1,0:T(8,128)S(1)} %insert_re.1.refs_0_), custom_call_target="tpu_custom_call" | custom-call | flops 536870912 | bytes 524288 | tf_op jit(solution)/shard_map/insert_im/pallas_call | solution.py:405
  (88 shorter events, 37.2 us)
Async XLA Ops:
  0.6 52.7 %collective-permute-start.16 = (bf16[256,4096]{1,0:T(8,128)(2,1)}, bf16[256,4096]{1,0:T(8,128)(2,1)}, u32[]{:S(2)}, u32[]{:S(2)}) collective-permute-start(bf16[256,4096]{1,0:T(8,128)(2,1)} %own_ref.1), channel_id=1, source_target_pairs={{0,4},{4,0},{8,12},{12,8},{16,20},{20,16},{24,28},{28,24},{32,36},... | collective-permute-start | bytes 6291464 | tf_op jit(solution)/shard_map/ppermute | solution.py:435
  1.6 8.5 %collective-permute-start.2 = (bf16[2,8,2304]{2,1,0:T(8,128)(2,1)S(1)}, bf16[2,8,2304]{2,1,0:T(8,128)(2,1)S(1)}, u32[]{:S(2)}, u32[]{:S(2)}) collective-permute-start(bf16[2,8,2304]{2,1,0:T(8,128)(2,1)S(1)} %slice.18.refs_0_), channel_id=1, source_target_pairs={{0,8},{4,12},{8,16},{12,20},{16,24},{20,28},{24,0},{28,4},{32,40},... | collective-permute-start | bytes 221192 | tf_op jit(solution)/shard_map/ppermute | solution.py:435
  10.2 14.1 %collective-permute-start.6 = (bf16[2,8,11136]{2,1,0:T(8,128)(2,1)S(1)}, bf16[2,8,11136]{2,1,0:T(8,128)(2,1)S(1)}, u32[]{:S(2)}, u32[]{:S(2)}) collective-permute-start(bf16[2,8,11136]{2,1,0:T(8,128)(2,1)S(1)} %assemble.1.refs_0_), channel_id=1, source_target_pairs={{0,32},{4,36},{8,40},{12,44},{16,48},{20,52},{24,56},{28,60},{32,6... | collective-permute-start | bytes 1069064 | tf_op jit(solution)/shard_map/ppermute | solution.py:435
  12.2 12.1 %collective-permute-start.3 = (bf16[2,8,11136]{2,1,0:T(8,128)(2,1)S(1)}, bf16[2,8,11136]{2,1,0:T(8,128)(2,1)S(1)}, u32[]{:S(2)}, u32[]{:S(2)}) collective-permute-start(bf16[2,8,11136]{2,1,0:T(8,128)(2,1)S(1)} %assemble.1.refs_0_), channel_id=1, source_target_pairs={{0,224},{4,228},{8,232},{12,236},{16,240},{20,244},{24,248},{28,25... | collective-permute-start | bytes 1069064 | tf_op jit(solution)/shard_map/ppermute | solution.py:435
  24.3 10.5 %collective-permute-start.7 = (bf16[2,8,11136]{2,1,0:T(8,128)(2,1)S(1)}, bf16[2,8,11136]{2,1,0:T(8,128)(2,1)S(1)}, u32[]{:S(2)}, u32[]{:S(2)}) collective-permute-start(bf16[2,8,11136]{2,1,0:T(8,128)(2,1)S(1)} %collective-permute-done.6.refs_4_.refs_7_), channel_id=1, source_target_pairs={{0,32},{4,36},{8,40},{12,44},{16,48},{20,52},{24,56},{28,60},{32,6... | collective-permute-start | bytes 1069064 | tf_op jit(solution)/shard_map/ppermute | solution.py:435
  24.3 10.5 %collective-permute-start.4 = (bf16[2,8,11136]{2,1,0:T(8,128)(2,1)S(1)}, bf16[2,8,11136]{2,1,0:T(8,128)(2,1)S(1)}, u32[]{:S(2)}, u32[]{:S(2)}) collective-permute-start(bf16[2,8,11136]{2,1,0:T(8,128)(2,1)S(1)} %collective-permute-done.3.refs_1_), channel_id=1, source_target_pairs={{0,224},{4,228},{8,232},{12,236},{16,240},{20,244},{24,248},{28,25... | collective-permute-start | bytes 1069064 | tf_op jit(solution)/shard_map/ppermute | solution.py:435
  34.8 9.6 %collective-permute-start.8 = (bf16[2,8,11136]{2,1,0:T(8,128)(2,1)S(1)}, bf16[2,8,11136]{2,1,0:T(8,128)(2,1)S(1)}, u32[]{:S(2)}, u32[]{:S(2)}) collective-permute-start(bf16[2,8,11136]{2,1,0:T(8,128)(2,1)S(1)} %collective-permute-done.7.refs_3_.refs_6_), channel_id=1, source_target_pairs={{0,32},{4,36},{8,40},{12,44},{16,48},{20,52},{24,56},{28,60},{32,6... | collective-permute-start | bytes 1069064 | tf_op jit(solution)/shard_map/ppermute | solution.py:435
  34.8 11.5 %collective-permute-start.5 = (bf16[2,8,11136]{2,1,0:T(8,128)(2,1)S(1)}, bf16[2,8,11136]{2,1,0:T(8,128)(2,1)S(1)}, u32[]{:S(2)}, u32[]{:S(2)}) collective-permute-start(bf16[2,8,11136]{2,1,0:T(8,128)(2,1)S(1)} %collective-permute-done.4.refs_2_), channel_id=1, source_target_pairs={{0,224},{4,228},{8,232},{12,236},{16,240},{20,244},{24,248},{28,25... | collective-permute-start | bytes 1069064 | tf_op jit(solution)/shard_map/ppermute | solution.py:435
  44.5 8.8 %collective-permute-start.9 = (bf16[2,8,11136]{2,1,0:T(8,128)(2,1)S(1)}, bf16[2,8,11136]{2,1,0:T(8,128)(2,1)S(1)}, u32[]{:S(2)}, u32[]{:S(2)}) collective-permute-start(bf16[2,8,11136]{2,1,0:T(8,128)(2,1)S(1)} %collective-permute-done.8.refs_2_.refs_5_), channel_id=1, source_target_pairs={{0,32},{4,36},{8,40},{12,44},{16,48},{20,52},{24,56},{28,60},{32,6... | collective-permute-start | bytes 1069064 | tf_op jit(solution)/shard_map/ppermute | solution.py:435
  44.5 18.3 %collective-permute-start.12 = (bf16[5,2,8,1920]{3,2,1,0:T(8,128)(2,1)S(1)}, bf16[5,2,8,1920]{3,2,1,0:T(8,128)(2,1)S(1)}, u32[]{:S(2)}, u32[]{:S(2)}) collective-permute-start(bf16[5,2,8,1920]{3,2,1,0:T(8,128)(2,1)S(1)} %pick.2), channel_id=1, source_target_pairs={{0,8},{4,12},{8,16},{12,20},{16,24},{20,28},{24,0},{28,4},{32,40},... | collective-permute-start | bytes 921608 | tf_op jit(solution)/shard_map/ppermute | solution.py:435
  44.6 23.0 %collective-permute-start.11 = (bf16[5,2,8,1920]{3,2,1,0:T(8,128)(2,1)S(1)}, bf16[5,2,8,1920]{3,2,1,0:T(8,128)(2,1)S(1)}, u32[]{:S(2)}, u32[]{:S(2)}) collective-permute-start(bf16[5,2,8,1920]{3,2,1,0:T(8,128)(2,1)S(1)} %pick.2), channel_id=1, source_target_pairs={{0,16},{4,20},{8,24},{12,28},{16,0},{20,4},{24,8},{28,12},{32,48},... | collective-permute-start | bytes 921608 | tf_op jit(solution)/shard_map/ppermute | solution.py:435
  46.3 21.3 %collective-permute-start.10 = (bf16[5,2,8,1920]{3,2,1,0:T(8,128)(2,1)S(1)}, bf16[5,2,8,1920]{3,2,1,0:T(8,128)(2,1)S(1)}, u32[]{:S(2)}, u32[]{:S(2)}) collective-permute-start(bf16[5,2,8,1920]{3,2,1,0:T(8,128)(2,1)S(1)} %pick.2), channel_id=1, source_target_pairs={{0,24},{4,28},{8,0},{12,4},{16,8},{20,12},{24,16},{28,20},{32,56},... | collective-permute-start | bytes 921608 | tf_op jit(solution)/shard_map/ppermute | solution.py:435
  53.3 14.4 %collective-permute-start.15 = (bf16[3,2,8,1920]{3,2,1,0:T(8,128)(2,1)S(1)}, bf16[3,2,8,1920]{3,2,1,0:T(8,128)(2,1)S(1)}, u32[]{:S(2)}, u32[]{:S(2)}) collective-permute-start(bf16[3,2,8,1920]{3,2,1,0:T(8,128)(2,1)S(1)} %pick.3), channel_id=1, source_target_pairs={{0,8},{4,12},{8,16},{12,20},{16,24},{20,28},{24,0},{28,4},{32,40},... | collective-permute-start | bytes 552968 | tf_op jit(solution)/shard_map/ppermute | solution.py:435
  53.4 14.3 %collective-permute-start.14 = (bf16[3,2,8,1920]{3,2,1,0:T(8,128)(2,1)S(1)}, bf16[3,2,8,1920]{3,2,1,0:T(8,128)(2,1)S(1)}, u32[]{:S(2)}, u32[]{:S(2)}) collective-permute-start(bf16[3,2,8,1920]{3,2,1,0:T(8,128)(2,1)S(1)} %pick.3), channel_id=1, source_target_pairs={{0,16},{4,20},{8,24},{12,28},{16,0},{20,4},{24,8},{28,12},{32,48},... | collective-permute-start | bytes 552968 | tf_op jit(solution)/shard_map/ppermute | solution.py:435
  86.2 11.1 %collective-permute-start.24 = (f16[4,2,8,2048]{3,2,1,0:T(8,128)(2,1)S(1)}, f16[4,2,8,2048]{3,2,1,0:T(8,128)(2,1)S(1)}, u32[]{:S(2)}, u32[]{:S(2)}) collective-permute-start(f16[4,2,8,2048]{3,2,1,0:T(8,128)(2,1)S(1)} %bitcast.51), channel_id=1, source_target_pairs={{0,32},{4,36},{8,40},{12,44},{16,48},{20,52},{24,56},{28,60},{32,6... | collective-permute-start | bytes 786440 | tf_op jit(solution)/shard_map/ppermute | solution.py:435
  86.3 11.1 %collective-permute-start.28 = (f16[4,2,8,2048]{3,2,1,0:T(8,128)(2,1)S(1)}, f16[4,2,8,2048]{3,2,1,0:T(8,128)(2,1)S(1)}, u32[]{:S(2)}, u32[]{:S(2)}) collective-permute-start(f16[4,2,8,2048]{3,2,1,0:T(8,128)(2,1)S(1)} %bitcast.50), channel_id=1, source_target_pairs={{0,224},{4,228},{8,232},{12,236},{16,240},{20,244},{24,248},{28,25... | collective-permute-start | bytes 786440 | tf_op jit(solution)/shard_map/ppermute | solution.py:435
  94.1 18.9 %collective-permute-start.23 = (f16[8,2,8,2048]{3,2,1,0:T(8,128)(2,1)S(1)}, f16[8,2,8,2048]{3,2,1,0:T(8,128)(2,1)S(1)}, u32[]{:S(2)}, u32[]{:S(2)}) collective-permute-start(f16[8,2,8,2048]{3,2,1,0:T(8,128)(2,1)S(1)} %bitcast.49), channel_id=1, source_target_pairs={{0,24},{4,28},{8,0},{12,4},{16,8},{20,12},{24,16},{28,20},{32,56},... | collective-permute-start | bytes 1572872 | tf_op jit(solution)/shard_map/ppermute | solution.py:435
  96.0 17.1 %collective-permute-start.22 = (f16[8,2,8,2048]{3,2,1,0:T(8,128)(2,1)S(1)}, f16[8,2,8,2048]{3,2,1,0:T(8,128)(2,1)S(1)}, u32[]{:S(2)}, u32[]{:S(2)}) collective-permute-start(f16[8,2,8,2048]{3,2,1,0:T(8,128)(2,1)S(1)} %bitcast.48), channel_id=1, source_target_pairs={{0,16},{4,20},{8,24},{12,28},{16,0},{20,4},{24,8},{28,12},{32,48},... | collective-permute-start | bytes 1572872 | tf_op jit(solution)/shard_map/ppermute | solution.py:435
  97.3 23.2 %collective-permute-start.21 = (f16[8,2,8,2048]{3,2,1,0:T(8,128)(2,1)S(1)}, f16[8,2,8,2048]{3,2,1,0:T(8,128)(2,1)S(1)}, u32[]{:S(2)}, u32[]{:S(2)}) collective-permute-start(f16[8,2,8,2048]{3,2,1,0:T(8,128)(2,1)S(1)} %bitcast.47), channel_id=1, source_target_pairs={{0,8},{4,12},{8,16},{12,20},{16,24},{20,28},{24,0},{28,4},{32,40},... | collective-permute-start | bytes 1572872 | tf_op jit(solution)/shard_map/ppermute | solution.py:435
  97.3 7.7 %collective-permute-start.25 = (f16[4,2,8,2048]{3,2,1,0:T(8,128)(2,1)S(1)}, f16[4,2,8,2048]{3,2,1,0:T(8,128)(2,1)S(1)}, u32[]{:S(2)}, u32[]{:S(2)}) collective-permute-start(f16[4,2,8,2048]{3,2,1,0:T(8,128)(2,1)S(1)} %add_convert_fusion.5), channel_id=1, source_target_pairs={{0,32},{4,36},{8,40},{12,44},{16,48},{20,52},{24,56},{28,60},{32,6... | collective-permute-start | bytes 786440 | tf_op jit(solution)/shard_map/ppermute | solution.py:435
  105.1 7.7 %collective-permute-start.26 = (f16[4,2,8,2048]{3,2,1,0:T(8,128)(2,1)S(1)}, f16[4,2,8,2048]{3,2,1,0:T(8,128)(2,1)S(1)}, u32[]{:S(2)}, u32[]{:S(2)}) collective-permute-start(f16[4,2,8,2048]{3,2,1,0:T(8,128)(2,1)S(1)} %add_convert_fusion.4), channel_id=1, source_target_pairs={{0,32},{4,36},{8,40},{12,44},{16,48},{20,52},{24,56},{28,60},{32,6... | collective-permute-start | bytes 786440 | tf_op jit(solution)/shard_map/ppermute | solution.py:435
  105.3 21.3 %collective-permute-start.30 = (f16[4,2,8,2048]{3,2,1,0:T(8,128)(2,1)S(1)}, f16[4,2,8,2048]{3,2,1,0:T(8,128)(2,1)S(1)}, u32[]{:S(2)}, u32[]{:S(2)}) collective-permute-start(f16[4,2,8,2048]{3,2,1,0:T(8,128)(2,1)S(1)} %add_convert_fusion.1), channel_id=1, source_target_pairs={{0,224},{4,228},{8,232},{12,236},{16,240},{20,244},{24,248},{28,25... | collective-permute-start | bytes 786440 | tf_op jit(solution)/shard_map/ppermute | solution.py:435
  112.9 13.7 %collective-permute-start.27 = (f16[4,2,8,2048]{3,2,1,0:T(8,128)(2,1)S(1)}, f16[4,2,8,2048]{3,2,1,0:T(8,128)(2,1)S(1)}, u32[]{:S(2)}, u32[]{:S(2)}) collective-permute-start(f16[4,2,8,2048]{3,2,1,0:T(8,128)(2,1)S(1)} %add_convert_fusion.3), channel_id=1, source_target_pairs={{0,32},{4,36},{8,40},{12,44},{16,48},{20,52},{24,56},{28,60},{32,6... | collective-permute-start | bytes 786440 | tf_op jit(solution)/shard_map/ppermute | solution.py:435
  121.6 22.6 %all-to-all-start = ((f16[8,2,8,2048]{3,2,1,0:T(8,128)(2,1)}), f16[8,2,8,2048]{3,2,1,0:T(8,128)(2,1)S(1)}, u32[]{:S(2)}, u32[]{:S(2)}) async-start(f16[8,2,8,2048]{3,2,1,0:T(8,128)(2,1)} %add_convert_fusion), calls=%async_computation | async-start | bytes 1048576 | tf_op jit(solution)/shard_map/all_to_all | solution.py:439
  (17 other events, 173.1 us)

commit v6 on v5

--- a/solution.py
+++ b/solution.py
@@ -297,11 +297,11 @@
 
 def partial_kernel(z_first, sig_ref, pos_ref, *refs):
     if not z_first:
-        w_ref, bound_ref, image_ref, *out_refs = refs
+        w_ref, bound_ref, im_ref, *out_refs = refs
         bound = bound_ref[4:5, 0:1]
     else:
         st_ref, *every = refs[:5]
-        image_ref, *out_refs, w_ref, ev_ref = refs[5:]
+        re_ref, im_ref, *out_refs, w_ref, ev_ref = refs[5:]
         for q in range(2):
             tops = [r[q : q + 1, :] for r in every]
             top = jnp.maximum(jnp.maximum(tops[0], tops[1]), jnp.maximum(tops[2], tops[3]))
@@ -319,14 +319,14 @@
         for q in range(2)
     ]
 
-    @pl.loop(0, PIX // PTILE)
-    def _(i):
-        at = pl.ds(pl.multiple_of(i * PTILE, PTILE), PTILE)
+    def one_tile(image_ref, start, out_start, width):
+        at_in = pl.ds(pl.multiple_of(start, 128), width)
+        at = pl.ds(pl.multiple_of(out_start, 128), width)
         for q in range(2):
             value = (
                 jnp.dot(
                     w_ref[q],
-                    image_ref[q, :, :, at].reshape(ROWS, PTILE),
+                    image_ref[q, :, :, at_in].reshape(ROWS, width),
                     preferred_element_type=jnp.float32,
                 )
                 * scale
@@ -344,24 +344,31 @@
                 else:
                     out_ref[rows, at] += block
 
-
-def partial_sums(z_first, sig, pos, weights, images):
+    if z_first:
+        pl.loop(0, PIX // PTILE)(lambda i: one_tile(re_ref, i * PTILE, i * PTILE, PTILE))
+        one_tile(im_ref, 0, PIX, BORDER)
+    else:
+        half = REST // 2
+        pl.loop(0, 2)(lambda i: one_tile(im_ref, BORDER + i * half, i * half, half))
+
+
+def partial_sums(z_first, sig, pos, weights, *images):
     many, rows = (Z, X * 16) if z_first else (X, Z * 16)
-    out_shape = [pltpu.VMEM((rows, PIX), jnp.float32)] * many
+    out_shape = [pltpu.VMEM((rows, SPLIT if z_first else REST), jnp.float32)] * many
     if z_first:
         out_shape.append(pltpu.VMEM((2, COLS, ROWS), jnp.bfloat16))
         out_shape.append(jax.ShapeDtypeStruct((1, N), jnp.float32))
     return pl.pallas_call(
         lambda *refs: partial_kernel(z_first, *refs),
-        in_specs=[SMEM, SMEM] + [VMEM] * (len(weights) + 1),
+        in_specs=[SMEM, SMEM] + [VMEM] * (len(weights) + len(images)),
         out_specs=[VMEM] * len(out_shape),
         out_shape=out_shape,
         compiler_params=limit(4),
         cost_estimate=pl.CostEstimate(
             flops=2 * ROWS * COLS * FEATURES, bytes_accessed=16 * 1024 * 1024, transcendentals=0
         ),
-        name="partial_re" if z_first else "partial_im",
-    )(sig, pos, *[in_vmem(v) for v in weights], in_vmem(images))
+        name="partial_first" if z_first else "partial_rest",
+    )(sig, pos, *[in_vmem(v) for v in (*weights, *images)])
 
 
 HIGH, LOW = 32, 128
@@ -369,50 +376,60 @@
 
 def insert_kernel(bound_ref, w_ref, ins_ref, *refs):
     scale = bound_ref[4:5, 0:1] * (1.0 / HEADROOM)
-    high_ids = lax.broadcasted_iota(jnp.int32, (HIGH, PIX), 0)
-    low_ids = lax.broadcasted_iota(jnp.int32, (LOW, PIX), 0)
-
-    def step(i, acc):
+
+    def add(acc, i, at, at_ids, width):
         row = pl.ds(i, 1)
-        ids = ins_ref[row, :]
+        ids = ins_ref[row, at_ids]
         high = lax.shift_right_logical(ids, 7)
         low = lax.bitwise_and(ids, LOW - 1)
-        value = w_ref[row, :] * scale
+        value = w_ref[row, at] * scale
         head = value.astype(jnp.bfloat16).astype(jnp.float32)
         tail = value - head
-        here = high == high_ids
+        here = high == lax.broadcasted_iota(jnp.int32, (HIGH, width), 0)
         rows = jnp.concatenate(
             [jnp.where(here, head, 0.0), jnp.where(here, tail, 0.0)], axis=0
         ).astype(jnp.bfloat16)
-        table = jnp.where(low == low_ids, 1.0, 0.0).astype(jnp.bfloat16)
+        there = low == lax.broadcasted_iota(jnp.int32, (LOW, width), 0)
+        table = jnp.where(there, 1.0, 0.0).astype(jnp.bfloat16)
         return acc + lax.dot_general(rows, table, DIMS, preferred_element_type=jnp.float32)
 
     empty = jnp.zeros((2 * HIGH, LOW), jnp.float32)
-    acc = lax.fori_loop(0, 16, step, empty, unroll=1 if len(refs) == 1 else 4)
-    slab = acc[:HIGH] + acc[HIGH:]
-    if len(refs) == 1:
-        refs[0][...] = slab
-    else:
-        re_ref, out_ref = refs
+    if len(refs) == 3:
+        re_ref, im_ref, out_ref = refs
+        step = lambda i, acc: add(acc, i, slice(0, REST), slice(BORDER, PIX), REST)
+        acc = lax.fori_loop(0, 16, step, empty, unroll=4)
+        slab = im_ref[...] + acc[:HIGH] + acc[HIGH:]
         for h in range(HIGH):
             at = slice(h * LOW, (h + 1) * LOW)
             out_ref[0:1, at] = re_ref[h : h + 1, :]
             out_ref[1:2, at] = slab[h : h + 1, :]
-
-
-def insert(bound, weighted, insertion, *re):
-    shape = (2, VOX) if re else (HIGH, LOW)
+    else:
+        re_ref, im_ref = refs
+
+        def step(i, both):
+            re, im = both
+            re = add(re, i, slice(0, PIX), slice(0, PIX), PIX)
+            im = add(im, i, slice(PIX, SPLIT), slice(0, BORDER), BORDER)
+            return re, im
+
+        re, im = lax.fori_loop(0, 16, step, (empty, empty), unroll=2)
+        re_ref[...] = re[:HIGH] + re[HIGH:]
+        im_ref[...] = im[:HIGH] + im[HIGH:]
+
+
+def insert(bound, weighted, insertion, *slabs):
+    slab = jax.ShapeDtypeStruct((HIGH, LOW), jnp.float32)
     return pl.pallas_call(
         insert_kernel,
-        in_specs=[VMEM] * (3 + len(re)),
-        out_specs=VMEM,
-        out_shape=jax.ShapeDtypeStruct(shape, jnp.float32),
+        in_specs=[VMEM] * (3 + len(slabs)),
+        out_specs=VMEM if slabs else [VMEM, VMEM],
+        out_shape=jax.ShapeDtypeStruct((2, VOX), jnp.float32) if slabs else [slab, slab],
         compiler_params=limit(8),
         cost_estimate=pl.CostEstimate(
             flops=4 * HIGH * LOW * 16 * PIX, bytes_accessed=512 * 1024, transcendentals=0
         ),
-        name="insert_im" if re else "insert_re",
-    )(bound, weighted.reshape(16, PIX), insertion, *re)
+        name="insert_rest" if slabs else "insert_first",
+    )(bound, weighted.reshape(16, weighted.shape[-1]), insertion, *slabs)
 
 
 def img_index(z, x, c):
@@ -516,13 +533,13 @@
     scores, stats = score_rest(sig, pos, messages, batches, shifted, acc)
     merged = merge(stats, send(stats, dc=1))
     every = exchange_refs(merged)
-    *sums_re, weights, evidence = partial_sums(True, sig, pos, (scores, *every), shifted[0])
-    sums_im = partial_sums(False, sig, pos, (weights, merged), shifted[1])
-    total_re = scatter_z_first([v.reshape(X, 2, 8, PIX) for v in sums_re])
-    total_im = scatter_x_first([v.reshape(Z, 2, 8, PIX) for v in sums_im])
+    *sums, weights, evidence = partial_sums(True, sig, pos, (scores, *every), *shifted)
+    sums_rest = partial_sums(False, sig, pos, (weights, merged), shifted[1])
+    total = scatter_z_first([v.reshape(X, 2, 8, SPLIT) for v in sums])
+    total_rest = scatter_x_first([v.reshape(Z, 2, 8, REST) for v in sums_rest])
     ids = insertion.reshape(16, PIX)
-    slab = insert(merged, total_re, ids)
-    volume = insert(merged, total_im, ids, slab)
+    slabs = insert(merged, total, ids)
+    volume = insert(merged, total_rest, ids, *slabs)
     return volume, evidence.reshape(N)
 
 

time: 151 us -> 164 us (1.086); the launches traced: 148 us -> 164 us
  waiting for transfers between devices: 56.6 us -> 72.5 us
    ppermute x31, waiting for transfers between devices: 52.1 us -> 61.3 us  [send(): return lax.ppermute(value, 'img', pairs(dz, dx, dc))]
    all_to_all x1, waiting for transfers between devices: 2.8 us -> 9.46 us  [all_to_all_z(): lax.all_to_all(value, 'img', split_axis=0, concat_axis=0, tiled=True, axi...]
  transfers between devices with their start and end apart: 35 -> 35, of which waited for: 16 -> 16; matrix products, arithmetic and copies ran while one was open for 2% -> 2% of each run, Pallas kernels for 14% -> 12%
where the time goes in v6:
time: 164 us
  waiting for transfers between devices  72.5 us (44%)
  starting transfers between devices  51.5 us (31%)
  Pallas kernels  33.4 us (20%)
  local copies, waits for them, and re-layouts  3.46 us (2%)
  other arithmetic  1.95 us (1%)
    ppermute x31, waiting for transfers between devices, send(): return lax.ppermute(value, 'img', pairs(dz, dx, dc))  61.3 us
    ppermute x31, starting transfers between devices, send(): return lax.ppermute(value, 'img', pairs(dz, dx, dc))  41.5 us
    pallas_call x2, Pallas kernels, partial_sums(): pl.pallas_call(lambda *refs: partial_kernel(z_first, *refs), in_specs=[SM...  9.95 us
    all_to_all x1, waiting for transfers between devices, all_to_all_z(): lax.all_to_all(value, 'img', split_axis=0, concat_axis=0, tiled=True, axi...  9.46 us
    pallas_call x2, Pallas kernels, insert(): pl.pallas_call(insert_kernel, in_specs=[VMEM] * (3 + len(slabs)), out_spe...  8.54 us
    pallas_call x1, Pallas kernels, shifted_images(): pl.pallas_call(shift_kernel, in_specs=[VMEM] * 3, out_specs=[VMEM, VMEM],...  5.49 us
    all_to_all x1, starting transfers between devices, all_to_all_z(): lax.all_to_all(value, 'img', split_axis=0, concat_axis=0, tiled=True, axi...  5.11 us
    ppermute x3, starting transfers between devices, exchange_refs(): lax.ppermute(value, 'ref', [(r, (r + k) % REFS) for r in range(REFS)])  4.94 us
  transfers between devices with their start and end apart: 35, of which 16 were waited for; matrix products, arithmetic and copies ran while one was open for 2% of the time, Pallas kernels for 12%

profile of v6, /device:TPU:8, one launch (start us, length us, event | category | flops | bytes accessed | tf_op | source)
XLA Modules:
  0.0 163.8 jit_solution(4354471498015059977)
XLA Ops:
  12.2 4.0 %collective-permute-start.3 = (bf16[2,8,11136]{2,1,0:T(8,128)(2,1)S(1)}, bf16[2,8,11136]{2,1,0:T(8,128)(2,1)S(1)}, u32[]{:S(2)}, u32[]{:S(2)}) collective-permute-start(bf16[2,8,11136]{2,1,0:T(8,128)(2,1)S(1)} %assemble.1.refs_0_), channel_id=1, source_target_pairs={{0,224},{4,228},{8,232},{12,236},{16,240},{20,244},{24,248},{28,25... | collective-permute-start | bytes 1069064 | tf_op jit(solution)/shard_map/ppermute | solution.py:452
  16.3 8.0 %collective-permute-done.6.refs_4_.refs_7_ = bf16[2,8,11136]{2,1,0:T(8,128)(2,1)S(1)} collective-permute-done((bf16[2,8,11136]{2,1,0:T(8,128)(2,1)S(1)}, bf16[2,8,11136]{2,1,0:T(8,128)(2,1)S(1)}, u32[]{:S(2)}, u32[]{:S(2)}) %collective-permute-start.6) | collective-permute-done | bytes 356384 | tf_op jit(solution)/shard_map/ppermute | solution.py:452
  24.3 3.2 %collective-permute-start.4 = (bf16[2,8,11136]{2,1,0:T(8,128)(2,1)S(1)}, bf16[2,8,11136]{2,1,0:T(8,128)(2,1)S(1)}, u32[]{:S(2)}, u32[]{:S(2)}) collective-permute-start(bf16[2,8,11136]{2,1,0:T(8,128)(2,1)S(1)} %collective-permute-done.3.refs_1_), channel_id=1, source_target_pairs={{0,224},{4,228},{8,232},{12,236},{16,240},{20,244},{24,248},{28,25... | collective-permute-start | bytes 1069064 | tf_op jit(solution)/shard_map/ppermute | solution.py:452
  27.5 7.3 %collective-permute-done.7.refs_3_.refs_6_ = bf16[2,8,11136]{2,1,0:T(8,128)(2,1)S(1)} collective-permute-done((bf16[2,8,11136]{2,1,0:T(8,128)(2,1)S(1)}, bf16[2,8,11136]{2,1,0:T(8,128)(2,1)S(1)}, u32[]{:S(2)}, u32[]{:S(2)}) %collective-permute-start.7) | collective-permute-done | bytes 356384 | tf_op jit(solution)/shard_map/ppermute | solution.py:452
  34.8 3.2 %collective-permute-start.5 = (bf16[2,8,11136]{2,1,0:T(8,128)(2,1)S(1)}, bf16[2,8,11136]{2,1,0:T(8,128)(2,1)S(1)}, u32[]{:S(2)}, u32[]{:S(2)}) collective-permute-start(bf16[2,8,11136]{2,1,0:T(8,128)(2,1)S(1)} %collective-permute-done.4.refs_2_), channel_id=1, source_target_pairs={{0,224},{4,228},{8,232},{12,236},{16,240},{20,244},{24,248},{28,25... | collective-permute-start | bytes 1069064 | tf_op jit(solution)/shard_map/ppermute | solution.py:452
  38.0 6.4 %collective-permute-done.8.refs_2_.refs_5_ = bf16[2,8,11136]{2,1,0:T(8,128)(2,1)S(1)} collective-permute-done((bf16[2,8,11136]{2,1,0:T(8,128)(2,1)S(1)}, bf16[2,8,11136]{2,1,0:T(8,128)(2,1)S(1)}, u32[]{:S(2)}, u32[]{:S(2)}) %collective-permute-start.8) | collective-permute-done | bytes 356384 | tf_op jit(solution)/shard_map/ppermute | solution.py:452
  48.8 4.4 %collective-permute-done.9.refs_1_.refs_4_ = bf16[2,8,11136]{2,1,0:T(8,128)(2,1)S(1)} collective-permute-done((bf16[2,8,11136]{2,1,0:T(8,128)(2,1)S(1)}, bf16[2,8,11136]{2,1,0:T(8,128)(2,1)S(1)}, u32[]{:S(2)}, u32[]{:S(2)}) %collective-permute-start.9) | collective-permute-done | bytes 356384 | tf_op jit(solution)/shard_map/ppermute | solution.py:452
  54.9 5.5 %shift.1 = (bf16[2,5,256,2048]{3,2,1,0:T(8,128)(2,1)S(1)}, bf16[2,5,256,2048]{3,2,1,0:T(8,128)(2,1)S(1)}) custom-call(f32[8,2048]{1,0:T(8,128)S(1)} %copy-done.4, bf16[256,4096]{1,0:T(8,128)(2,1)S(1)} %copy-done.2, bf16[256,4096]{1,0:T(8,128)(2,1)} %collective-permute-done.16.mate_ref), custom_call_target="tpu_custom_call" | custom-call | flops 25165824 | bytes 25165824 | tf_op jit(solution)/shard_map/shift/pallas_call | solution.py:138
  63.2 4.4 %score_first.1.refs_15_ = f32[2,1280,256]{2,1,0:T(8,128)S(1)} custom-call(s32[2,512]{1,0:T(2,128)S(1)} %constant_dynamic-slice_fusion.sig_ref.refs_0_, s32[4]{0:T(128)S(1)} %pad_add_fusion.pos_ref.refs_1_, bf16[2,8,11136]{2,1,0:T(8,128)(2,1)S(1)} %assemble.1.refs_0_, bf16[2,8,11136]{2,1,0:T(8,128)(2,1)S(1)} %collective-permute-done.3.refs_1_, ...), custom_call_target="tpu_custom_call" | custom-call | flops 3019898880 | bytes 16777216 | tf_op jit(solution)/shard_map/score_first/pallas_call | solution.py:186
  68.3 4.6 %score_rest.1 = (f32[2,256,1280]{2,1,0:T(8,128)S(1)}, f32[8,256]{1,0:T(8,128)S(1)}) custom-call(s32[2,512]{1,0:T(2,128)S(1)} %constant_dynamic-slice_fusion.sig_ref.refs_0_, s32[4]{0:T(128)S(1)} %pad_add_fusion.pos_ref.refs_1_, bf16[2,8,11136]{2,1,0:T(8,128)(2,1)S(1)} %assemble.1.refs_0_, bf16[2,8,11136]{2,1,0:T(8,128)(2,1)S(1)} %collective-permute-done.3.refs_1_, ...), custom_call_target="tpu_custom_call" | custom-call | flops 2348810240 | bytes 16777216 | tf_op jit(solution)/shard_map/score_rest/pallas_call | solution.py:249
  81.0 5.8 %partial_first.1 = (f32[64,2304]{1,0:T(8,128)S(1)}, f32[64,2304]{1,0:T(8,128)S(1)}, f32[64,2304]{1,0:T(8,128)S(1)}, f32[64,2304]{1,0:T(8,128)S(1)}, f32[64,2304]...) custom-call(s32[2,512]{1,0:T(2,128)S(1)} %constant_dynamic-slice_fus, ...), custom_call_target="tpu_custom_call" | custom-call | flops 2684354560 | bytes 16777216 | tf_op jit(solution)/shard_map/partial_first/pallas_call | solution.py:361
  86.9 3.3 %collective-permute-start.28 = (f16[4,2,8,2304]{3,2,1,0:T(8,128)(2,1)S(1)}, f16[4,2,8,2304]{3,2,1,0:T(8,128)(2,1)S(1)}, u32[]{:S(2)}, u32[]{:S(2)}) collective-permute-start(f16[4,2,8,2304]{3,2,1,0:T(8,128)(2,1)S(1)} %bitcast.50), channel_id=1, source_target_pairs={{0,224},{4,228},{8,232},{12,236},{16,240},{20,244},{24,248},{28,25... | collective-permute-start | bytes 884744 | tf_op jit(solution)/shard_map/ppermute | solution.py:452
  90.2 5.6 %collective-permute-done.24 = f16[4,2,8,2304]{3,2,1,0:T(8,128)(2,1)S(1)} collective-permute-done((f16[4,2,8,2304]{3,2,1,0:T(8,128)(2,1)S(1)}, f16[4,2,8,2304]{3,2,1,0:T(8,128)(2,1)S(1)}, u32[]{:S(2)}, u32[]{:S(2)}) %collective-permute-start.24) | collective-permute-done | bytes 294944 | tf_op jit(solution)/shard_map/ppermute | solution.py:452
  96.0 3.3 %collective-permute-start.29 = (f16[4,2,8,2304]{3,2,1,0:T(8,128)(2,1)S(1)}, f16[4,2,8,2304]{3,2,1,0:T(8,128)(2,1)S(1)}, u32[]{:S(2)}, u32[]{:S(2)}) collective-permute-start(f16[4,2,8,2304]{3,2,1,0:T(8,128)(2,1)S(1)} %add_convert_fusion.2), channel_id=1, source_target_pairs={{0,224},{4,228},{8,232},{12,236},{16,240},{20,244},{24,248},{28,25... | collective-permute-start | bytes 884744 | tf_op jit(solution)/shard_map/ppermute | solution.py:452
  99.3 4.7 %collective-permute-done.25 = f16[4,2,8,2304]{3,2,1,0:T(8,128)(2,1)S(1)} collective-permute-done((f16[4,2,8,2304]{3,2,1,0:T(8,128)(2,1)S(1)}, f16[4,2,8,2304]{3,2,1,0:T(8,128)(2,1)S(1)}, u32[]{:S(2)}, u32[]{:S(2)}) %collective-permute-start.25) | collective-permute-done | bytes 294944 | tf_op jit(solution)/shard_map/ppermute | solution.py:452
  104.5 3.3 %collective-permute-start.30 = (f16[4,2,8,2304]{3,2,1,0:T(8,128)(2,1)S(1)}, f16[4,2,8,2304]{3,2,1,0:T(8,128)(2,1)S(1)}, u32[]{:S(2)}, u32[]{:S(2)}) collective-permute-start(f16[4,2,8,2304]{3,2,1,0:T(8,128)(2,1)S(1)} %add_convert_fusion.1), channel_id=1, source_target_pairs={{0,224},{4,228},{8,232},{12,236},{16,240},{20,244},{24,248},{28,25... | collective-permute-start | bytes 884744 | tf_op jit(solution)/shard_map/ppermute | solution.py:452
  107.7 4.6 %collective-permute-done.26 = f16[4,2,8,2304]{3,2,1,0:T(8,128)(2,1)S(1)} collective-permute-done((f16[4,2,8,2304]{3,2,1,0:T(8,128)(2,1)S(1)}, f16[4,2,8,2304]{3,2,1,0:T(8,128)(2,1)S(1)}, u32[]{:S(2)}, u32[]{:S(2)}) %collective-permute-start.26) | collective-permute-done | bytes 294944 | tf_op jit(solution)/shard_map/ppermute | solution.py:452
  112.6 4.2 %partial_rest.1 = (f32[128,1792]{1,0:T(8,128)S(1)}, f32[128,1792]{1,0:T(8,128)S(1)}, f32[128,1792]{1,0:T(8,128)S(1)}, f32[128,1792]{1,0:T(8,128)S(1)}) custom-call(s32[2,512]{1,0:T(2,128)S(1)} %constant_dynamic-slice_fusion.sig_ref.refs_0_, s32[4]{0:T(128)S(1)} %pad_add_fusion.pos_ref.refs_1_, bf16[2,256,1280]{2,1,0:T(8,128)(2,1)S(1)} %get-tuple-element.32.refs_2_, ...), custom_call_target="tpu_custom_call" | custom-call | flops 2684354560 | bytes 16777216 | tf_op jit(solution)/shard_map/partial_rest/pallas_call | solution.py:361
  124.0 11.8 %collective-permute-done.23 = f16[8,2,8,1792]{3,2,1,0:T(8,128)(2,1)S(1)} collective-permute-done((f16[8,2,8,1792]{3,2,1,0:T(8,128)(2,1)S(1)}, f16[8,2,8,1792]{3,2,1,0:T(8,128)(2,1)S(1)}, u32[]{:S(2)}, u32[]{:S(2)}) %collective-permute-start.23) | collective-permute-done | bytes 458784 | tf_op jit(solution)/shard_map/ppermute | solution.py:452
  135.8 3.7 %collective-permute-done.21 = f16[8,2,8,1792]{3,2,1,0:T(8,128)(2,1)S(1)} collective-permute-done((f16[8,2,8,1792]{3,2,1,0:T(8,128)(2,1)S(1)}, f16[8,2,8,1792]{3,2,1,0:T(8,128)(2,1)S(1)}, u32[]{:S(2)}, u32[]{:S(2)}) %collective-permute-start.21) | collective-permute-done | bytes 458784 | tf_op jit(solution)/shard_map/ppermute | solution.py:452
  140.5 5.1 %all-to-all-start = ((f16[8,2,8,1792]{3,2,1,0:T(8,128)(2,1)}), f16[8,2,8,1792]{3,2,1,0:T(8,128)(2,1)S(1)}, u32[]{:S(2)}, u32[]{:S(2)}) async-start(f16[8,2,8,1792]{3,2,1,0:T(8,128)(2,1)} %add_convert_fusion), calls=%async_computation | async-start | bytes 917504 | tf_op jit(solution)/shard_map/all_to_all | solution.py:456
  145.7 4.7 %insert_first.1 = (f32[32,128]{1,0:T(8,128)S(1)}, f32[32,128]{1,0:T(8,128)S(1)}) custom-call(f32[8,256]{1,0:T(8,128)S(1)} %merge.1.refs_3_.bound_ref, f32[16,2304]{1,0:T(8,128)S(1)} %fusion.3.w_ref, s32[16,2048]{1,0:T(8,128)S(1)} %bitcast.45), custom_call_target="tpu_custom_call" | custom-call | flops 536870912 | bytes 524288 | tf_op jit(solution)/shard_map/insert_first/pallas_call | solution.py:422
  150.4 9.5 %all-to-all-done = f16[8,2,8,1792]{3,2,1,0:T(8,128)(2,1)S(1)} async-done(((f16[8,2,8,1792]{3,2,1,0:T(8,128)(2,1)}), f16[8,2,8,1792]{3,2,1,0:T(8,128)(2,1)S(1)}, u32[]{:S(2)}, u32[]{:S(2)}) %all-to-all-start) | async-done | bytes 458784 | tf_op jit(solution)/shard_map/all_to_all | solution.py:456
  159.9 3.8 %insert_rest.1 = f32[2,4096]{1,0:T(2,128)} custom-call(f32[8,256]{1,0:T(8,128)S(1)} %merge.1.refs_3_.bound_ref, f32[16,1792]{1,0:T(8,128)S(1)} %bitcast.44, s32[16,2048]{1,0:T(8,128)S(1)} %bitcast.46, f32[32,128]{1,0:T(8,128)S(1)} %get-tuple-element.45.refs_0_, f32[32,128]{1,0:T(8,128)S(1)} %get-tuple-element.46.refs_1_), custom_call_target="tpu_custom_call" | custom-call | flops 536870912 | bytes 524288 | tf_op jit(solution)/shard_map/insert_rest/pallas_call | solution.py:422
  (88 shorter events, 38.5 us)
Async XLA Ops:
  0.6 52.7 %collective-permute-start.16 = (bf16[256,4096]{1,0:T(8,128)(2,1)}, bf16[256,4096]{1,0:T(8,128)(2,1)}, u32[]{:S(2)}, u32[]{:S(2)}) collective-permute-start(bf16[256,4096]{1,0:T(8,128)(2,1)} %own_ref.1), channel_id=1, source_target_pairs={{0,4},{4,0},{8,12},{12,8},{16,20},{20,16},{24,28},{28,24},{32,36},... | collective-permute-start | bytes 6291464 | tf_op jit(solution)/shard_map/ppermute | solution.py:452
  1.6 8.5 %collective-permute-start.2 = (bf16[2,8,2304]{2,1,0:T(8,128)(2,1)S(1)}, bf16[2,8,2304]{2,1,0:T(8,128)(2,1)S(1)}, u32[]{:S(2)}, u32[]{:S(2)}) collective-permute-start(bf16[2,8,2304]{2,1,0:T(8,128)(2,1)S(1)} %slice.18.refs_0_), channel_id=1, source_target_pairs={{0,8},{4,12},{8,16},{12,20},{16,24},{20,28},{24,0},{28,4},{32,40},... | collective-permute-start | bytes 221192 | tf_op jit(solution)/shard_map/ppermute | solution.py:452
  10.2 14.1 %collective-permute-start.6 = (bf16[2,8,11136]{2,1,0:T(8,128)(2,1)S(1)}, bf16[2,8,11136]{2,1,0:T(8,128)(2,1)S(1)}, u32[]{:S(2)}, u32[]{:S(2)}) collective-permute-start(bf16[2,8,11136]{2,1,0:T(8,128)(2,1)S(1)} %assemble.1.refs_0_), channel_id=1, source_target_pairs={{0,32},{4,36},{8,40},{12,44},{16,48},{20,52},{24,56},{28,60},{32,6... | collective-permute-start | bytes 1069064 | tf_op jit(solution)/shard_map/ppermute | solution.py:452
  12.2 12.1 %collective-permute-start.3 = (bf16[2,8,11136]{2,1,0:T(8,128)(2,1)S(1)}, bf16[2,8,11136]{2,1,0:T(8,128)(2,1)S(1)}, u32[]{:S(2)}, u32[]{:S(2)}) collective-permute-start(bf16[2,8,11136]{2,1,0:T(8,128)(2,1)S(1)} %assemble.1.refs_0_), channel_id=1, source_target_pairs={{0,224},{4,228},{8,232},{12,236},{16,240},{20,244},{24,248},{28,25... | collective-permute-start | bytes 1069064 | tf_op jit(solution)/shard_map/ppermute | solution.py:452
  24.3 10.5 %collective-permute-start.7 = (bf16[2,8,11136]{2,1,0:T(8,128)(2,1)S(1)}, bf16[2,8,11136]{2,1,0:T(8,128)(2,1)S(1)}, u32[]{:S(2)}, u32[]{:S(2)}) collective-permute-start(bf16[2,8,11136]{2,1,0:T(8,128)(2,1)S(1)} %collective-permute-done.6.refs_4_.refs_7_), channel_id=1, source_target_pairs={{0,32},{4,36},{8,40},{12,44},{16,48},{20,52},{24,56},{28,60},{32,6... | collective-permute-start | bytes 1069064 | tf_op jit(solution)/shard_map/ppermute | solution.py:452
  24.3 10.5 %collective-permute-start.4 = (bf16[2,8,11136]{2,1,0:T(8,128)(2,1)S(1)}, bf16[2,8,11136]{2,1,0:T(8,128)(2,1)S(1)}, u32[]{:S(2)}, u32[]{:S(2)}) collective-permute-start(bf16[2,8,11136]{2,1,0:T(8,128)(2,1)S(1)} %collective-permute-done.3.refs_1_), channel_id=1, source_target_pairs={{0,224},{4,228},{8,232},{12,236},{16,240},{20,244},{24,248},{28,25... | collective-permute-start | bytes 1069064 | tf_op jit(solution)/shard_map/ppermute | solution.py:452
  34.8 9.6 %collective-permute-start.8 = (bf16[2,8,11136]{2,1,0:T(8,128)(2,1)S(1)}, bf16[2,8,11136]{2,1,0:T(8,128)(2,1)S(1)}, u32[]{:S(2)}, u32[]{:S(2)}) collective-permute-start(bf16[2,8,11136]{2,1,0:T(8,128)(2,1)S(1)} %collective-permute-done.7.refs_3_.refs_6_), channel_id=1, source_target_pairs={{0,32},{4,36},{8,40},{12,44},{16,48},{20,52},{24,56},{28,60},{32,6... | collective-permute-start | bytes 1069064 | tf_op jit(solution)/shard_map/ppermute | solution.py:452
  34.8 11.5 %collective-permute-start.5 = (bf16[2,8,11136]{2,1,0:T(8,128)(2,1)S(1)}, bf16[2,8,11136]{2,1,0:T(8,128)(2,1)S(1)}, u32[]{:S(2)}, u32[]{:S(2)}) collective-permute-start(bf16[2,8,11136]{2,1,0:T(8,128)(2,1)S(1)} %collective-permute-done.4.refs_2_), channel_id=1, source_target_pairs={{0,224},{4,228},{8,232},{12,236},{16,240},{20,244},{24,248},{28,25... | collective-permute-start | bytes 1069064 | tf_op jit(solution)/shard_map/ppermute | solution.py:452
  44.5 8.8 %collective-permute-start.9 = (bf16[2,8,11136]{2,1,0:T(8,128)(2,1)S(1)}, bf16[2,8,11136]{2,1,0:T(8,128)(2,1)S(1)}, u32[]{:S(2)}, u32[]{:S(2)}) collective-permute-start(bf16[2,8,11136]{2,1,0:T(8,128)(2,1)S(1)} %collective-permute-done.8.refs_2_.refs_5_), channel_id=1, source_target_pairs={{0,32},{4,36},{8,40},{12,44},{16,48},{20,52},{24,56},{28,60},{32,6... | collective-permute-start | bytes 1069064 | tf_op jit(solution)/shard_map/ppermute | solution.py:452
  44.5 18.3 %collective-permute-start.12 = (bf16[5,2,8,1920]{3,2,1,0:T(8,128)(2,1)S(1)}, bf16[5,2,8,1920]{3,2,1,0:T(8,128)(2,1)S(1)}, u32[]{:S(2)}, u32[]{:S(2)}) collective-permute-start(bf16[5,2,8,1920]{3,2,1,0:T(8,128)(2,1)S(1)} %pick.2), channel_id=1, source_target_pairs={{0,8},{4,12},{8,16},{12,20},{16,24},{20,28},{24,0},{28,4},{32,40},... | collective-permute-start | bytes 921608 | tf_op jit(solution)/shard_map/ppermute | solution.py:452
  44.6 23.0 %collective-permute-start.11 = (bf16[5,2,8,1920]{3,2,1,0:T(8,128)(2,1)S(1)}, bf16[5,2,8,1920]{3,2,1,0:T(8,128)(2,1)S(1)}, u32[]{:S(2)}, u32[]{:S(2)}) collective-permute-start(bf16[5,2,8,1920]{3,2,1,0:T(8,128)(2,1)S(1)} %pick.2), channel_id=1, source_target_pairs={{0,16},{4,20},{8,24},{12,28},{16,0},{20,4},{24,8},{28,12},{32,48},... | collective-permute-start | bytes 921608 | tf_op jit(solution)/shard_map/ppermute | solution.py:452
  46.3 21.3 %collective-permute-start.10 = (bf16[5,2,8,1920]{3,2,1,0:T(8,128)(2,1)S(1)}, bf16[5,2,8,1920]{3,2,1,0:T(8,128)(2,1)S(1)}, u32[]{:S(2)}, u32[]{:S(2)}) collective-permute-start(bf16[5,2,8,1920]{3,2,1,0:T(8,128)(2,1)S(1)} %pick.2), channel_id=1, source_target_pairs={{0,24},{4,28},{8,0},{12,4},{16,8},{20,12},{24,16},{28,20},{32,56},... | collective-permute-start | bytes 921608 | tf_op jit(solution)/shard_map/ppermute | solution.py:452
  53.3 14.4 %collective-permute-start.15 = (bf16[3,2,8,1920]{3,2,1,0:T(8,128)(2,1)S(1)}, bf16[3,2,8,1920]{3,2,1,0:T(8,128)(2,1)S(1)}, u32[]{:S(2)}, u32[]{:S(2)}) collective-permute-start(bf16[3,2,8,1920]{3,2,1,0:T(8,128)(2,1)S(1)} %pick.3), channel_id=1, source_target_pairs={{0,8},{4,12},{8,16},{12,20},{16,24},{20,28},{24,0},{28,4},{32,40},... | collective-permute-start | bytes 552968 | tf_op jit(solution)/shard_map/ppermute | solution.py:452
  53.4 14.3 %collective-permute-start.14 = (bf16[3,2,8,1920]{3,2,1,0:T(8,128)(2,1)S(1)}, bf16[3,2,8,1920]{3,2,1,0:T(8,128)(2,1)S(1)}, u32[]{:S(2)}, u32[]{:S(2)}) collective-permute-start(bf16[3,2,8,1920]{3,2,1,0:T(8,128)(2,1)S(1)} %pick.3), channel_id=1, source_target_pairs={{0,16},{4,20},{8,24},{12,28},{16,0},{20,4},{24,8},{28,12},{32,48},... | collective-permute-start | bytes 552968 | tf_op jit(solution)/shard_map/ppermute | solution.py:452
  86.8 9.0 %collective-permute-start.24 = (f16[4,2,8,2304]{3,2,1,0:T(8,128)(2,1)S(1)}, f16[4,2,8,2304]{3,2,1,0:T(8,128)(2,1)S(1)}, u32[]{:S(2)}, u32[]{:S(2)}) collective-permute-start(f16[4,2,8,2304]{3,2,1,0:T(8,128)(2,1)S(1)} %bitcast.51), channel_id=1, source_target_pairs={{0,32},{4,36},{8,40},{12,44},{16,48},{20,52},{24,56},{28,60},{32,6... | collective-permute-start | bytes 884744 | tf_op jit(solution)/shard_map/ppermute | solution.py:452
  86.9 9.0 %collective-permute-start.28 = (f16[4,2,8,2304]{3,2,1,0:T(8,128)(2,1)S(1)}, f16[4,2,8,2304]{3,2,1,0:T(8,128)(2,1)S(1)}, u32[]{:S(2)}, u32[]{:S(2)}) collective-permute-start(f16[4,2,8,2304]{3,2,1,0:T(8,128)(2,1)S(1)} %bitcast.50), channel_id=1, source_target_pairs={{0,224},{4,228},{8,232},{12,236},{16,240},{20,244},{24,248},{28,25... | collective-permute-start | bytes 884744 | tf_op jit(solution)/shard_map/ppermute | solution.py:452
  104.5 15.6 %collective-permute-start.30 = (f16[4,2,8,2304]{3,2,1,0:T(8,128)(2,1)S(1)}, f16[4,2,8,2304]{3,2,1,0:T(8,128)(2,1)S(1)}, u32[]{:S(2)}, u32[]{:S(2)}) collective-permute-start(f16[4,2,8,2304]{3,2,1,0:T(8,128)(2,1)S(1)} %add_convert_fusion.1), channel_id=1, source_target_pairs={{0,224},{4,228},{8,232},{12,236},{16,240},{20,244},{24,248},{28,25... | collective-permute-start | bytes 884744 | tf_op jit(solution)/shard_map/ppermute | solution.py:452
  116.9 18.9 %collective-permute-start.23 = (f16[8,2,8,1792]{3,2,1,0:T(8,128)(2,1)S(1)}, f16[8,2,8,1792]{3,2,1,0:T(8,128)(2,1)S(1)}, u32[]{:S(2)}, u32[]{:S(2)}) collective-permute-start(f16[8,2,8,1792]{3,2,1,0:T(8,128)(2,1)S(1)} %bitcast.49), channel_id=1, source_target_pairs={{0,24},{4,28},{8,0},{12,4},{16,8},{20,12},{24,16},{28,20},{32,56},... | collective-permute-start | bytes 1376264 | tf_op jit(solution)/shard_map/ppermute | solution.py:452
  118.7 17.1 %collective-permute-start.22 = (f16[8,2,8,1792]{3,2,1,0:T(8,128)(2,1)S(1)}, f16[8,2,8,1792]{3,2,1,0:T(8,128)(2,1)S(1)}, u32[]{:S(2)}, u32[]{:S(2)}) collective-permute-start(f16[8,2,8,1792]{3,2,1,0:T(8,128)(2,1)S(1)} %bitcast.48), channel_id=1, source_target_pairs={{0,16},{4,20},{8,24},{12,28},{16,0},{20,4},{24,8},{28,12},{32,48},... | collective-permute-start | bytes 1376264 | tf_op jit(solution)/shard_map/ppermute | solution.py:452
  120.0 19.5 %collective-permute-start.21 = (f16[8,2,8,1792]{3,2,1,0:T(8,128)(2,1)S(1)}, f16[8,2,8,1792]{3,2,1,0:T(8,128)(2,1)S(1)}, u32[]{:S(2)}, u32[]{:S(2)}) collective-permute-start(f16[8,2,8,1792]{3,2,1,0:T(8,128)(2,1)S(1)} %bitcast.47), channel_id=1, source_target_pairs={{0,8},{4,12},{8,16},{12,20},{16,24},{20,28},{24,0},{28,4},{32,40},... | collective-permute-start | bytes 1376264 | tf_op jit(solution)/shard_map/ppermute | solution.py:452
  120.7 24.9 %collective-permute-start.31 = (f16[2,8,2304]{2,1,0:T(8,128)(2,1)S(1)}, f16[2,8,2304]{2,1,0:T(8,128)(2,1)S(1)}, u32[]{:S(2)}, u32[]{:S(2)}) collective-permute-start(f16[2,8,2304]{2,1,0:T(8,128)(2,1)S(1)} %get-tuple-element.50), channel_id=1, source_target_pairs={{0,8},{4,12},{8,16},{12,20},{16,24},{20,28},{24,0},{28,4},{32,40},... | collective-permute-start | bytes 221192 | tf_op jit(solution)/shard_map/ppermute | solution.py:452
  122.4 23.2 %collective-permute-start.33 = (f16[2,8,2304]{2,1,0:T(8,128)(2,1)S(1)}, f16[2,8,2304]{2,1,0:T(8,128)(2,1)S(1)}, u32[]{:S(2)}, u32[]{:S(2)}) collective-permute-start(f16[2,8,2304]{2,1,0:T(8,128)(2,1)S(1)} %get-tuple-element.51), channel_id=1, source_target_pairs={{0,24},{4,28},{8,0},{12,4},{16,8},{20,12},{24,16},{28,20},{32,56},... | collective-permute-start | bytes 221192 | tf_op jit(solution)/shard_map/ppermute | solution.py:452
  135.8 9.8 %collective-permute-start.32 = (f16[2,8,2304]{2,1,0:T(8,128)(2,1)S(1)}, f16[2,8,2304]{2,1,0:T(8,128)(2,1)S(1)}, u32[]{:S(2)}, u32[]{:S(2)}) collective-permute-start(f16[2,8,2304]{2,1,0:T(8,128)(2,1)S(1)} %get-tuple-element.52), channel_id=1, source_target_pairs={{0,16},{4,20},{8,24},{12,28},{16,0},{20,4},{24,8},{28,12},{32,48},... | collective-permute-start | bytes 221192 | tf_op jit(solution)/shard_map/ppermute | solution.py:452
  140.5 19.4 %all-to-all-start = ((f16[8,2,8,1792]{3,2,1,0:T(8,128)(2,1)}), f16[8,2,8,1792]{3,2,1,0:T(8,128)(2,1)S(1)}, u32[]{:S(2)}, u32[]{:S(2)}) async-start(f16[8,2,8,1792]{3,2,1,0:T(8,128)(2,1)} %add_convert_fusion), calls=%async_computation | async-start | bytes 917504 | tf_op jit(solution)/shard_map/all_to_all | solution.py:456
  (17 other events, 192.0 us)

commit v7 on v6

--- a/solution.py
+++ b/solution.py
@@ -22,10 +22,11 @@
 SCALE = 2.0 / math.sqrt(FEATURES)
 HEADROOM = 2.5
 EXTRA = 128
-SPLIT = 2304
+SPLIT = 2560
 REST = FEATURES - SPLIT
 BORDER = SPLIT - PIX
 UNIT = REST + EXTRA
+FAR = 2 * SPLIT
 MESSAGE = X * SPLIT + UNIT
 EARLY = (0, 1, 2, 6, 7)
 LATE = (3, 4, 5)
@@ -96,7 +97,7 @@
 def pick_kernel(*refs):
     *messages, out_ref = refs
     for k, message in enumerate(messages):
-        out_ref[k] = message[:, :, X * SPLIT :]
+        out_ref[k] = message[:, :, message.shape[2] - UNIT :]
 
 
 def pick(messages):
@@ -159,15 +160,21 @@
 DIMS = (((1,), (1,)), ((), ()))
 
 
+def message_part(messages, dz, block, start, stop):
+    if dz == Z // 2 and start >= FAR:
+        return messages[Z][block, :, start - FAR : stop - FAR]
+    return messages[dz][block, :, start:stop]
+
+
 def score_first_kernel(sig_ref, pos_ref, *refs):
-    messages, (re_ref, im_ref, acc_ref, sel) = refs[:Z], refs[Z:]
+    messages, (re_ref, im_ref, acc_ref, sel) = refs[: Z + 1], refs[Z + 1 :]
 
     @pl.loop(0, 2)
     def _(q):
         for o in range(RUNS):
             dz, dx = o // X, o % X
             _, second, _ = run_entry(sig_ref, pos_ref, q, dz, dx)
-            sel[o] = messages[dz][second, :, dx * SPLIT : (dx + 1) * SPLIT]
+            sel[o] = message_part(messages, dz, second, dx * SPLIT, (dx + 1) * SPLIT)
         acc_ref[q] = lax.dot_general(
             re_ref[q].reshape(ROWS, PIX),
             sel[:, :, 0:PIX].reshape(COLS, PIX),
@@ -185,7 +192,7 @@
 def score_first(sig, pos, messages, shifted):
     return pl.pallas_call(
         score_first_kernel,
-        in_specs=[SMEM, SMEM] + [VMEM] * (Z + 2),
+        in_specs=[SMEM, SMEM] + [VMEM] * (Z + 3),
         out_specs=VMEM,
         out_shape=pltpu.VMEM((2, ROWS, COLS), jnp.float32),
         scratch_shapes=[pltpu.VMEM((RUNS, 8, SPLIT), jnp.bfloat16)],
@@ -198,13 +205,13 @@
 
 
 def score_rest_kernel(sig_ref, pos_ref, *refs):
-    messages, batches = refs[:Z], refs[Z : Z + 6]
-    im_ref, acc = refs[Z + 6 : Z + 8]
-    st_ref, stat_ref, sel, work, mask = refs[Z + 8 :]
+    messages, batches = refs[: Z + 1], refs[Z + 1 : Z + 7]
+    im_ref, acc = refs[Z + 7 : Z + 9]
+    st_ref, stat_ref, sel, work, mask = refs[Z + 9 :]
 
     def unit(dz, dx, second, at):
         if dx == 0:
-            return messages[dz][second, :, X * SPLIT + at.start : X * SPLIT + at.stop]
+            return message_part(messages, dz, second, X * SPLIT + at.start, X * SPLIT + at.stop)
         early = dz in EARLY
         place = (EARLY if early else LATE).index(dz)
         return batches[dx - 1 if early else dx + 2][place, second, :, at]
@@ -248,7 +255,7 @@
 def score_rest(sig, pos, messages, batches, shifted, acc):
     return pl.pallas_call(
         score_rest_kernel,
-        in_specs=[SMEM, SMEM] + [VMEM] * (Z + 8),
+        in_specs=[SMEM, SMEM] + [VMEM] * (Z + 9),
         out_specs=[VMEM, VMEM],
         out_shape=[
             pltpu.VMEM((2, COLS, ROWS), jnp.float32),
@@ -397,7 +404,7 @@
     if len(refs) == 3:
         re_ref, im_ref, out_ref = refs
         step = lambda i, acc: add(acc, i, slice(0, REST), slice(BORDER, PIX), REST)
-        acc = lax.fori_loop(0, 16, step, empty, unroll=4)
+        acc = lax.fori_loop(0, 16, step, empty, unroll=2)
         slab = im_ref[...] + acc[:HIGH] + acc[HIGH:]
         for h in range(HIGH):
             at = slice(h * LOW, (h + 1) * LOW)
@@ -412,7 +419,7 @@
             im = add(im, i, slice(PIX, SPLIT), slice(0, BORDER), BORDER)
             return re, im
 
-        re, im = lax.fori_loop(0, 16, step, (empty, empty), unroll=2)
+        re, im = lax.fori_loop(0, 16, step, (empty, empty))
         re_ref[...] = re[:HIGH] + re[HIGH:]
         im_ref[...] = im[:HIGH] + im[HIGH:]
 
@@ -463,18 +470,20 @@
     row = [mine, send(mine, dx=-1), send(mine, dx=-2), send(mine, dx=1)]
     ahead = behind = assemble(row, unit)
     messages = {0: ahead}
-    for k in range(1, Z // 2 + 1):
+    for k in range(1, Z // 2):
         behind = send(behind, dz=1)
         messages[Z - k] = behind
-        if k < Z // 2:
-            ahead = send(ahead, dz=-1)
-            messages[k] = ahead
+        ahead = send(ahead, dz=-1)
+        messages[k] = ahead
+    left = send(behind[:, :, :FAR], dz=1)
+    right = send(ahead[:, :, FAR:], dz=-1)
+    late = [messages[3], right, messages[5]]
     batches = []
-    for places in (EARLY, LATE):
-        column = pick([messages[k] for k in places])
+    for column in (pick([messages[k] for k in EARLY]), pick(late)):
         for dx in (-1, -2, 1):
             batches.append(send(column, dx=dx))
-    return [messages[k] for k in range(Z)], batches
+    messages[Z // 2] = left
+    return [messages[k] for k in range(Z)] + [right], batches
 
 
 def wide(value):
@@ -486,17 +495,17 @@
 
 
 def scatter_z_first(parts):
-    half = Z // 2
-    behind = narrow(parts[half])
-    for k in range(half, 0, -1):
-        if k < half:
-            behind = narrow(parts[k] + wide(behind))
-        behind = send(behind, dz=1)
-    ahead = narrow(parts[half + 1])
-    for k in range(half - 1, 0, -1):
-        if k < half - 1:
-            ahead = narrow(parts[Z - k] + wide(ahead))
-        ahead = send(ahead, dz=-1)
+    far, cut = parts[Z // 2], X // 2
+    behind = send(narrow(far[:cut]), dz=1)
+    ahead = send(narrow(far[cut:]), dz=-1)
+    behind = jnp.concatenate([parts[3][:cut] + wide(behind), parts[3][cut:]])
+    ahead = jnp.concatenate([parts[5][:cut], parts[5][cut:] + wide(ahead)])
+    for k in range(3, 0, -1):
+        behind = send(narrow(behind), dz=1)
+        ahead = send(narrow(ahead), dz=-1)
+        if k > 1:
+            behind = parts[k - 1] + wide(behind)
+            ahead = parts[Z - k + 1] + wide(ahead)
     row = parts[0] + wide(behind) + wide(ahead)
     arrived = [send(narrow(row[k]), dx=k) for k in range(1, X)]
     return row[0] + wide(arrived[0]) + wide(arrived[1]) + wide(arrived[2])

time: 164 us -> 151 us (0.921)
  waiting for transfers between devices: 72.5 us -> 46.7 us
  starting transfers between devices: 51.5 us -> 61 us
    ppermute x31 -> x33, waiting for transfers between devices: 61.3 us -> 41.6 us  [send(): return lax.ppermute(value, 'img', pairs(dz, dx, dc))]
    ppermute x31 -> x33, starting transfers between devices: 41.5 us -> 52.5 us  [send(): return lax.ppermute(value, 'img', pairs(dz, dx, dc))]
    all_to_all x1, waiting for transfers between devices: 9.46 us -> 3.31 us  [all_to_all_z(): lax.all_to_all(value, 'img', split_axis=0, concat_axis=0, tiled=True, axi...]
    pallas_call x2, Pallas kernels: 8.54 us -> 10.8 us  [insert(): pl.pallas_call(insert_kernel, in_specs=[VMEM] * (3 + len(slabs)), out_spe...]
  transfers between devices with their start and end apart: 35 -> 37, of which waited for: 16 -> 14; matrix products, arithmetic and copies ran while one was open for 2% -> 2% of each run, Pallas kernels for 12% -> 7%
where the time goes in v7:
time: 151 us; the launch traced here: 149 us
  starting transfers between devices  61 us (40%)
  waiting for transfers between devices  46.7 us (31%)
  Pallas kernels  35 us (23%)
  local copies, waits for them, and re-layouts  3.55 us (2%)
  other arithmetic  2.2 us (1%)
    ppermute x33, starting transfers between devices, send(): return lax.ppermute(value, 'img', pairs(dz, dx, dc))  52.5 us
    ppermute x33, waiting for transfers between devices, send(): return lax.ppermute(value, 'img', pairs(dz, dx, dc))  41.6 us
    pallas_call x2, Pallas kernels, insert(): pl.pallas_call(insert_kernel, in_specs=[VMEM] * (3 + len(slabs)), out_spe...  10.8 us
    pallas_call x2, Pallas kernels, partial_sums(): pl.pallas_call(lambda *refs: partial_kernel(z_first, *refs), in_specs=[SM...  9.31 us
    pallas_call x1, Pallas kernels, shifted_images(): pl.pallas_call(shift_kernel, in_specs=[VMEM] * 3, out_specs=[VMEM, VMEM],...  5.49 us
    ppermute x3, starting transfers between devices, exchange_refs(): lax.ppermute(value, 'ref', [(r, (r + k) % REFS) for r in range(REFS)])  4.94 us
    pallas_call x1, Pallas kernels, score_first(): pl.pallas_call(score_first_kernel, in_specs=[SMEM, SMEM] + [VMEM] * (Z +...  4.77 us
    pallas_call x1, Pallas kernels, score_rest(): pl.pallas_call(score_rest_kernel, in_specs=[SMEM, SMEM] + [VMEM] * (Z + 9...  4.24 us
  transfers between devices with their start and end apart: 37, of which 14 were waited for; matrix products, arithmetic and copies ran while one was open for 2% of the time, Pallas kernels for 7%

profile of v7, /device:TPU:8, one launch (start us, length us, event | category | flops | bytes accessed | tf_op | source)
XLA Modules:
  0.0 149.4 jit_solution(3929367163860137497)
XLA Ops:
  10.5 5.9 %collective-permute-start.3 = (bf16[2,8,11904]{2,1,0:T(8,128)(2,1)S(1)}, bf16[2,8,11904]{2,1,0:T(8,128)(2,1)S(1)}, u32[]{:S(2)}, u32[]{:S(2)}) collective-permute-start(bf16[2,8,11904]{2,1,0:T(8,128)(2,1)S(1)} %assemble.1.refs_0_), channel_id=1, source_target_pairs={{0,224},{4,228},{8,232},{12,236},{16,240},{20,244},{24,248},{28,25... | collective-permute-start | bytes 1142792 | tf_op jit(solution)/shard_map/ppermute | solution.py:459
  16.4 7.9 %collective-permute-done.3.refs_1_ = bf16[2,8,11904]{2,1,0:T(8,128)(2,1)S(1)} collective-permute-done((bf16[2,8,11904]{2,1,0:T(8,128)(2,1)S(1)}, bf16[2,8,11904]{2,1,0:T(8,128)(2,1)S(1)}, u32[]{:S(2)}, u32[]{:S(2)}) %collective-permute-start.3) | collective-permute-done | bytes 380960 | tf_op jit(solution)/shard_map/ppermute | solution.py:459
  24.3 3.7 %collective-permute-start.4 = (bf16[2,8,11904]{2,1,0:T(8,128)(2,1)S(1)}, bf16[2,8,11904]{2,1,0:T(8,128)(2,1)S(1)}, u32[]{:S(2)}, u32[]{:S(2)}) collective-permute-start(bf16[2,8,11904]{2,1,0:T(8,128)(2,1)S(1)} %collective-permute-done.3.refs_1_), channel_id=1, source_target_pairs={{0,224},{4,228},{8,232},{12,236},{16,240},{20,244},{24,248},{28,25... | collective-permute-start | bytes 1142792 | tf_op jit(solution)/shard_map/ppermute | solution.py:459
  28.0 7.0 %collective-permute-done.4.refs_2_ = bf16[2,8,11904]{2,1,0:T(8,128)(2,1)S(1)} collective-permute-done((bf16[2,8,11904]{2,1,0:T(8,128)(2,1)S(1)}, bf16[2,8,11904]{2,1,0:T(8,128)(2,1)S(1)}, u32[]{:S(2)}, u32[]{:S(2)}) %collective-permute-start.4) | collective-permute-done | bytes 380960 | tf_op jit(solution)/shard_map/ppermute | solution.py:459
  35.1 3.7 %collective-permute-start.5 = (bf16[2,8,11904]{2,1,0:T(8,128)(2,1)S(1)}, bf16[2,8,11904]{2,1,0:T(8,128)(2,1)S(1)}, u32[]{:S(2)}, u32[]{:S(2)}) collective-permute-start(bf16[2,8,11904]{2,1,0:T(8,128)(2,1)S(1)} %collective-permute-done.4.refs_2_), channel_id=1, source_target_pairs={{0,224},{4,228},{8,232},{12,236},{16,240},{20,244},{24,248},{28,25... | collective-permute-start | bytes 1142792 | tf_op jit(solution)/shard_map/ppermute | solution.py:459
  38.9 6.1 %collective-permute-done.5.refs_0_.refs_3_ = bf16[2,8,11904]{2,1,0:T(8,128)(2,1)S(1)} collective-permute-done((bf16[2,8,11904]{2,1,0:T(8,128)(2,1)S(1)}, bf16[2,8,11904]{2,1,0:T(8,128)(2,1)S(1)}, u32[]{:S(2)}, u32[]{:S(2)}) %collective-permute-start.5) | collective-permute-done | bytes 380960 | tf_op jit(solution)/shard_map/ppermute | solution.py:459
  45.0 3.8 %collective-permute-start.10 = (bf16[2,8,6784]{2,1,0:T(8,128)(2,1)S(1)}, bf16[2,8,6784]{2,1,0:T(8,128)(2,1)S(1)}, u32[]{:S(2)}, u32[]{:S(2)}) collective-permute-start(bf16[2,8,6784]{2,1,0:T(8,128)(2,1)S(1)} %slice.78), channel_id=1, source_target_pairs={{0,224},{4,228},{8,232},{12,236},{16,240},{20,244},{24,248},{28,25... | collective-permute-start | bytes 651272 | tf_op jit(solution)/shard_map/ppermute | solution.py:459
  54.5 5.5 %shift.1 = (bf16[2,5,256,2048]{3,2,1,0:T(8,128)(2,1)S(1)}, bf16[2,5,256,2048]{3,2,1,0:T(8,128)(2,1)S(1)}) custom-call(f32[8,2048]{1,0:T(8,128)S(1)} %copy-done.4, bf16[256,4096]{1,0:T(8,128)(2,1)S(1)} %copy-done.2, bf16[256,4096]{1,0:T(8,128)(2,1)} %collective-permute-done.17.mate_ref), custom_call_target="tpu_custom_call" | custom-call | flops 25165824 | bytes 25165824 | tf_op jit(solution)/shard_map/shift/pallas_call | solution.py:139
  62.8 4.8 %score_first.1.refs_16_ = f32[2,1280,256]{2,1,0:T(8,128)S(1)} custom-call(s32[2,512]{1,0:T(2,128)S(1)} %constant_dynamic-slice_fusion.sig_ref.refs_0_, s32[4]{0:T(128)S(1)} %pad_add_fusion.pos_ref.refs_1_, bf16[2,8,11904]{2,1,0:T(8,128)(2,1)S(1)} %assemble.1.refs_0_, bf16[2,8,11904]{2,1,0:T(8,128)(2,1)S(1)} %collective-permute-done.3.refs_1_, ...), custom_call_target="tpu_custom_call" | custom-call | flops 3355443200 | bytes 16777216 | tf_op jit(solution)/shard_map/score_first/pallas_call | solution.py:193
  67.6 4.2 %score_rest.1 = (f32[2,256,1280]{2,1,0:T(8,128)S(1)}, f32[8,256]{1,0:T(8,128)S(1)}) custom-call(s32[2,512]{1,0:T(2,128)S(1)} %constant_dynamic-slice_fusion.sig_ref.refs_0_, s32[4]{0:T(128)S(1)} %pad_add_fusion.pos_ref.refs_1_, bf16[2,8,11904]{2,1,0:T(8,128)(2,1)S(1)} %assemble.1.refs_0_, bf16[2,8,11904]{2,1,0:T(8,128)(2,1)S(1)} %collective-permute-done.3.refs_1_, ...), custom_call_target="tpu_custom_call" | custom-call | flops 2013265920 | bytes 16777216 | tf_op jit(solution)/shard_map/score_rest/pallas_call | solution.py:256
  79.9 5.9 %partial_first.1 = (f32[64,2560]{1,0:T(8,128)S(1)}, f32[64,2560]{1,0:T(8,128)S(1)}, f32[64,2560]{1,0:T(8,128)S(1)}, f32[64,2560]{1,0:T(8,128)S(1)}, f32[64,2560]...) custom-call(s32[2,512]{1,0:T(2,128)S(1)} %constant_dynamic-slice_fus, ...), custom_call_target="tpu_custom_call" | custom-call | flops 2684354560 | bytes 16777216 | tf_op jit(solution)/shard_map/partial_first/pallas_call | solution.py:368
  85.8 3.4 %partial_rest.1 = (f32[128,1536]{1,0:T(8,128)S(1)}, f32[128,1536]{1,0:T(8,128)S(1)}, f32[128,1536]{1,0:T(8,128)S(1)}, f32[128,1536]{1,0:T(8,128)S(1)}) custom-call(s32[2,512]{1,0:T(2,128)S(1)} %constant_dynamic-slice_fusion.sig_ref.refs_0_, s32[4]{0:T(128)S(1)} %pad_add_fusion.pos_ref.refs_1_, bf16[2,256,1280]{2,1,0:T(8,128)(2,1)S(1)} %get-tuple-element.32.refs_2_, ...), custom_call_target="tpu_custom_call" | custom-call | flops 2684354560 | bytes 16777216 | tf_op jit(solution)/shard_map/partial_rest/pallas_call | solution.py:368
  89.3 3.8 %collective-permute-start.29 = (f16[2,2,8,2560]{3,2,1,0:T(8,128)(2,1)S(1)}, f16[2,2,8,2560]{3,2,1,0:T(8,128)(2,1)S(1)}, u32[]{:S(2)}, u32[]{:S(2)}) collective-permute-start(f16[2,2,8,2560]{3,2,1,0:T(8,128)(2,1)S(1)} %bitcast.56), channel_id=1, source_target_pairs={{0,224},{4,228},{8,232},{12,236},{16,240},{20,244},{24,248},{28,25... | collective-permute-start | bytes 491528 | tf_op jit(solution)/shard_map/ppermute | solution.py:459
  96.8 2.8 %collective-permute-done.25 = f16[2,2,8,2560]{3,2,1,0:T(8,128)(2,1)S(1)} collective-permute-done((f16[2,2,8,2560]{3,2,1,0:T(8,128)(2,1)S(1)}, f16[2,2,8,2560]{3,2,1,0:T(8,128)(2,1)S(1)}, u32[]{:S(2)}, u32[]{:S(2)}) %collective-permute-start.25) | collective-permute-done | bytes 163872 | tf_op jit(solution)/shard_map/ppermute | solution.py:459
  100.0 3.3 %collective-permute-start.30 = (f16[4,2,8,2560]{3,2,1,0:T(8,128)(2,1)S(1)}, f16[4,2,8,2560]{3,2,1,0:T(8,128)(2,1)S(1)}, u32[]{:S(2)}, u32[]{:S(2)}) collective-permute-start(f16[4,2,8,2560]{3,2,1,0:T(8,128)(2,1)S(1)} %pad_maximum_fusion.1), channel_id=1, source_target_pairs={{0,224},{4,228},{8,232},{12,236},{16,240},{20,244},{24,248},{28,25... | collective-permute-start | bytes 983048 | tf_op jit(solution)/shard_map/ppermute | solution.py:459
  103.3 4.8 %collective-permute-done.26 = f16[4,2,8,2560]{3,2,1,0:T(8,128)(2,1)S(1)} collective-permute-done((f16[4,2,8,2560]{3,2,1,0:T(8,128)(2,1)S(1)}, f16[4,2,8,2560]{3,2,1,0:T(8,128)(2,1)S(1)}, u32[]{:S(2)}, u32[]{:S(2)}) %collective-permute-start.26) | collective-permute-done | bytes 327712 | tf_op jit(solution)/shard_map/ppermute | solution.py:459
  108.4 3.3 %collective-permute-start.31 = (f16[4,2,8,2560]{3,2,1,0:T(8,128)(2,1)S(1)}, f16[4,2,8,2560]{3,2,1,0:T(8,128)(2,1)S(1)}, u32[]{:S(2)}, u32[]{:S(2)}) collective-permute-start(f16[4,2,8,2560]{3,2,1,0:T(8,128)(2,1)S(1)} %add_convert_fusion.2), channel_id=1, source_target_pairs={{0,224},{4,228},{8,232},{12,236},{16,240},{20,244},{24,248},{28,25... | collective-permute-start | bytes 983048 | tf_op jit(solution)/shard_map/ppermute | solution.py:459
  111.7 5.3 %collective-permute-done.27 = f16[4,2,8,2560]{3,2,1,0:T(8,128)(2,1)S(1)} collective-permute-done((f16[4,2,8,2560]{3,2,1,0:T(8,128)(2,1)S(1)}, f16[4,2,8,2560]{3,2,1,0:T(8,128)(2,1)S(1)}, u32[]{:S(2)}, u32[]{:S(2)}) %collective-permute-start.27) | collective-permute-done | bytes 327712 | tf_op jit(solution)/shard_map/ppermute | solution.py:459
  117.3 3.6 %collective-permute-start.32 = (f16[4,2,8,2560]{3,2,1,0:T(8,128)(2,1)S(1)}, f16[4,2,8,2560]{3,2,1,0:T(8,128)(2,1)S(1)}, u32[]{:S(2)}, u32[]{:S(2)}) collective-permute-start(f16[4,2,8,2560]{3,2,1,0:T(8,128)(2,1)S(1)} %add_convert_fusion.1), channel_id=1, source_target_pairs={{0,224},{4,228},{8,232},{12,236},{16,240},{20,244},{24,248},{28,25... | collective-permute-start | bytes 983048 | tf_op jit(solution)/shard_map/ppermute | solution.py:459
  121.9 3.6 %all-to-all-start = ((f16[8,2,8,1536]{3,2,1,0:T(8,128)(2,1)}), f16[8,2,8,1536]{3,2,1,0:T(8,128)(2,1)S(1)}, u32[]{:S(2)}, u32[]{:S(2)}) async-start(f16[8,2,8,1536]{3,2,1,0:T(8,128)(2,1)} %add_convert_fusion), calls=%async_computation | async-start | bytes 786432 | tf_op jit(solution)/shard_map/all_to_all | solution.py:463
  125.5 3.6 %collective-permute-done.28 = f16[4,2,8,2560]{3,2,1,0:T(8,128)(2,1)S(1)} collective-permute-done((f16[4,2,8,2560]{3,2,1,0:T(8,128)(2,1)S(1)}, f16[4,2,8,2560]{3,2,1,0:T(8,128)(2,1)S(1)}, u32[]{:S(2)}, u32[]{:S(2)}) %collective-permute-start.28) | collective-permute-done | bytes 327712 | tf_op jit(solution)/shard_map/ppermute | solution.py:459
  134.0 3.3 %all-to-all-done = f16[8,2,8,1536]{3,2,1,0:T(8,128)(2,1)S(1)} async-done(((f16[8,2,8,1536]{3,2,1,0:T(8,128)(2,1)}), f16[8,2,8,1536]{3,2,1,0:T(8,128)(2,1)S(1)}, u32[]{:S(2)}, u32[]{:S(2)}) %all-to-all-start) | async-done | bytes 393248 | tf_op jit(solution)/shard_map/all_to_all | solution.py:463
  138.7 6.5 %insert_first.1 = (f32[32,128]{1,0:T(8,128)S(1)}, f32[32,128]{1,0:T(8,128)S(1)}) custom-call(f32[8,256]{1,0:T(8,128)S(1)} %merge.1.refs_3_.bound_ref, f32[16,2560]{1,0:T(8,128)S(1)} %fusion.3.w_ref, s32[16,2048]{1,0:T(8,128)S(1)} %bitcast.47), custom_call_target="tpu_custom_call" | custom-call | flops 536870912 | bytes 524288 | tf_op jit(solution)/shard_map/insert_first/pallas_call | solution.py:429
  145.2 4.2 %insert_rest.1 = f32[2,4096]{1,0:T(2,128)} custom-call(f32[8,256]{1,0:T(8,128)S(1)} %merge.1.refs_3_.bound_ref, f32[16,1536]{1,0:T(8,128)S(1)} %bitcast.46, s32[16,2048]{1,0:T(8,128)S(1)} %bitcast.48, f32[32,128]{1,0:T(8,128)S(1)} %get-tuple-element.45.refs_0_, f32[32,128]{1,0:T(8,128)S(1)} %get-tuple-element.46.refs_1_), custom_call_target="tpu_custom_call" | custom-call | flops 536870912 | bytes 524288 | tf_op jit(solution)/shard_map/insert_rest/pallas_call | solution.py:429
  (99 shorter events, 38.4 us)
Async XLA Ops:
  0.6 51.5 %collective-permute-start.17 = (bf16[256,4096]{1,0:T(8,128)(2,1)}, bf16[256,4096]{1,0:T(8,128)(2,1)}, u32[]{:S(2)}, u32[]{:S(2)}) collective-permute-start(bf16[256,4096]{1,0:T(8,128)(2,1)} %own_ref.1), channel_id=1, source_target_pairs={{0,4},{4,0},{8,12},{12,8},{16,20},{20,16},{24,28},{28,24},{32,36},... | collective-permute-start | bytes 6291464 | tf_op jit(solution)/shard_map/ppermute | solution.py:459
  1.6 8.5 %collective-permute-start.2 = (bf16[2,8,2560]{2,1,0:T(8,128)(2,1)S(1)}, bf16[2,8,2560]{2,1,0:T(8,128)(2,1)S(1)}, u32[]{:S(2)}, u32[]{:S(2)}) collective-permute-start(bf16[2,8,2560]{2,1,0:T(8,128)(2,1)S(1)} %slice.60.refs_0_), channel_id=1, source_target_pairs={{0,8},{4,12},{8,16},{12,20},{16,24},{20,28},{24,0},{28,4},{32,40},... | collective-permute-start | bytes 245768 | tf_op jit(solution)/shard_map/ppermute | solution.py:459
  10.5 13.8 %collective-permute-start.3 = (bf16[2,8,11904]{2,1,0:T(8,128)(2,1)S(1)}, bf16[2,8,11904]{2,1,0:T(8,128)(2,1)S(1)}, u32[]{:S(2)}, u32[]{:S(2)}) collective-permute-start(bf16[2,8,11904]{2,1,0:T(8,128)(2,1)S(1)} %assemble.1.refs_0_), channel_id=1, source_target_pairs={{0,224},{4,228},{8,232},{12,236},{16,240},{20,244},{24,248},{28,25... | collective-permute-start | bytes 1142792 | tf_op jit(solution)/shard_map/ppermute | solution.py:459
  16.4 11.6 %collective-permute-start.6 = (bf16[2,8,11904]{2,1,0:T(8,128)(2,1)S(1)}, bf16[2,8,11904]{2,1,0:T(8,128)(2,1)S(1)}, u32[]{:S(2)}, u32[]{:S(2)}) collective-permute-start(bf16[2,8,11904]{2,1,0:T(8,128)(2,1)S(1)} %assemble.1.refs_0_), channel_id=1, source_target_pairs={{0,32},{4,36},{8,40},{12,44},{16,48},{20,52},{24,56},{28,60},{32,6... | collective-permute-start | bytes 1142792 | tf_op jit(solution)/shard_map/ppermute | solution.py:459
  24.3 10.7 %collective-permute-start.4 = (bf16[2,8,11904]{2,1,0:T(8,128)(2,1)S(1)}, bf16[2,8,11904]{2,1,0:T(8,128)(2,1)S(1)}, u32[]{:S(2)}, u32[]{:S(2)}) collective-permute-start(bf16[2,8,11904]{2,1,0:T(8,128)(2,1)S(1)} %collective-permute-done.3.refs_1_), channel_id=1, source_target_pairs={{0,224},{4,228},{8,232},{12,236},{16,240},{20,244},{24,248},{28,25... | collective-permute-start | bytes 1142792 | tf_op jit(solution)/shard_map/ppermute | solution.py:459
  28.0 10.7 %collective-permute-start.7 = (bf16[2,8,11904]{2,1,0:T(8,128)(2,1)S(1)}, bf16[2,8,11904]{2,1,0:T(8,128)(2,1)S(1)}, u32[]{:S(2)}, u32[]{:S(2)}) collective-permute-start(bf16[2,8,11904]{2,1,0:T(8,128)(2,1)S(1)} %collective-permute-done.6.refs_4_.refs_7_), channel_id=1, source_target_pairs={{0,32},{4,36},{8,40},{12,44},{16,48},{20,52},{24,56},{28,60},{32,6... | collective-permute-start | bytes 1142792 | tf_op jit(solution)/shard_map/ppermute | solution.py:459
  35.1 9.9 %collective-permute-start.5 = (bf16[2,8,11904]{2,1,0:T(8,128)(2,1)S(1)}, bf16[2,8,11904]{2,1,0:T(8,128)(2,1)S(1)}, u32[]{:S(2)}, u32[]{:S(2)}) collective-permute-start(bf16[2,8,11904]{2,1,0:T(8,128)(2,1)S(1)} %collective-permute-done.4.refs_2_), channel_id=1, source_target_pairs={{0,224},{4,228},{8,232},{12,236},{16,240},{20,244},{24,248},{28,25... | collective-permute-start | bytes 1142792 | tf_op jit(solution)/shard_map/ppermute | solution.py:459
  38.7 10.0 %collective-permute-start.8 = (bf16[2,8,11904]{2,1,0:T(8,128)(2,1)S(1)}, bf16[2,8,11904]{2,1,0:T(8,128)(2,1)S(1)}, u32[]{:S(2)}, u32[]{:S(2)}) collective-permute-start(bf16[2,8,11904]{2,1,0:T(8,128)(2,1)S(1)} %collective-permute-done.7.refs_3_.refs_6_), channel_id=1, source_target_pairs={{0,32},{4,36},{8,40},{12,44},{16,48},{20,52},{24,56},{28,60},{32,6... | collective-permute-start | bytes 1142792 | tf_op jit(solution)/shard_map/ppermute | solution.py:459
  38.8 21.2 %collective-permute-start.13 = (bf16[5,2,8,1664]{3,2,1,0:T(8,128)(2,1)S(1)}, bf16[5,2,8,1664]{3,2,1,0:T(8,128)(2,1)S(1)}, u32[]{:S(2)}, u32[]{:S(2)}) collective-permute-start(bf16[5,2,8,1664]{3,2,1,0:T(8,128)(2,1)S(1)} %pick.2), channel_id=1, source_target_pairs={{0,8},{4,12},{8,16},{12,20},{16,24},{20,28},{24,0},{28,4},{32,40},... | collective-permute-start | bytes 798728 | tf_op jit(solution)/shard_map/ppermute | solution.py:459
  48.7 13.1 %collective-permute-start.9 = (bf16[2,8,5120]{2,1,0:T(8,128)(2,1)S(1)}, bf16[2,8,5120]{2,1,0:T(8,128)(2,1)S(1)}, u32[]{:S(2)}, u32[]{:S(2)}) collective-permute-start(bf16[2,8,5120]{2,1,0:T(8,128)(2,1)S(1)} %slice.77), channel_id=1, source_target_pairs={{0,32},{4,36},{8,40},{12,44},{16,48},{20,52},{24,56},{28,60},{32,6... | collective-permute-start | bytes 491528 | tf_op jit(solution)/shard_map/ppermute | solution.py:459
  48.8 18.7 %collective-permute-start.12 = (bf16[5,2,8,1664]{3,2,1,0:T(8,128)(2,1)S(1)}, bf16[5,2,8,1664]{3,2,1,0:T(8,128)(2,1)S(1)}, u32[]{:S(2)}, u32[]{:S(2)}) collective-permute-start(bf16[5,2,8,1664]{3,2,1,0:T(8,128)(2,1)S(1)} %pick.2), channel_id=1, source_target_pairs={{0,16},{4,20},{8,24},{12,28},{16,0},{20,4},{24,8},{28,12},{32,48},... | collective-permute-start | bytes 798728 | tf_op jit(solution)/shard_map/ppermute | solution.py:459
  52.1 15.4 %collective-permute-start.11 = (bf16[5,2,8,1664]{3,2,1,0:T(8,128)(2,1)S(1)}, bf16[5,2,8,1664]{3,2,1,0:T(8,128)(2,1)S(1)}, u32[]{:S(2)}, u32[]{:S(2)}) collective-permute-start(bf16[5,2,8,1664]{3,2,1,0:T(8,128)(2,1)S(1)} %pick.2), channel_id=1, source_target_pairs={{0,24},{4,28},{8,0},{12,4},{16,8},{20,12},{24,16},{28,20},{32,56},... | collective-permute-start | bytes 798728 | tf_op jit(solution)/shard_map/ppermute | solution.py:459
  52.2 15.4 %collective-permute-start.16 = (bf16[3,2,8,1664]{3,2,1,0:T(8,128)(2,1)S(1)}, bf16[3,2,8,1664]{3,2,1,0:T(8,128)(2,1)S(1)}, u32[]{:S(2)}, u32[]{:S(2)}) collective-permute-start(bf16[3,2,8,1664]{3,2,1,0:T(8,128)(2,1)S(1)} %pick.3), channel_id=1, source_target_pairs={{0,8},{4,12},{8,16},{12,20},{16,24},{20,28},{24,0},{28,4},{32,40},... | collective-permute-start | bytes 479240 | tf_op jit(solution)/shard_map/ppermute | solution.py:459
  89.3 10.5 %collective-permute-start.29 = (f16[2,2,8,2560]{3,2,1,0:T(8,128)(2,1)S(1)}, f16[2,2,8,2560]{3,2,1,0:T(8,128)(2,1)S(1)}, u32[]{:S(2)}, u32[]{:S(2)}) collective-permute-start(f16[2,2,8,2560]{3,2,1,0:T(8,128)(2,1)S(1)} %bitcast.56), channel_id=1, source_target_pairs={{0,224},{4,228},{8,232},{12,236},{16,240},{20,244},{24,248},{28,25... | collective-permute-start | bytes 491528 | tf_op jit(solution)/shard_map/ppermute | solution.py:459
  93.2 27.7 %collective-permute-start.24 = (f16[8,2,8,1536]{3,2,1,0:T(8,128)(2,1)S(1)}, f16[8,2,8,1536]{3,2,1,0:T(8,128)(2,1)S(1)}, u32[]{:S(2)}, u32[]{:S(2)}) collective-permute-start(f16[8,2,8,1536]{3,2,1,0:T(8,128)(2,1)S(1)} %bitcast.55), channel_id=1, source_target_pairs={{0,24},{4,28},{8,0},{12,4},{16,8},{20,12},{24,16},{28,20},{32,56},... | collective-permute-start | bytes 1179656 | tf_op jit(solution)/shard_map/ppermute | solution.py:459
  95.7 25.2 %collective-permute-start.23 = (f16[8,2,8,1536]{3,2,1,0:T(8,128)(2,1)S(1)}, f16[8,2,8,1536]{3,2,1,0:T(8,128)(2,1)S(1)}, u32[]{:S(2)}, u32[]{:S(2)}) collective-permute-start(f16[8,2,8,1536]{3,2,1,0:T(8,128)(2,1)S(1)} %bitcast.54), channel_id=1, source_target_pairs={{0,16},{4,20},{8,24},{12,28},{16,0},{20,4},{24,8},{28,12},{32,48},... | collective-permute-start | bytes 1179656 | tf_op jit(solution)/shard_map/ppermute | solution.py:459
  96.7 24.2 %collective-permute-start.22 = (f16[8,2,8,1536]{3,2,1,0:T(8,128)(2,1)S(1)}, f16[8,2,8,1536]{3,2,1,0:T(8,128)(2,1)S(1)}, u32[]{:S(2)}, u32[]{:S(2)}) collective-permute-start(f16[8,2,8,1536]{3,2,1,0:T(8,128)(2,1)S(1)} %bitcast.53), channel_id=1, source_target_pairs={{0,8},{4,12},{8,16},{12,20},{16,24},{20,28},{24,0},{28,4},{32,40},... | collective-permute-start | bytes 1179656 | tf_op jit(solution)/shard_map/ppermute | solution.py:459
  99.8 8.4 %collective-permute-start.26 = (f16[4,2,8,2560]{3,2,1,0:T(8,128)(2,1)S(1)}, f16[4,2,8,2560]{3,2,1,0:T(8,128)(2,1)S(1)}, u32[]{:S(2)}, u32[]{:S(2)}) collective-permute-start(f16[4,2,8,2560]{3,2,1,0:T(8,128)(2,1)S(1)} %pad_maximum_fusion), channel_id=1, source_target_pairs={{0,32},{4,36},{8,40},{12,44},{16,48},{20,52},{24,56},{28,60},{32,6... | collective-permute-start | bytes 983048 | tf_op jit(solution)/shard_map/ppermute | solution.py:459
  100.0 8.3 %collective-permute-start.30 = (f16[4,2,8,2560]{3,2,1,0:T(8,128)(2,1)S(1)}, f16[4,2,8,2560]{3,2,1,0:T(8,128)(2,1)S(1)}, u32[]{:S(2)}, u32[]{:S(2)}) collective-permute-start(f16[4,2,8,2560]{3,2,1,0:T(8,128)(2,1)S(1)} %pad_maximum_fusion.1), channel_id=1, source_target_pairs={{0,224},{4,228},{8,232},{12,236},{16,240},{20,244},{24,248},{28,25... | collective-permute-start | bytes 983048 | tf_op jit(solution)/shard_map/ppermute | solution.py:459
  108.2 8.8 %collective-permute-start.27 = (f16[4,2,8,2560]{3,2,1,0:T(8,128)(2,1)S(1)}, f16[4,2,8,2560]{3,2,1,0:T(8,128)(2,1)S(1)}, u32[]{:S(2)}, u32[]{:S(2)}) collective-permute-start(f16[4,2,8,2560]{3,2,1,0:T(8,128)(2,1)S(1)} %add_convert_fusion.4), channel_id=1, source_target_pairs={{0,32},{4,36},{8,40},{12,44},{16,48},{20,52},{24,56},{28,60},{32,6... | collective-permute-start | bytes 983048 | tf_op jit(solution)/shard_map/ppermute | solution.py:459
  108.4 8.8 %collective-permute-start.31 = (f16[4,2,8,2560]{3,2,1,0:T(8,128)(2,1)S(1)}, f16[4,2,8,2560]{3,2,1,0:T(8,128)(2,1)S(1)}, u32[]{:S(2)}, u32[]{:S(2)}) collective-permute-start(f16[4,2,8,2560]{3,2,1,0:T(8,128)(2,1)S(1)} %add_convert_fusion.2), channel_id=1, source_target_pairs={{0,224},{4,228},{8,232},{12,236},{16,240},{20,244},{24,248},{28,25... | collective-permute-start | bytes 983048 | tf_op jit(solution)/shard_map/ppermute | solution.py:459
  117.1 12.0 %collective-permute-start.28 = (f16[4,2,8,2560]{3,2,1,0:T(8,128)(2,1)S(1)}, f16[4,2,8,2560]{3,2,1,0:T(8,128)(2,1)S(1)}, u32[]{:S(2)}, u32[]{:S(2)}) collective-permute-start(f16[4,2,8,2560]{3,2,1,0:T(8,128)(2,1)S(1)} %add_convert_fusion.3), channel_id=1, source_target_pairs={{0,32},{4,36},{8,40},{12,44},{16,48},{20,52},{24,56},{28,60},{32,6... | collective-permute-start | bytes 983048 | tf_op jit(solution)/shard_map/ppermute | solution.py:459
  117.3 11.8 %collective-permute-start.32 = (f16[4,2,8,2560]{3,2,1,0:T(8,128)(2,1)S(1)}, f16[4,2,8,2560]{3,2,1,0:T(8,128)(2,1)S(1)}, u32[]{:S(2)}, u32[]{:S(2)}) collective-permute-start(f16[4,2,8,2560]{3,2,1,0:T(8,128)(2,1)S(1)} %add_convert_fusion.1), channel_id=1, source_target_pairs={{0,224},{4,228},{8,232},{12,236},{16,240},{20,244},{24,248},{28,25... | collective-permute-start | bytes 983048 | tf_op jit(solution)/shard_map/ppermute | solution.py:459
  121.9 15.4 %all-to-all-start = ((f16[8,2,8,1536]{3,2,1,0:T(8,128)(2,1)}), f16[8,2,8,1536]{3,2,1,0:T(8,128)(2,1)S(1)}, u32[]{:S(2)}, u32[]{:S(2)}) async-start(f16[8,2,8,1536]{3,2,1,0:T(8,128)(2,1)} %add_convert_fusion), calls=%async_computation | async-start | bytes 786432 | tf_op jit(solution)/shard_map/all_to_all | solution.py:463
  (19 other events, 191.0 us)

commit v8 on v7

--- a/solution.py
+++ b/solution.py
@@ -28,6 +28,9 @@
 UNIT = REST + EXTRA
 FAR = 2 * SPLIT
 MESSAGE = X * SPLIT + UNIT
+FIRST = 2304
+OTHERS = FEATURES - FIRST
+EDGE = FIRST - PIX
 EARLY = (0, 1, 2, 6, 7)
 LATE = (3, 4, 5)
 
@@ -353,15 +356,15 @@
 
     if z_first:
         pl.loop(0, PIX // PTILE)(lambda i: one_tile(re_ref, i * PTILE, i * PTILE, PTILE))
-        one_tile(im_ref, 0, PIX, BORDER)
+        one_tile(im_ref, 0, PIX, EDGE)
     else:
-        half = REST // 2
-        pl.loop(0, 2)(lambda i: one_tile(im_ref, BORDER + i * half, i * half, half))
+        half = OTHERS // 2
+        pl.loop(0, 2)(lambda i: one_tile(im_ref, EDGE + i * half, i * half, half))
 
 
 def partial_sums(z_first, sig, pos, weights, *images):
     many, rows = (Z, X * 16) if z_first else (X, Z * 16)
-    out_shape = [pltpu.VMEM((rows, SPLIT if z_first else REST), jnp.float32)] * many
+    out_shape = [pltpu.VMEM((rows, FIRST if z_first else OTHERS), jnp.float32)] * many
     if z_first:
         out_shape.append(pltpu.VMEM((2, COLS, ROWS), jnp.bfloat16))
         out_shape.append(jax.ShapeDtypeStruct((1, N), jnp.float32))
@@ -403,8 +406,8 @@
     empty = jnp.zeros((2 * HIGH, LOW), jnp.float32)
     if len(refs) == 3:
         re_ref, im_ref, out_ref = refs
-        step = lambda i, acc: add(acc, i, slice(0, REST), slice(BORDER, PIX), REST)
-        acc = lax.fori_loop(0, 16, step, empty, unroll=2)
+        step = lambda i, acc: add(acc, i, slice(0, OTHERS), slice(EDGE, PIX), OTHERS)
+        acc = lax.fori_loop(0, 16, step, empty, unroll=4)
         slab = im_ref[...] + acc[:HIGH] + acc[HIGH:]
         for h in range(HIGH):
             at = slice(h * LOW, (h + 1) * LOW)
@@ -416,10 +419,10 @@
         def step(i, both):
             re, im = both
             re = add(re, i, slice(0, PIX), slice(0, PIX), PIX)
-            im = add(im, i, slice(PIX, SPLIT), slice(0, BORDER), BORDER)
+            im = add(im, i, slice(PIX, FIRST), slice(0, EDGE), EDGE)
             return re, im
 
-        re, im = lax.fori_loop(0, 16, step, (empty, empty))
+        re, im = lax.fori_loop(0, 16, step, (empty, empty), unroll=2)
         re_ref[...] = re[:HIGH] + re[HIGH:]
         im_ref[...] = im[:HIGH] + im[HIGH:]
 
@@ -495,17 +498,17 @@
 
 
 def scatter_z_first(parts):
-    far, cut = parts[Z // 2], X // 2
-    behind = send(narrow(far[:cut]), dz=1)
-    ahead = send(narrow(far[cut:]), dz=-1)
-    behind = jnp.concatenate([parts[3][:cut] + wide(behind), parts[3][cut:]])
-    ahead = jnp.concatenate([parts[5][:cut], parts[5][cut:] + wide(ahead)])
-    for k in range(3, 0, -1):
-        behind = send(narrow(behind), dz=1)
-        ahead = send(narrow(ahead), dz=-1)
-        if k > 1:
-            behind = parts[k - 1] + wide(behind)
-            ahead = parts[Z - k + 1] + wide(ahead)
+    half = Z // 2
+    behind = narrow(parts[half])
+    for k in range(half, 0, -1):
+        if k < half:
+            behind = narrow(parts[k] + wide(behind))
+        behind = send(behind, dz=1)
+    ahead = narrow(parts[half + 1])
+    for k in range(half - 1, 0, -1):
+        if k < half - 1:
+            ahead = narrow(parts[Z - k] + wide(ahead))
+        ahead = send(ahead, dz=-1)
     row = parts[0] + wide(behind) + wide(ahead)
     arrived = [send(narrow(row[k]), dx=k) for k in range(1, X)]
     return row[0] + wide(arrived[0]) + wide(arrived[1]) + wide(arrived[2])
@@ -544,8 +547,8 @@
     every = exchange_refs(merged)
     *sums, weights, evidence = partial_sums(True, sig, pos, (scores, *every), *shifted)
     sums_rest = partial_sums(False, sig, pos, (weights, merged), shifted[1])
-    total = scatter_z_first([v.reshape(X, 2, 8, SPLIT) for v in sums])
-    total_rest = scatter_x_first([v.reshape(Z, 2, 8, REST) for v in sums_rest])
+    total = scatter_z_first([v.reshape(X, 2, 8, FIRST) for v in sums])
+    total_rest = scatter_x_first([v.reshape(Z, 2, 8, OTHERS) for v in sums_rest])
     ids = insertion.reshape(16, PIX)
     slabs = insert(merged, total, ids)
     volume = insert(merged, total_rest, ids, *slabs)

time: 151 us -> 164 us (1.086)
  waiting for transfers between devices: 46.7 us -> 67 us
  starting transfers between devices: 61 us -> 57 us
    ppermute x33 -> x32, waiting for transfers between devices: 41.6 us -> 55.2 us  [send(): return lax.ppermute(value, 'img', pairs(dz, dx, dc))]
    all_to_all x1, waiting for transfers between devices: 3.31 us -> 9.94 us  [all_to_all_z(): lax.all_to_all(value, 'img', split_axis=0, concat_axis=0, tiled=True, axi...]
    ppermute x33 -> x32, starting transfers between devices: 52.5 us -> 47.6 us  [send(): return lax.ppermute(value, 'img', pairs(dz, dx, dc))]
    pallas_call x2, Pallas kernels: 10.8 us -> 8.55 us  [insert(): pl.pallas_call(insert_kernel, in_specs=[VMEM] * (3 + len(slabs)), out_spe...]
  transfers between devices with their start and end apart: 37 -> 36, of which waited for: 14 -> 15; matrix products, arithmetic and copies ran while one was open for 2% -> 2% of each run, Pallas kernels for 7% -> 12%
where the time goes in v8:
time: 164 us
  waiting for transfers between devices  67 us (41%)
  starting transfers between devices  57 us (35%)
  Pallas kernels  33.4 us (20%)
  local copies, waits for them, and re-layouts  3.49 us (2%)
  other arithmetic  1.96 us (1%)
    ppermute x32, waiting for transfers between devices, send(): return lax.ppermute(value, 'img', pairs(dz, dx, dc))  55.2 us
    ppermute x32, starting transfers between devices, send(): return lax.ppermute(value, 'img', pairs(dz, dx, dc))  47.6 us
    pallas_call x2, Pallas kernels, partial_sums(): pl.pallas_call(lambda *refs: partial_kernel(z_first, *refs), in_specs=[SM...  9.96 us
    all_to_all x1, waiting for transfers between devices, all_to_all_z(): lax.all_to_all(value, 'img', split_axis=0, concat_axis=0, tiled=True, axi...  9.94 us
    pallas_call x2, Pallas kernels, insert(): pl.pallas_call(insert_kernel, in_specs=[VMEM] * (3 + len(slabs)), out_spe...  8.55 us
    pallas_call x1, Pallas kernels, shifted_images(): pl.pallas_call(shift_kernel, in_specs=[VMEM] * 3, out_specs=[VMEM, VMEM],...  5.49 us
    ppermute x3, starting transfers between devices, exchange_refs(): lax.ppermute(value, 'ref', [(r, (r + k) % REFS) for r in range(REFS)])  4.94 us
    pallas_call x1, Pallas kernels, score_first(): pl.pallas_call(score_first_kernel, in_specs=[SMEM, SMEM] + [VMEM] * (Z +...  4.77 us
  transfers between devices with their start and end apart: 36, of which 15 were waited for; matrix products, arithmetic and copies ran while one was open for 2% of the time, Pallas kernels for 12%

profile of v8, /device:TPU:8, one launch (start us, length us, event | category | flops | bytes accessed | tf_op | source)
XLA Modules:
  0.0 163.8 jit_solution(15142830727019137434)
XLA Ops:
  10.5 5.9 %collective-permute-start.3 = (bf16[2,8,11904]{2,1,0:T(8,128)(2,1)S(1)}, bf16[2,8,11904]{2,1,0:T(8,128)(2,1)S(1)}, u32[]{:S(2)}, u32[]{:S(2)}) collective-permute-start(bf16[2,8,11904]{2,1,0:T(8,128)(2,1)S(1)} %assemble.1.refs_0_), channel_id=1, source_target_pairs={{0,224},{4,228},{8,232},{12,236},{16,240},{20,244},{24,248},{28,25... | collective-permute-start | bytes 1142792 | tf_op jit(solution)/shard_map/ppermute | solution.py:462
  16.4 7.9 %collective-permute-done.3.refs_1_ = bf16[2,8,11904]{2,1,0:T(8,128)(2,1)S(1)} collective-permute-done((bf16[2,8,11904]{2,1,0:T(8,128)(2,1)S(1)}, bf16[2,8,11904]{2,1,0:T(8,128)(2,1)S(1)}, u32[]{:S(2)}, u32[]{:S(2)}) %collective-permute-start.3) | collective-permute-done | bytes 380960 | tf_op jit(solution)/shard_map/ppermute | solution.py:462
  24.3 3.7 %collective-permute-start.4 = (bf16[2,8,11904]{2,1,0:T(8,128)(2,1)S(1)}, bf16[2,8,11904]{2,1,0:T(8,128)(2,1)S(1)}, u32[]{:S(2)}, u32[]{:S(2)}) collective-permute-start(bf16[2,8,11904]{2,1,0:T(8,128)(2,1)S(1)} %collective-permute-done.3.refs_1_), channel_id=1, source_target_pairs={{0,224},{4,228},{8,232},{12,236},{16,240},{20,244},{24,248},{28,25... | collective-permute-start | bytes 1142792 | tf_op jit(solution)/shard_map/ppermute | solution.py:462
  28.0 7.0 %collective-permute-done.4.refs_2_ = bf16[2,8,11904]{2,1,0:T(8,128)(2,1)S(1)} collective-permute-done((bf16[2,8,11904]{2,1,0:T(8,128)(2,1)S(1)}, bf16[2,8,11904]{2,1,0:T(8,128)(2,1)S(1)}, u32[]{:S(2)}, u32[]{:S(2)}) %collective-permute-start.4) | collective-permute-done | bytes 380960 | tf_op jit(solution)/shard_map/ppermute | solution.py:462
  35.1 3.7 %collective-permute-start.5 = (bf16[2,8,11904]{2,1,0:T(8,128)(2,1)S(1)}, bf16[2,8,11904]{2,1,0:T(8,128)(2,1)S(1)}, u32[]{:S(2)}, u32[]{:S(2)}) collective-permute-start(bf16[2,8,11904]{2,1,0:T(8,128)(2,1)S(1)} %collective-permute-done.4.refs_2_), channel_id=1, source_target_pairs={{0,224},{4,228},{8,232},{12,236},{16,240},{20,244},{24,248},{28,25... | collective-permute-start | bytes 1142792 | tf_op jit(solution)/shard_map/ppermute | solution.py:462
  38.9 6.1 %collective-permute-done.5.refs_0_.refs_3_ = bf16[2,8,11904]{2,1,0:T(8,128)(2,1)S(1)} collective-permute-done((bf16[2,8,11904]{2,1,0:T(8,128)(2,1)S(1)}, bf16[2,8,11904]{2,1,0:T(8,128)(2,1)S(1)}, u32[]{:S(2)}, u32[]{:S(2)}) %collective-permute-start.5) | collective-permute-done | bytes 380960 | tf_op jit(solution)/shard_map/ppermute | solution.py:462
  45.0 3.8 %collective-permute-start.10 = (bf16[2,8,6784]{2,1,0:T(8,128)(2,1)S(1)}, bf16[2,8,6784]{2,1,0:T(8,128)(2,1)S(1)}, u32[]{:S(2)}, u32[]{:S(2)}) collective-permute-start(bf16[2,8,6784]{2,1,0:T(8,128)(2,1)S(1)} %slice.32), channel_id=1, source_target_pairs={{0,224},{4,228},{8,232},{12,236},{16,240},{20,244},{24,248},{28,25... | collective-permute-start | bytes 651272 | tf_op jit(solution)/shard_map/ppermute | solution.py:462
  54.5 5.5 %shift.1 = (bf16[2,5,256,2048]{3,2,1,0:T(8,128)(2,1)S(1)}, bf16[2,5,256,2048]{3,2,1,0:T(8,128)(2,1)S(1)}) custom-call(f32[8,2048]{1,0:T(8,128)S(1)} %copy-done.4, bf16[256,4096]{1,0:T(8,128)(2,1)S(1)} %copy-done.2, bf16[256,4096]{1,0:T(8,128)(2,1)} %collective-permute-done.17.mate_ref), custom_call_target="tpu_custom_call" | custom-call | flops 25165824 | bytes 25165824 | tf_op jit(solution)/shard_map/shift/pallas_call | solution.py:142
  62.8 4.8 %score_first.1.refs_16_ = f32[2,1280,256]{2,1,0:T(8,128)S(1)} custom-call(s32[2,512]{1,0:T(2,128)S(1)} %constant_dynamic-slice_fusion.sig_ref.refs_0_, s32[4]{0:T(128)S(1)} %pad_add_fusion.pos_ref.refs_1_, bf16[2,8,11904]{2,1,0:T(8,128)(2,1)S(1)} %assemble.1.refs_0_, bf16[2,8,11904]{2,1,0:T(8,128)(2,1)S(1)} %collective-permute-done.3.refs_1_, ...), custom_call_target="tpu_custom_call" | custom-call | flops 3355443200 | bytes 16777216 | tf_op jit(solution)/shard_map/score_first/pallas_call | solution.py:196
  67.6 4.2 %score_rest.1 = (f32[2,256,1280]{2,1,0:T(8,128)S(1)}, f32[8,256]{1,0:T(8,128)S(1)}) custom-call(s32[2,512]{1,0:T(2,128)S(1)} %constant_dynamic-slice_fusion.sig_ref.refs_0_, s32[4]{0:T(128)S(1)} %pad_add_fusion.pos_ref.refs_1_, bf16[2,8,11904]{2,1,0:T(8,128)(2,1)S(1)} %assemble.1.refs_0_, bf16[2,8,11904]{2,1,0:T(8,128)(2,1)S(1)} %collective-permute-done.3.refs_1_, ...), custom_call_target="tpu_custom_call" | custom-call | flops 2013265920 | bytes 16777216 | tf_op jit(solution)/shard_map/score_rest/pallas_call | solution.py:259
  79.9 5.8 %partial_first.1 = (f32[64,2304]{1,0:T(8,128)S(1)}, f32[64,2304]{1,0:T(8,128)S(1)}, f32[64,2304]{1,0:T(8,128)S(1)}, f32[64,2304]{1,0:T(8,128)S(1)}, f32[64,2304]...) custom-call(s32[2,512]{1,0:T(2,128)S(1)} %constant_dynamic-slice_fus, ...), custom_call_target="tpu_custom_call" | custom-call | flops 2684354560 | bytes 16777216 | tf_op jit(solution)/shard_map/partial_first/pallas_call | solution.py:371
  85.9 3.8 %collective-permute-start.29 = (f16[4,2,8,2304]{3,2,1,0:T(8,128)(2,1)S(1)}, f16[4,2,8,2304]{3,2,1,0:T(8,128)(2,1)S(1)}, u32[]{:S(2)}, u32[]{:S(2)}) collective-permute-start(f16[4,2,8,2304]{3,2,1,0:T(8,128)(2,1)S(1)} %bitcast.50), channel_id=1, source_target_pairs={{0,224},{4,228},{8,232},{12,236},{16,240},{20,244},{24,248},{28,25... | collective-permute-start | bytes 884744 | tf_op jit(solution)/shard_map/ppermute | solution.py:462
  89.6 5.8 %collective-permute-done.25 = f16[4,2,8,2304]{3,2,1,0:T(8,128)(2,1)S(1)} collective-permute-done((f16[4,2,8,2304]{3,2,1,0:T(8,128)(2,1)S(1)}, f16[4,2,8,2304]{3,2,1,0:T(8,128)(2,1)S(1)}, u32[]{:S(2)}, u32[]{:S(2)}) %collective-permute-start.25) | collective-permute-done | bytes 294944 | tf_op jit(solution)/shard_map/ppermute | solution.py:462
  95.7 3.5 %collective-permute-start.30 = (f16[4,2,8,2304]{3,2,1,0:T(8,128)(2,1)S(1)}, f16[4,2,8,2304]{3,2,1,0:T(8,128)(2,1)S(1)}, u32[]{:S(2)}, u32[]{:S(2)}) collective-permute-start(f16[4,2,8,2304]{3,2,1,0:T(8,128)(2,1)S(1)} %add_convert_fusion.2), channel_id=1, source_target_pairs={{0,224},{4,228},{8,232},{12,236},{16,240},{20,244},{24,248},{28,25... | collective-permute-start | bytes 884744 | tf_op jit(solution)/shard_map/ppermute | solution.py:462
  99.2 4.7 %collective-permute-done.26 = f16[4,2,8,2304]{3,2,1,0:T(8,128)(2,1)S(1)} collective-permute-done((f16[4,2,8,2304]{3,2,1,0:T(8,128)(2,1)S(1)}, f16[4,2,8,2304]{3,2,1,0:T(8,128)(2,1)S(1)}, u32[]{:S(2)}, u32[]{:S(2)}) %collective-permute-start.26) | collective-permute-done | bytes 294944 | tf_op jit(solution)/shard_map/ppermute | solution.py:462
  104.1 3.3 %collective-permute-start.31 = (f16[4,2,8,2304]{3,2,1,0:T(8,128)(2,1)S(1)}, f16[4,2,8,2304]{3,2,1,0:T(8,128)(2,1)S(1)}, u32[]{:S(2)}, u32[]{:S(2)}) collective-permute-start(f16[4,2,8,2304]{3,2,1,0:T(8,128)(2,1)S(1)} %add_convert_fusion.1), channel_id=1, source_target_pairs={{0,224},{4,228},{8,232},{12,236},{16,240},{20,244},{24,248},{28,25... | collective-permute-start | bytes 884744 | tf_op jit(solution)/shard_map/ppermute | solution.py:462
  107.4 4.5 %collective-permute-done.27 = f16[4,2,8,2304]{3,2,1,0:T(8,128)(2,1)S(1)} collective-permute-done((f16[4,2,8,2304]{3,2,1,0:T(8,128)(2,1)S(1)}, f16[4,2,8,2304]{3,2,1,0:T(8,128)(2,1)S(1)}, u32[]{:S(2)}, u32[]{:S(2)}) %collective-permute-start.27) | collective-permute-done | bytes 294944 | tf_op jit(solution)/shard_map/ppermute | solution.py:462
  112.1 4.2 %partial_rest.1 = (f32[128,1792]{1,0:T(8,128)S(1)}, f32[128,1792]{1,0:T(8,128)S(1)}, f32[128,1792]{1,0:T(8,128)S(1)}, f32[128,1792]{1,0:T(8,128)S(1)}) custom-call(s32[2,512]{1,0:T(2,128)S(1)} %constant_dynamic-slice_fusion.sig_ref.refs_0_, s32[4]{0:T(128)S(1)} %pad_add_fusion.pos_ref.refs_1_, bf16[2,256,1280]{2,1,0:T(8,128)(2,1)S(1)} %get-tuple-element.32.refs_2_, ...), custom_call_target="tpu_custom_call" | custom-call | flops 2684354560 | bytes 16777216 | tf_op jit(solution)/shard_map/partial_rest/pallas_call | solution.py:371
  123.5 12.6 %collective-permute-done.24 = f16[8,2,8,1792]{3,2,1,0:T(8,128)(2,1)S(1)} collective-permute-done((f16[8,2,8,1792]{3,2,1,0:T(8,128)(2,1)S(1)}, f16[8,2,8,1792]{3,2,1,0:T(8,128)(2,1)S(1)}, u32[]{:S(2)}, u32[]{:S(2)}) %collective-permute-start.24) | collective-permute-done | bytes 458784 | tf_op jit(solution)/shard_map/ppermute | solution.py:462
  136.2 3.4 %collective-permute-done.22 = f16[8,2,8,1792]{3,2,1,0:T(8,128)(2,1)S(1)} collective-permute-done((f16[8,2,8,1792]{3,2,1,0:T(8,128)(2,1)S(1)}, f16[8,2,8,1792]{3,2,1,0:T(8,128)(2,1)S(1)}, u32[]{:S(2)}, u32[]{:S(2)}) %collective-permute-start.22) | collective-permute-done | bytes 458784 | tf_op jit(solution)/shard_map/ppermute | solution.py:462
  140.7 4.5 %all-to-all-start = ((f16[8,2,8,1792]{3,2,1,0:T(8,128)(2,1)}), f16[8,2,8,1792]{3,2,1,0:T(8,128)(2,1)S(1)}, u32[]{:S(2)}, u32[]{:S(2)}) async-start(f16[8,2,8,1792]{3,2,1,0:T(8,128)(2,1)} %add_convert_fusion), calls=%async_computation | async-start | bytes 917504 | tf_op jit(solution)/shard_map/all_to_all | solution.py:466
  145.2 4.7 %insert_first.1 = (f32[32,128]{1,0:T(8,128)S(1)}, f32[32,128]{1,0:T(8,128)S(1)}) custom-call(f32[8,256]{1,0:T(8,128)S(1)} %merge.1.refs_3_.bound_ref, f32[16,2304]{1,0:T(8,128)S(1)} %fusion.3.w_ref, s32[16,2048]{1,0:T(8,128)S(1)} %bitcast.45), custom_call_target="tpu_custom_call" | custom-call | flops 536870912 | bytes 524288 | tf_op jit(solution)/shard_map/insert_first/pallas_call | solution.py:432
  149.9 9.9 %all-to-all-done = f16[8,2,8,1792]{3,2,1,0:T(8,128)(2,1)S(1)} async-done(((f16[8,2,8,1792]{3,2,1,0:T(8,128)(2,1)}), f16[8,2,8,1792]{3,2,1,0:T(8,128)(2,1)S(1)}, u32[]{:S(2)}, u32[]{:S(2)}) %all-to-all-start) | async-done | bytes 458784 | tf_op jit(solution)/shard_map/all_to_all | solution.py:466
  159.9 3.8 %insert_rest.1 = f32[2,4096]{1,0:T(2,128)} custom-call(f32[8,256]{1,0:T(8,128)S(1)} %merge.1.refs_3_.bound_ref, f32[16,1792]{1,0:T(8,128)S(1)} %bitcast.44, s32[16,2048]{1,0:T(8,128)S(1)} %bitcast.46, f32[32,128]{1,0:T(8,128)S(1)} %get-tuple-element.45.refs_0_, f32[32,128]{1,0:T(8,128)S(1)} %get-tuple-element.46.refs_1_), custom_call_target="tpu_custom_call" | custom-call | flops 536870912 | bytes 524288 | tf_op jit(solution)/shard_map/insert_rest/pallas_call | solution.py:432
  (92 shorter events, 35.7 us)
Async XLA Ops:
  0.6 51.5 %collective-permute-start.17 = (bf16[256,4096]{1,0:T(8,128)(2,1)}, bf16[256,4096]{1,0:T(8,128)(2,1)}, u32[]{:S(2)}, u32[]{:S(2)}) collective-permute-start(bf16[256,4096]{1,0:T(8,128)(2,1)} %own_ref.1), channel_id=1, source_target_pairs={{0,4},{4,0},{8,12},{12,8},{16,20},{20,16},{24,28},{28,24},{32,36},... | collective-permute-start | bytes 6291464 | tf_op jit(solution)/shard_map/ppermute | solution.py:462
  1.6 8.5 %collective-permute-start.2 = (bf16[2,8,2560]{2,1,0:T(8,128)(2,1)S(1)}, bf16[2,8,2560]{2,1,0:T(8,128)(2,1)S(1)}, u32[]{:S(2)}, u32[]{:S(2)}) collective-permute-start(bf16[2,8,2560]{2,1,0:T(8,128)(2,1)S(1)} %slice.24.refs_0_), channel_id=1, source_target_pairs={{0,8},{4,12},{8,16},{12,20},{16,24},{20,28},{24,0},{28,4},{32,40},... | collective-permute-start | bytes 245768 | tf_op jit(solution)/shard_map/ppermute | solution.py:462
  10.5 13.8 %collective-permute-start.3 = (bf16[2,8,11904]{2,1,0:T(8,128)(2,1)S(1)}, bf16[2,8,11904]{2,1,0:T(8,128)(2,1)S(1)}, u32[]{:S(2)}, u32[]{:S(2)}) collective-permute-start(bf16[2,8,11904]{2,1,0:T(8,128)(2,1)S(1)} %assemble.1.refs_0_), channel_id=1, source_target_pairs={{0,224},{4,228},{8,232},{12,236},{16,240},{20,244},{24,248},{28,25... | collective-permute-start | bytes 1142792 | tf_op jit(solution)/shard_map/ppermute | solution.py:462
  16.4 11.6 %collective-permute-start.6 = (bf16[2,8,11904]{2,1,0:T(8,128)(2,1)S(1)}, bf16[2,8,11904]{2,1,0:T(8,128)(2,1)S(1)}, u32[]{:S(2)}, u32[]{:S(2)}) collective-permute-start(bf16[2,8,11904]{2,1,0:T(8,128)(2,1)S(1)} %assemble.1.refs_0_), channel_id=1, source_target_pairs={{0,32},{4,36},{8,40},{12,44},{16,48},{20,52},{24,56},{28,60},{32,6... | collective-permute-start | bytes 1142792 | tf_op jit(solution)/shard_map/ppermute | solution.py:462
  24.3 10.7 %collective-permute-start.4 = (bf16[2,8,11904]{2,1,0:T(8,128)(2,1)S(1)}, bf16[2,8,11904]{2,1,0:T(8,128)(2,1)S(1)}, u32[]{:S(2)}, u32[]{:S(2)}) collective-permute-start(bf16[2,8,11904]{2,1,0:T(8,128)(2,1)S(1)} %collective-permute-done.3.refs_1_), channel_id=1, source_target_pairs={{0,224},{4,228},{8,232},{12,236},{16,240},{20,244},{24,248},{28,25... | collective-permute-start | bytes 1142792 | tf_op jit(solution)/shard_map/ppermute | solution.py:462
  28.0 10.7 %collective-permute-start.7 = (bf16[2,8,11904]{2,1,0:T(8,128)(2,1)S(1)}, bf16[2,8,11904]{2,1,0:T(8,128)(2,1)S(1)}, u32[]{:S(2)}, u32[]{:S(2)}) collective-permute-start(bf16[2,8,11904]{2,1,0:T(8,128)(2,1)S(1)} %collective-permute-done.6.refs_4_.refs_7_), channel_id=1, source_target_pairs={{0,32},{4,36},{8,40},{12,44},{16,48},{20,52},{24,56},{28,60},{32,6... | collective-permute-start | bytes 1142792 | tf_op jit(solution)/shard_map/ppermute | solution.py:462
  35.1 9.9 %collective-permute-start.5 = (bf16[2,8,11904]{2,1,0:T(8,128)(2,1)S(1)}, bf16[2,8,11904]{2,1,0:T(8,128)(2,1)S(1)}, u32[]{:S(2)}, u32[]{:S(2)}) collective-permute-start(bf16[2,8,11904]{2,1,0:T(8,128)(2,1)S(1)} %collective-permute-done.4.refs_2_), channel_id=1, source_target_pairs={{0,224},{4,228},{8,232},{12,236},{16,240},{20,244},{24,248},{28,25... | collective-permute-start | bytes 1142792 | tf_op jit(solution)/shard_map/ppermute | solution.py:462
  38.7 10.0 %collective-permute-start.8 = (bf16[2,8,11904]{2,1,0:T(8,128)(2,1)S(1)}, bf16[2,8,11904]{2,1,0:T(8,128)(2,1)S(1)}, u32[]{:S(2)}, u32[]{:S(2)}) collective-permute-start(bf16[2,8,11904]{2,1,0:T(8,128)(2,1)S(1)} %collective-permute-done.7.refs_3_.refs_6_), channel_id=1, source_target_pairs={{0,32},{4,36},{8,40},{12,44},{16,48},{20,52},{24,56},{28,60},{32,6... | collective-permute-start | bytes 1142792 | tf_op jit(solution)/shard_map/ppermute | solution.py:462
  38.8 21.2 %collective-permute-start.13 = (bf16[5,2,8,1664]{3,2,1,0:T(8,128)(2,1)S(1)}, bf16[5,2,8,1664]{3,2,1,0:T(8,128)(2,1)S(1)}, u32[]{:S(2)}, u32[]{:S(2)}) collective-permute-start(bf16[5,2,8,1664]{3,2,1,0:T(8,128)(2,1)S(1)} %pick.2), channel_id=1, source_target_pairs={{0,8},{4,12},{8,16},{12,20},{16,24},{20,28},{24,0},{28,4},{32,40},... | collective-permute-start | bytes 798728 | tf_op jit(solution)/shard_map/ppermute | solution.py:462
  48.7 13.1 %collective-permute-start.9 = (bf16[2,8,5120]{2,1,0:T(8,128)(2,1)S(1)}, bf16[2,8,5120]{2,1,0:T(8,128)(2,1)S(1)}, u32[]{:S(2)}, u32[]{:S(2)}) collective-permute-start(bf16[2,8,5120]{2,1,0:T(8,128)(2,1)S(1)} %slice.31), channel_id=1, source_target_pairs={{0,32},{4,36},{8,40},{12,44},{16,48},{20,52},{24,56},{28,60},{32,6... | collective-permute-start | bytes 491528 | tf_op jit(solution)/shard_map/ppermute | solution.py:462
  48.8 18.7 %collective-permute-start.12 = (bf16[5,2,8,1664]{3,2,1,0:T(8,128)(2,1)S(1)}, bf16[5,2,8,1664]{3,2,1,0:T(8,128)(2,1)S(1)}, u32[]{:S(2)}, u32[]{:S(2)}) collective-permute-start(bf16[5,2,8,1664]{3,2,1,0:T(8,128)(2,1)S(1)} %pick.2), channel_id=1, source_target_pairs={{0,16},{4,20},{8,24},{12,28},{16,0},{20,4},{24,8},{28,12},{32,48},... | collective-permute-start | bytes 798728 | tf_op jit(solution)/shard_map/ppermute | solution.py:462
  52.1 15.4 %collective-permute-start.11 = (bf16[5,2,8,1664]{3,2,1,0:T(8,128)(2,1)S(1)}, bf16[5,2,8,1664]{3,2,1,0:T(8,128)(2,1)S(1)}, u32[]{:S(2)}, u32[]{:S(2)}) collective-permute-start(bf16[5,2,8,1664]{3,2,1,0:T(8,128)(2,1)S(1)} %pick.2), channel_id=1, source_target_pairs={{0,24},{4,28},{8,0},{12,4},{16,8},{20,12},{24,16},{28,20},{32,56},... | collective-permute-start | bytes 798728 | tf_op jit(solution)/shard_map/ppermute | solution.py:462
  52.2 15.4 %collective-permute-start.16 = (bf16[3,2,8,1664]{3,2,1,0:T(8,128)(2,1)S(1)}, bf16[3,2,8,1664]{3,2,1,0:T(8,128)(2,1)S(1)}, u32[]{:S(2)}, u32[]{:S(2)}) collective-permute-start(bf16[3,2,8,1664]{3,2,1,0:T(8,128)(2,1)S(1)} %pick.3), channel_id=1, source_target_pairs={{0,8},{4,12},{8,16},{12,20},{16,24},{20,28},{24,0},{28,4},{32,40},... | collective-permute-start | bytes 479240 | tf_op jit(solution)/shard_map/ppermute | solution.py:462
  85.7 9.7 %collective-permute-start.25 = (f16[4,2,8,2304]{3,2,1,0:T(8,128)(2,1)S(1)}, f16[4,2,8,2304]{3,2,1,0:T(8,128)(2,1)S(1)}, u32[]{:S(2)}, u32[]{:S(2)}) collective-permute-start(f16[4,2,8,2304]{3,2,1,0:T(8,128)(2,1)S(1)} %bitcast.51), channel_id=1, source_target_pairs={{0,32},{4,36},{8,40},{12,44},{16,48},{20,52},{24,56},{28,60},{32,6... | collective-permute-start | bytes 884744 | tf_op jit(solution)/shard_map/ppermute | solution.py:462
  85.9 9.7 %collective-permute-start.29 = (f16[4,2,8,2304]{3,2,1,0:T(8,128)(2,1)S(1)}, f16[4,2,8,2304]{3,2,1,0:T(8,128)(2,1)S(1)}, u32[]{:S(2)}, u32[]{:S(2)}) collective-permute-start(f16[4,2,8,2304]{3,2,1,0:T(8,128)(2,1)S(1)} %bitcast.50), channel_id=1, source_target_pairs={{0,224},{4,228},{8,232},{12,236},{16,240},{20,244},{24,248},{28,25... | collective-permute-start | bytes 884744 | tf_op jit(solution)/shard_map/ppermute | solution.py:462
  95.5 8.4 %collective-permute-start.26 = (f16[4,2,8,2304]{3,2,1,0:T(8,128)(2,1)S(1)}, f16[4,2,8,2304]{3,2,1,0:T(8,128)(2,1)S(1)}, u32[]{:S(2)}, u32[]{:S(2)}) collective-permute-start(f16[4,2,8,2304]{3,2,1,0:T(8,128)(2,1)S(1)} %add_convert_fusion.5), channel_id=1, source_target_pairs={{0,32},{4,36},{8,40},{12,44},{16,48},{20,52},{24,56},{28,60},{32,6... | collective-permute-start | bytes 884744 | tf_op jit(solution)/shard_map/ppermute | solution.py:462
  104.1 15.6 %collective-permute-start.31 = (f16[4,2,8,2304]{3,2,1,0:T(8,128)(2,1)S(1)}, f16[4,2,8,2304]{3,2,1,0:T(8,128)(2,1)S(1)}, u32[]{:S(2)}, u32[]{:S(2)}) collective-permute-start(f16[4,2,8,2304]{3,2,1,0:T(8,128)(2,1)S(1)} %add_convert_fusion.1), channel_id=1, source_target_pairs={{0,224},{4,228},{8,232},{12,236},{16,240},{20,244},{24,248},{28,25... | collective-permute-start | bytes 884744 | tf_op jit(solution)/shard_map/ppermute | solution.py:462
  116.4 19.7 %collective-permute-start.24 = (f16[8,2,8,1792]{3,2,1,0:T(8,128)(2,1)S(1)}, f16[8,2,8,1792]{3,2,1,0:T(8,128)(2,1)S(1)}, u32[]{:S(2)}, u32[]{:S(2)}) collective-permute-start(f16[8,2,8,1792]{3,2,1,0:T(8,128)(2,1)S(1)} %bitcast.49), channel_id=1, source_target_pairs={{0,24},{4,28},{8,0},{12,4},{16,8},{20,12},{24,16},{28,20},{32,56},... | collective-permute-start | bytes 1376264 | tf_op jit(solution)/shard_map/ppermute | solution.py:462
  118.6 17.6 %collective-permute-start.23 = (f16[8,2,8,1792]{3,2,1,0:T(8,128)(2,1)S(1)}, f16[8,2,8,1792]{3,2,1,0:T(8,128)(2,1)S(1)}, u32[]{:S(2)}, u32[]{:S(2)}) collective-permute-start(f16[8,2,8,1792]{3,2,1,0:T(8,128)(2,1)S(1)} %bitcast.48), channel_id=1, source_target_pairs={{0,16},{4,20},{8,24},{12,28},{16,0},{20,4},{24,8},{28,12},{32,48},... | collective-permute-start | bytes 1376264 | tf_op jit(solution)/shard_map/ppermute | solution.py:462
  119.7 19.9 %collective-permute-start.22 = (f16[8,2,8,1792]{3,2,1,0:T(8,128)(2,1)S(1)}, f16[8,2,8,1792]{3,2,1,0:T(8,128)(2,1)S(1)}, u32[]{:S(2)}, u32[]{:S(2)}) collective-permute-start(f16[8,2,8,1792]{3,2,1,0:T(8,128)(2,1)S(1)} %bitcast.47), channel_id=1, source_target_pairs={{0,8},{4,12},{8,16},{12,20},{16,24},{20,28},{24,0},{28,4},{32,40},... | collective-permute-start | bytes 1376264 | tf_op jit(solution)/shard_map/ppermute | solution.py:462
  120.2 24.9 %collective-permute-start.32 = (f16[2,8,2304]{2,1,0:T(8,128)(2,1)S(1)}, f16[2,8,2304]{2,1,0:T(8,128)(2,1)S(1)}, u32[]{:S(2)}, u32[]{:S(2)}) collective-permute-start(f16[2,8,2304]{2,1,0:T(8,128)(2,1)S(1)} %get-tuple-element.50), channel_id=1, source_target_pairs={{0,8},{4,12},{8,16},{12,20},{16,24},{20,28},{24,0},{28,4},{32,40},... | collective-permute-start | bytes 221192 | tf_op jit(solution)/shard_map/ppermute | solution.py:462
  122.4 22.7 %collective-permute-start.34 = (f16[2,8,2304]{2,1,0:T(8,128)(2,1)S(1)}, f16[2,8,2304]{2,1,0:T(8,128)(2,1)S(1)}, u32[]{:S(2)}, u32[]{:S(2)}) collective-permute-start(f16[2,8,2304]{2,1,0:T(8,128)(2,1)S(1)} %get-tuple-element.51), channel_id=1, source_target_pairs={{0,24},{4,28},{8,0},{12,4},{16,8},{20,12},{24,16},{28,20},{32,56},... | collective-permute-start | bytes 221192 | tf_op jit(solution)/shard_map/ppermute | solution.py:462
  136.2 9.0 %collective-permute-start.33 = (f16[2,8,2304]{2,1,0:T(8,128)(2,1)S(1)}, f16[2,8,2304]{2,1,0:T(8,128)(2,1)S(1)}, u32[]{:S(2)}, u32[]{:S(2)}) collective-permute-start(f16[2,8,2304]{2,1,0:T(8,128)(2,1)S(1)} %get-tuple-element.52), channel_id=1, source_target_pairs={{0,16},{4,20},{8,24},{12,28},{16,0},{20,4},{24,8},{28,12},{32,48},... | collective-permute-start | bytes 221192 | tf_op jit(solution)/shard_map/ppermute | solution.py:462
  140.7 19.2 %all-to-all-start = ((f16[8,2,8,1792]{3,2,1,0:T(8,128)(2,1)}), f16[8,2,8,1792]{3,2,1,0:T(8,128)(2,1)S(1)}, u32[]{:S(2)}, u32[]{:S(2)}) async-start(f16[8,2,8,1792]{3,2,1,0:T(8,128)(2,1)} %add_convert_fusion), calls=%async_computation | async-start | bytes 917504 | tf_op jit(solution)/shard_map/all_to_all | solution.py:466
  (18 other events, 197.5 us)
